TPU v7x, 128 devices: a whole 4x4x4 slice. The times are simulated.
128 devices in a mesh: rep: 8 (over y_hi, x), tr: 8 (over y_lo, z), tc: 2 (over core).
Axes of the slice: x: 4, y: 4 (y_hi: 2, y_lo: 2; y = y_hi * 2 + y_lo), z: 4, core: 2. Of those that a mesh axis runs over, the one named last changes fastest.
Arguments:
- tokens: bfloat16 [512, 16, 8, 1600], P(('rep', 'tr'), None, None, 'tc'), may hold values from -6 to 6
- prefix_kv: bfloat16 [512, 256, 512], P(('rep', 'tr'), None, 'tc')
- ssm_state: float32 [512, 16, 3200], P(('rep', 'tr'), None, 'tc'), may hold values from -6 to 6
- conv_state: float32 [512, 3, 3200], P(('rep', 'tr'), None, 'tc'), may hold values from -6 to 6
- prefix_len: int32 [512], replicated, may hold values from 1 to 256
- group_size: int32 [512], replicated, may hold values from 8 to 16
- serve_replica: int32 [512], replicated, may hold values from 0 to 7, as said below
- in_gain: float32 [1600], P('tc'), may hold values from 0.5 to 1.5
- w_query: bfloat16 [1600, 1024], P(('rep', 'tr'), 'tc'), may hold values from -0.15625 to 0.15625
- w_keyval: bfloat16 [1600, 512], P(('rep', 'tr'), 'tc'), may hold values from -0.15625 to 0.15625
- w_inner: bfloat16 [1600, 2, 3200], P(('rep', 'tr'), None, 'tc'), may hold values from -0.15625 to 0.15625
- conv_weight: float32 [4, 3200], P(None, 'tc'), may hold values from -3 to 3
- conv_bias: float32 [3200], P('tc'), may hold values from -3 to 3
- w_xproj: bfloat16 [3200, 132], P('tc'), may hold values from -0.109375 to 0.109375
- dt_weight: bfloat16 [100, 3200], P(None, 'tc'), may hold values from -0.625 to 0.625
- dt_bias: float32 [3200], P('tc'), may hold values from -4.5 to -1
- decay_log: float32 [16, 3200], P(None, 'tc'), may hold values from -1 to 2.5
- skip_gain: float32 [3200], P('tc'), may hold values from 0.5 to 1.5
- w_attn_out: bfloat16 [1024, 1600], P('tc', ('rep', 'tr'))
- w_ssm_out: bfloat16 [3200, 1600], P('tc', ('rep', 'tr'))
- attn_gain: float32 [1600], replicated, may hold values from 0.5 to 1.5
- ssm_gain: float32 [1600], replicated, may hold values from 0.5 to 1.5
Outputs:
- mixed: bfloat16 [512, 16, 8, 1600], P(('rep', 'tr'), None, None, 'tc')
Inputs may be any that keep to these rules, and one draw needn't show every extreme that they name: `serve_replica`: within each aligned block of 8 groups every replica is named equally often.
All inputs are finite; a program needn't handle non-finite values.
Results may differ from a plain program's by a relative error of at most 0.013.
Values may be sent and summed in bfloat16 or wider, within the bound.
A program may use at most 192 MiB of HBM per device.

v0:
```python
import jax
import jax.numpy as jnp
from jax import lax
from jax.sharding import PartitionSpec as P

D = 1600
HD = 64
QH = 16
KVH = 4


EPSILON = 1e-06


def table_pick(served, table):
    matches = served[:, None] == jnp.arange(table.shape[0], dtype=jnp.int32)[None, :]
    return jnp.sum(jnp.where(matches, table[None, :], 0), axis=1)


def prefix_scores(group_query, key_block, length, score_scale):
    scores = (
        jnp.einsum("rtkjd,pkd->rtkjp", group_query, key_block, preferred_element_type=jnp.float32)
        * score_scale
    )
    positions = jnp.arange(key_block.shape[0], dtype=jnp.int32)
    return jnp.where(positions < length, scores, -jnp.inf)


def local(
    tokens,
    prefix_kv,
    ssm_state,
    conv_state,
    prefix_len,
    group_size,
    serve_replica,
    in_gain,
    w_query,
    w_keyval,
    w_inner,
    conv_weight,
    conv_bias,
    w_xproj,
    dt_weight,
    dt_bias,
    decay_log,
    skip_gain,
    w_attn_out,
    w_ssm_out,
    attn_gain,
    ssm_gain,
):
    rep_count = lax.axis_size("rep")
    my_replica = lax.axis_index("rep")
    row_axis = lax.axis_size("tr")
    my_row = lax.axis_index("tr")
    tensor_count = lax.axis_size("tc")
    tensor_index = lax.axis_index("tc")
    group_count, slot_count, new_count, width_part = tokens.shape
    pair_count = group_count // rep_count
    head_dim = HD
    kv_here = KVH // tensor_count
    per_kv = QH // KVH
    heads_here = QH // tensor_count
    score_scale = head_dim ** (-0.5)
    row_count = group_count * slot_count * new_count
    request_count = group_count * slot_count
    route_plan = serve_replica.reshape(rep_count, row_axis, group_count)
    column = lax.dynamic_index_in_dim(route_plan, my_row, 1, keepdims=False)
    orders = jnp.argsort(column, axis=1, stable=True)
    send_order = lax.dynamic_index_in_dim(orders, my_replica, 0, keepdims=False)
    picked = lax.dynamic_slice_in_dim(orders, my_replica * pair_count, pair_count, 1)
    block_ids = jnp.arange(rep_count, dtype=jnp.int32) * row_axis + my_row
    served = (block_ids[:, None] * group_count + picked).reshape(group_count)
    lengths = table_pick(served, prefix_len)
    live_sizes = table_pick(served, group_size)
    moved_tokens, moved_cache = (
        lax.all_to_all(
            jnp.take(tokens, send_order, axis=0), "rep", split_axis=0, concat_axis=0, tiled=True
        ),
        lax.all_to_all(
            jnp.take(prefix_kv, send_order, axis=0), "rep", split_axis=0, concat_axis=0, tiled=True
        ),
    )
    moved_state, moved_conv = (
        lax.all_to_all(
            jnp.take(ssm_state, send_order, axis=0).astype(jnp.bfloat16),
            "rep",
            split_axis=0,
            concat_axis=0,
            tiled=True,
        ).astype(jnp.float32),
        lax.all_to_all(
            jnp.take(conv_state, send_order, axis=0).astype(jnp.bfloat16),
            "rep",
            split_axis=0,
            concat_axis=0,
            tiled=True,
        ).astype(jnp.float32),
    )
    x_rows = moved_tokens.reshape(row_count, width_part).astype(jnp.float32)
    square_sums = lax.psum(jnp.sum(x_rows * x_rows, axis=1), "tc")
    inv_rms = lax.rsqrt(square_sums / D + EPSILON)
    normed_part = (x_rows * inv_rms[:, None] * in_gain[None, :]).astype(jnp.bfloat16)
    normed = lax.all_gather(normed_part, "tc", axis=1, tiled=True)
    channels = w_inner.shape[2]
    inner_cols = w_inner.reshape(w_inner.shape[0], 2 * channels)
    pieces = (
        lax.all_gather(w_query, ("rep", "tr"), axis=0, tiled=True),
        lax.all_gather(w_keyval, ("rep", "tr"), axis=0, tiled=True),
        lax.all_gather(inner_cols, ("rep", "tr"), axis=0, tiled=True),
    )
    query_run = jnp.dot(normed, pieces[0], preferred_element_type=jnp.float32)
    keyval_run = jnp.dot(normed, pieces[1], preferred_element_type=jnp.float32)
    inner_run = jnp.dot(normed, pieces[2], preferred_element_type=jnp.float32)
    query = query_run.astype(jnp.bfloat16).reshape(
        group_count, slot_count, new_count, kv_here, per_kv, head_dim
    )
    keyval = keyval_run.astype(jnp.bfloat16).reshape(
        group_count, slot_count, new_count, kv_here, 2, head_dim
    )
    cache_len = moved_cache.shape[1]
    cache_heads = moved_cache.reshape(group_count, cache_len, kv_here, 2, head_dim)
    causal = jnp.arange(new_count)[None, :] <= jnp.arange(new_count)[:, None]

    def attend(group_args):
        group_query, group_kv, group_cache, length = group_args
        key_all = group_cache[:, :, 0]
        value_all = group_cache[:, :, 1]
        own_scores = (
            jnp.einsum(
                "rtkjd,rskd->rtkjs",
                group_query,
                group_kv[:, :, :, 0],
                preferred_element_type=jnp.float32,
            )
            * score_scale
        )
        own_scores = jnp.where(causal[None, :, None, None, :], own_scores, -jnp.inf)
        own_max = jnp.max(own_scores, axis=4)
        scores = prefix_scores(group_query, key_all, length, score_scale)
        row_max = jnp.maximum(jnp.max(scores, axis=4), own_max)
        prefix_weights = jnp.exp(scores - row_max[..., None])
        row_totals = jnp.sum(prefix_weights, axis=4)
        weighted = jnp.einsum(
            "rtkjp,pkd->rtkjd",
            prefix_weights.astype(jnp.bfloat16),
            value_all,
            preferred_element_type=jnp.float32,
        )
        own_weights = jnp.exp(own_scores - row_max[..., None])
        row_totals = row_totals + jnp.sum(own_weights, axis=4)
        weighted = weighted + jnp.einsum(
            "rtkjs,rskd->rtkjd",
            own_weights.astype(jnp.bfloat16),
            group_kv[:, :, :, 1],
            preferred_element_type=jnp.float32,
        )
        return (
            (weighted / row_totals[..., None])
            .astype(jnp.bfloat16)
            .reshape(slot_count, new_count, heads_here * head_dim)
        )

    heads = lax.map(attend, (query, keyval, cache_heads, lengths)).reshape(
        row_count, heads_here * head_dim
    )
    inner = inner_run.reshape(group_count, slot_count, new_count, 2, channels)
    conv_in = inner[:, :, :, 0]
    gate = inner[:, :, :, 1].reshape(row_count, channels)
    history = jnp.broadcast_to(
        moved_conv[:, None], (group_count, slot_count, moved_conv.shape[1], channels)
    )
    sequence = jnp.concatenate([history, conv_in], axis=2)
    conv_sum = jnp.broadcast_to(conv_bias, (group_count, slot_count, new_count, channels))
    for tap_index in range(conv_weight.shape[0]):
        conv_sum = (
            conv_sum + conv_weight[tap_index] * sequence[:, :, tap_index : tap_index + new_count]
        )
    conv_out = jax.nn.silu(conv_sum).astype(jnp.bfloat16).reshape(row_count, channels)
    projected = lax.psum(
        jnp.dot(conv_out, w_xproj, preferred_element_type=jnp.float32).astype(jnp.bfloat16), "tc"
    ).astype(jnp.float32)
    rank_width = dt_weight.shape[0]
    state_size = decay_log.shape[0]
    step_in = projected[:, :rank_width].astype(jnp.bfloat16)
    input_mix = projected[:, rank_width : rank_width + state_size]
    output_mix = projected[:, rank_width + state_size :]
    step_size = jax.nn.softplus(
        jnp.dot(step_in, dt_weight, preferred_element_type=jnp.float32) + dt_bias
    )
    decay_rate = -jnp.exp(decay_log)

    def token_major(values):
        return values.reshape(request_count, new_count, values.shape[1]).swapaxes(0, 1)

    start_state = jnp.broadcast_to(
        moved_state[:, None], (group_count, slot_count, state_size, channels)
    ).reshape(request_count, state_size, channels)

    def advance(carried, inputs):
        step_now, value_now, mix_in, mix_out = inputs
        carried = (
            jnp.exp(step_now[:, None, :] * decay_rate[None]) * carried
            + (step_now * value_now)[:, None, :] * mix_in[:, :, None]
        )
        result = jnp.sum(carried * mix_out[:, :, None], axis=1) + skip_gain * value_now
        return (carried, result)

    last_state, outputs = lax.scan(
        advance,
        start_state,
        (
            token_major(step_size),
            token_major(conv_out.astype(jnp.float32)),
            token_major(input_mix),
            token_major(output_mix),
        ),
    )
    ssm_out = outputs.swapaxes(0, 1).reshape(row_count, channels)
    gated = (ssm_out * jax.nn.silu(gate)).astype(jnp.bfloat16)
    pieces = (
        lax.all_gather(w_attn_out, ("rep", "tr"), axis=1, tiled=True),
        lax.all_gather(w_ssm_out, ("rep", "tr"), axis=1, tiled=True),
    )
    attn_part = jnp.dot(heads, pieces[0], preferred_element_type=jnp.float32)
    ssm_part = jnp.dot(gated, pieces[1], preferred_element_type=jnp.float32)
    attn_cols, ssm_cols = (
        lax.psum_scatter(
            attn_part.astype(jnp.bfloat16), "tc", scatter_dimension=1, tiled=True
        ).astype(jnp.float32),
        lax.psum_scatter(
            ssm_part.astype(jnp.bfloat16), "tc", scatter_dimension=1, tiled=True
        ).astype(jnp.float32),
    )
    attn_sq, ssm_sq = lax.psum(
        (jnp.sum(attn_cols * attn_cols, axis=1), jnp.sum(ssm_cols * ssm_cols, axis=1)), "tc"
    )
    attn_share = lax.dynamic_slice_in_dim(attn_gain, tensor_index * width_part, width_part, 0)
    ssm_share = lax.dynamic_slice_in_dim(ssm_gain, tensor_index * width_part, width_part, 0)
    attn_rms = lax.rsqrt(attn_sq / D + EPSILON)[:, None]
    ssm_rms = lax.rsqrt(ssm_sq / D + EPSILON)[:, None]
    branch = 0.5 * (attn_share * attn_cols * attn_rms + ssm_share * ssm_cols * ssm_rms)
    live = jnp.arange(slot_count)[None, :] < live_sizes[:, None]
    live_rows = jnp.broadcast_to(live[:, :, None], (group_count, slot_count, new_count)).reshape(
        row_count, 1
    )
    mixed = jnp.where(live_rows, x_rows + branch, 0.0).astype(jnp.bfloat16)
    return mixed.reshape(group_count, slot_count, new_count, width_part)


def solution(mesh):
    placed = (
        P(("rep", "tr"), None, None, "tc"),
        P(("rep", "tr"), None, "tc"),
        P(("rep", "tr"), None, "tc"),
        P(("rep", "tr"), None, "tc"),
        P(),
        P(),
        P(),
        P("tc"),
        P(("rep", "tr"), "tc"),
        P(("rep", "tr"), "tc"),
        P(("rep", "tr"), None, "tc"),
        P(None, "tc"),
        P("tc"),
        P("tc", None),
        P(None, "tc"),
        P("tc"),
        P(None, "tc"),
        P("tc"),
        P("tc", ("rep", "tr")),
        P("tc", ("rep", "tr")),
        P(),
        P(),
    )
    return jax.shard_map(
        local,
        mesh=mesh,
        in_specs=placed,
        out_specs=P(("rep", "tr"), None, None, "tc"),
        check_vma=False,
    )
```

profile of v0, /device:TPU:0, one launch (start us, length us, event | category | flops | bytes accessed | tf_op | source)
XLA Modules:
  0.0 1649.2 jit_solution(8832406001314647902)
XLA Ops:
  13.5 32.8 %all_to_all.20 = bf16[8,16,8,800]{3,2,1,0:T(8,128)(2,1)S(1)} all-to-all(bf16[8,16,8,800]{3,2,1,0:T(8,128)(2,1)S(1)} %broadcast_select_fusion), channel_id=1, replica_groups=mesh['rep'=8,'tr'=8,'tc'=2] {'rep'}, dimensions={0} | all-to-all | bytes 3276800 | tf_op jit(solution)/shard_map/all_to_all | solution.py:78
  64.0 187.4 %all-gather.1 = bf16[64,25,256]{2,1,0:T(8,128)(2,1)S(1)} all-gather(bf16[1,25,256]{2,1,0:T(8,128)(2,1)S(1)} %bitcast.200), channel_id=1, replica_groups=mesh['rep'=8,'tr'=8,'tc'=2] {'rep','tr'}, dimensions={0}, use_global_device_ids=true | all-gather | bytes 832000 | tf_op jit(solution)/shard_map/all_gather | solution.py:110
  262.7 82.2 %all-gather.13.cloned.1.call-done = bf16[64,25,512]{2,1,0:T(8,128)(2,1)} async-done(((bf16[1,25,512]{2,1,0:T(8,128)(2,1)}), bf16[64,25,512]{2,1,0:T(8,128)(2,1)}) %all-gather.13.cloned.1.call-update) | async-done | bytes 1638416 | tf_op jit(solution)/shard_map/all_gather | solution.py:109
  347.5 330.6 %all-gather.15.cloned.1.call-done = bf16[64,25,512]{2,1,0:T(8,128)(2,1)} async-done(((bf16[1,25,512]{2,1,0:T(8,128)(2,1)}), bf16[64,25,512]{2,1,0:T(8,128)(2,1)}) %all-gather.15.cloned.1.call-update) | async-done | bytes 1638416 | tf_op jit(solution)/shard_map/all_gather | solution.py:223
  681.8 13.0 all-gather.11.cloned.1.call-done
  705.6 69.9 %while.24 = (s32[]{:T(128)}, bf16[8,16,8,512]{3,2,1,0:T(8,128)(2,1)}, bf16[8,256,2,2,64]{1,4,3,2,0:T(8,128)(2,1)}, s32[8]{0:T(128)S(1)}, bf16[8,16,8,2,4,64]{5,4...) while((s32[]{:T(128)}, bf16[8,16,8,512]{3,2,1,0:T(8,128)(2,1)}, ...), condition=%wide.region_10.11_spmd.clone, body=%wide.region_5.10_spmd.clone.sunk | while | flops 71293248 | bytes 7227317 | solution.py:165
  775.4 277.5 %all-gather.17.cloned.1.call-done = bf16[64,25,3200]{2,1,0:T(8,128)(2,1)} async-done(((bf16[1,25,3200]{2,1,0:T(8,128)(2,1)}), bf16[64,25,3200]{2,1,0:T(8,128)(2,1)}) %all-gather.17.cloned.1.call-update) | async-done | bytes 10240016 | tf_op jit(solution)/shard_map/all_gather | solution.py:111
  1053.0 11.8 reshape.228
  1064.8 19.0 %fusion.52 = f32[1024,3200]{1,0:T(8,128)} fusion(bf16[1024,1600]{0,1:T(8,128)(2,1)} %all-gather.11.cloned.1.call-done, bf16[1600,3200]{1,0:T(8,128)(2,1)} %reshape.228), kind=kOutput, calls=%fused_computation.124 | convolution fusion | flops 10485760000 | bytes 26624000 | tf_op jit(solution)/shard_map/dot_general | solution.py:115
  1083.8 17.6 %reshape.180 = f32[8,16,8,2,1600]{4,3,2,1,0:T(2,128)} reshape(f32[1024,3200]{1,0:T(8,128)} %fusion.52) | data formatting | bytes 26214400 | tf_op jit(solution)/shard_map/reshape | solution.py:168
  1101.4 16.1 fusion.50
  1124.6 15.4 multiply_convert_fusion
  1148.7 244.3 %all-gather.19.cloned.1.call-done = bf16[64,25,1600]{2,1,0:T(8,128)(2,1)} async-done(((bf16[1,25,1600]{2,1,0:T(8,128)(2,1)}), bf16[64,25,1600]{2,1,0:T(8,128)(2,1)}) %all-gather.19.cloned.1.call-update) | async-done | bytes 5120016 | tf_op jit(solution)/shard_map/all_gather | solution.py:224
  1393.1 8.8 reshape.230
  1401.8 5.3 copy.170
  1407.2 6.3 copy.192
  1413.5 5.8 all-reduce.3.cloned.1.call-done
  1419.3 7.6 compare_select_fusion
  1426.8 7.5 copy.169
  1435.6 5.9 broadcast_in_dim.164
  1441.5 155.4 %while.23 = (s32[]{:T(128)}, f32[128,16,1600]{2,1,0:T(8,128)}, f32[8,128,1600]{2,1,0:T(8,128)}, f32[8,128,1600]{2,0,1:T(8,128)}, f32[16,1600]{1,0:T(8,128)S(1)},...) while((s32[]{:T(128)}, f32[128,16,1600]{2,1,0:T(8,128)}, ...), condition=%wide.region_17.18_spmd, body=%wide.region_15.17_spmd.sunk | while | flops 20070400 | bytes 37087612 | solution.py:210
  1446.4 12.3 multiply_reduce_fusion.3
  1465.8 12.3 multiply_reduce_fusion.3
  1485.2 12.3 multiply_reduce_fusion.3
  1504.7 12.3 multiply_reduce_fusion.3
  1524.1 12.3 multiply_reduce_fusion.3
  1543.5 12.3 multiply_reduce_fusion.3
  1563.0 12.3 multiply_reduce_fusion.3
  1582.5 12.3 multiply_reduce_fusion.3
  1596.9 8.8 fusion.34
  1605.8 10.2 convolution_convert_fusion
  1623.4 7.9 reduce-scatter.5.cloned.1.call-done
  (339 shorter events, 214.0 us)
Async XLA Ops:
  6.5 3.3 copy-start
  6.5 338.4 %all-gather.13.cloned.1.call-start = ((), (), s32[]{:S(2)}) async-start(), calls=%async_computation.10 | async-start | bytes 2129920 | tf_op jit(solution)/shard_map/all_gather | solution.py:109
  7.3 670.8 %all-gather.15.cloned.1.call-start = ((), (), s32[]{:S(2)}) async-start(), calls=%async_computation.11 | async-start | bytes 2129920 | tf_op jit(solution)/shard_map/all_gather | solution.py:223
  8.0 41.6 %copy-start.12 = (f32[800]{0:T(1024)S(1)}, f32[800]{0:T(1024)}, u32[]{:S(2)}) copy-start(f32[800]{0:T(1024)} %param.33) | copy-start | bytes 9604
  8.0 686.8 %all-gather.11.cloned.1.call-start = ((), (), s32[]{:S(2)}) async-start(), calls=%async_computation.6 | async-start | bytes 4915200 | tf_op jit(solution)/shard_map/all_gather | solution.py:105
  46.8 9.5 copy-start.7
  46.8 10.5 copy-start.5
  52.5 11.5 copy-start.10
  56.3 198.2 %copy-start.3 = (f32[8,3,1600]{2,0,1:T(8,128)S(1)}, f32[8,3,1600]{2,0,1:T(8,128)}, u32[]{:S(2)}) copy-start(f32[8,3,1600]{2,0,1:T(8,128)} %param.29) | copy-start | bytes 460804
  56.3 199.7 %copy-start.9 = (f32[4,1600]{1,0:T(4,128)S(1)}, f32[4,1600]{1,0:T(4,128)}, u32[]{:S(2)}) copy-start(f32[4,1600]{1,0:T(4,128)} %param.37) | copy-start | bytes 76804
  56.3 199.8 %copy-start.15 = (s32[512]{0:T(512)S(1)}, s32[512]{0:T(512)}, u32[]{:S(2)}) copy-start(s32[512]{0:T(512)} %param.31) | copy-start | bytes 6148
  56.3 199.8 %copy-start.16 = (s32[512]{0:T(512)S(1)}, s32[512]{0:T(512)}, u32[]{:S(2)}) copy-start(s32[512]{0:T(512)} %param.30) | copy-start | bytes 6148
  56.3 200.5 %copy-start.8 = (f32[16,1600]{1,0:T(8,128)S(1)}, f32[16,1600]{1,0:T(8,128)}, u32[]{:S(2)}) copy-start(f32[16,1600]{1,0:T(8,128)} %param.42) | copy-start | bytes 307204
  56.3 996.6 %all-gather.17.cloned.1.call-start = ((), (), s32[]{:S(2)}) async-start(), calls=%async_computation.12 | async-start | bytes 13312000 | tf_op jit(solution)/shard_map/all_gather | solution.py:111
  59.1 198.6 %all-to-all-start.1 = ((bf16[8,256,256]{2,1,0:T(8,128)(2,1)}), bf16[8,256,256]{2,1,0:T(8,128)(2,1)S(1)}, u32[]{:S(2)}, u32[]{:S(2)}) async-start(bf16[8,256,256]{2,1,0:T(8,128)(2,1)} %broadcast_select_fusion.1), calls=%async_computation.1 | async-start | bytes 2097152 | tf_op jit(solution)/shard_map/all_to_all | solution.py:81
  63.4 1329.7 %all-gather.19.cloned.1.call-start = ((), (), s32[]{:S(2)}) async-start(), calls=%async_computation.13 | async-start | bytes 6922240 | tf_op jit(solution)/shard_map/all_gather | solution.py:224
  257.7 863.1 %all-to-all-start.3 = ((bf16[8,3,1600]{2,1,0:T(4,128)(2,1)}), bf16[8,3,1600]{2,1,0:T(4,128)(2,1)S(1)}, u32[]{:S(2)}, u32[]{:S(2)}) async-start(bf16[8,3,1600]{2,1,0:T(4,128)(2,1)} %copy.168), calls=%async_computation.4 | async-start | bytes 212992 | tf_op jit(solution)/shard_map/all_to_all | solution.py:93
  1117.5 7.1 copy-start.11
  1120.8 314.8 %all-to-all-start.2 = ((bf16[8,16,1600]{2,1,0:T(8,128)(2,1)}), bf16[8,16,1600]{2,1,0:T(8,128)(2,1)S(1)}, u32[]{:S(2)}, u32[]{:S(2)}) async-start(bf16[8,16,1600]{2,1,0:T(8,128)(2,1)} %select_convert_fusion), calls=%async_computation.3 | async-start | bytes 851968 | tf_op jit(solution)/shard_map/all_to_all | solution.py:86
  1124.3 294.9 %all-reduce.3.cloned.1.call-start = ((), (), s32[]{:S(2)}) async-start(), calls=%async_computation.8 | async-start | bytes 557056 | tf_op jit(solution)/shard_map/psum | solution.py:181
  1124.6 17.1 %copy-start.18 = (bf16[1600,132]{0,1:T(8,128)(2,1)S(1)}, bf16[1600,132]{0,1:T(8,128)(2,1)}, u32[]{:S(2)}) copy-start(bf16[1600,132]{0,1:T(8,128)(2,1)} %param.39) | copy-start | bytes 1267204
  1124.6 19.2 %copy-start.4 = (bf16[1600,512]{1,0:T(8,128)(2,1)S(1)}, bf16[1600,512]{1,0:T(8,128)(2,1)}, u32[]{:S(2)}) copy-start(bf16[1600,512]{1,0:T(8,128)(2,1)} %reshape.226) | copy-start | bytes 4915204
  1140.0 1.7 copy-start.2
  1143.8 477.7 %reduce-scatter.3.cloned.1.call-start = ((), (), s32[]{:S(2)}) async-start(), calls=%async_computation.7 | async-start | bytes 4915200 | tf_op jit(solution)/shard_map/reduce_scatter | solution.py:229
  1148.7 482.6 %reduce-scatter.5.cloned.1.call-start = ((), (), s32[]{:S(2)}) async-start(), calls=%async_computation.9 | async-start | bytes 4915200 | tf_op jit(solution)/shard_map/reduce_scatter | solution.py:232
  1407.2 12.1 copy-start.19
  1407.2 12.1 copy-start.20
  1435.6 5.9 copy-start.6
  1605.8 10.3 copy-start.13
  1605.8 10.4 copy-start.14
  1605.8 10.4 copy-start.17
  1621.4 20.7 %copy-start.1 = (bf16[8,16,8,800]{3,2,1,0:T(8,128)(2,1)S(1)}, bf16[8,16,8,800]{3,2,1,0:T(8,128)(2,1)}, u32[]{:S(2)}) copy-start(bf16[8,16,8,800]{3,2,1,0:T(8,128)(2,1)} %param.26) | copy-start | bytes 4915204
Sparse Core Ops, SparseCore 0:
  9.0 335.8 all-gather.12
  346.6 331.4 all-gather.14
  679.8 14.9 all-gather.10
  696.3 356.6 all-gather.16
  1054.4 338.5 all-gather.18
  1395.4 23.8 all-reduce.2
  1421.7 15.0 reduce-scatter.2
  1616.2 15.0 reduce-scatter.4
where the time goes:
time: 1660 us; the launch traced here: 1650 us
  waiting for transfers between devices  963 us (58%)
  blocking collectives  225 us (14%)
  local copies, waits for them, and re-layouts  186 us (11%)
  other arithmetic  177 us (11%)
  matrix products  71.2 us (4%)
    all_gather x1, waiting for transfers between devices, local(): lax.all_gather(w_attn_out, ('rep', 'tr'), axis=1, tiled=True)  331 us
    all_gather x1, waiting for transfers between devices, local(): lax.all_gather(inner_cols, ('rep', 'tr'), axis=0, tiled=True)  278 us
    all_gather x1, waiting for transfers between devices, local(): lax.all_gather(w_ssm_out, ('rep', 'tr'), axis=1, tiled=True)  244 us
    all_gather x1, blocking collectives, local(): lax.all_gather(w_keyval, ('rep', 'tr'), axis=0, tiled=True)  187 us
    reduce_sum x8, other arithmetic, advance(): jnp.sum(carried * mix_out[:, :, None], axis=1) + skip_gain * value_now  98.4 us
    all_gather x1, waiting for transfers between devices, local(): lax.all_gather(w_query, ('rep', 'tr'), axis=0, tiled=True)  82.2 us
    unnamed x50, local copies, waits for them, and re-layouts  40.4 us
  transfers between devices with their start and end apart: 11, of which 7 were waited for; matrix products, arithmetic and copies ran while one was open for 26% of the time, Pallas kernels for 0%

commit v1 on v0

v1 whole, which is shorter than its diff:
```python
import functools

import jax
import jax.numpy as jnp
import numpy as np
from jax import lax
from jax.experimental import pallas as pl
from jax.experimental.pallas import tpu as pltpu
from jax.sharding import PartitionSpec as P

D = 1600
HD = 64
QH = 16
KVH = 4
EPSILON = 1e-06
LOG2E = 1.4426950408889634

SHARD = 25
CONV_AT, GATE_AT, QKV_AT, IN_ODD, IN_COLS = 0, 1664, 3328, 4096, 4352
SSM_AT, ATT_AT, OUT_ODD, OUT_COLS = 0, 1664, 2176, 2304
CH = 1600
CHP = 1664
CHT = 1792
HALF = 800
HP = 896
MESH = pl.DeviceIdType.MESH
ANY = pl.BlockSpec(memory_space=pl.ANY)
F32 = jnp.float32
BF16 = jnp.bfloat16


def feature_table():
    table = np.full((2, HP), -1, np.int32)
    for half in range(2):
        at = 0
        for rot in range(3):
            for ylo in range(2):
                for x in range(4):
                    for z in range(4):
                        device = x * 8 + ylo * 4 + z
                        for j in range(8):
                            table[half, at] = device * SHARD + rot * 8 + j
                            at += 1
        for ylo in range(2):
            for x in range(4):
                for z in range(4):
                    device = x * 8 + ylo * 4 + z
                    table[half, 768 + 32 * half + ylo * 16 + x * 4 + z] = device * SHARD + 24
    return table


def torus_position():
    rep, tr, tc = lax.axis_index("rep"), lax.axis_index("tr"), lax.axis_index("tc")
    return {"x": rep % 4, "y": (rep // 4) * 2 + tr // 4, "z": tr % 4}, tc


def device_at(pos, tc):
    return ((pos["y"] // 2) * 4 + pos["x"], (pos["y"] % 2) * 4 + pos["z"], tc)


def moved(pos, axis, step):
    out = dict(pos)
    out[axis] = (pos[axis] + step + 4) % 4
    return out


ORDERS = (("x", "y", "z"), ("y", "z", "x"), ("z", "x", "y"))


class Ring:
    def __init__(self, rot, axis, span, offset_axis, offset, split, source, gathered, sems, slot, pos, tc):
        self.pos, self.tc, self.axis = pos, tc, axis
        self.rot, self.span, self.offset_axis, self.offset, self.split = rot, span, offset_axis, offset, split
        self.source, self.gathered = source, gathered
        self.send, self.recv, self.slot = sems[0], sems[1], slot

    def view(self, home, part=None):
        index = [self.rot]
        for name in ("y", "x", "z"):
            if name in self.span:
                if part is not None and self.split == name:
                    index.append(pl.ds(2 * part, 2))
                else:
                    index.append(pl.ds(0, 4))
            else:
                at = home[name]
                if name == self.offset_axis:
                    at = (at + self.offset + 4) % 4
                index.append(at)
        if part is not None and self.split is None:
            columns = self.gathered.shape[-1]
            middle = columns // 256 * 128
            index += [slice(None), pl.ds(0, middle) if part == 0 else pl.ds(middle, columns - middle)]
        return self.gathered.at[tuple(index)]

    def copy(self, number):
        step = 1 if number % 2 == 0 else -1
        if number < 2:
            home, part, source = self.pos, None, self.source
        else:
            home, part, source = moved(self.pos, self.axis, -step), number - 2, None
        there = self.view(home, part)
        return pltpu.make_async_remote_copy(
            src_ref=there if source is None else source,
            dst_ref=there,
            send_sem=self.send.at[self.slot + number],
            recv_sem=self.recv.at[self.slot + number],
            device_id=device_at(moved(self.pos, self.axis, step), self.tc),
            device_id_type=MESH,
        )

    def start(self):
        self.copy(0).start()
        self.copy(1).start()

    def forward(self):
        for number in (0, 1):
            self.copy(number).wait_recv()
            self.copy(number + 2).start()

    def finish(self):
        self.copy(2).wait_recv()
        self.copy(3).wait_recv()

    def drain(self):
        for number in range(4):
            self.copy(number).wait_send()


class Gather:
    def __init__(self, shard, gathered, send, recv, local_sem, pos, tc):
        sems = (send, recv)
        self.kept = [
            pltpu.make_async_copy(
                shard.at[rot], gathered.at[rot, pos["y"], pos["x"], pos["z"]], local_sem.at[rot]
            )
            for rot in range(3)
        ]
        first, second, third = [], [], []
        for rot, (one, two, three) in enumerate(ORDERS):
            at = rot * 24
            first.append(Ring(rot, one, (), None, 0, None, shard.at[rot], gathered, sems, at, pos, tc))
            second.append(Ring(rot, two, (one,), None, 0, one, None, gathered, sems, at + 4, pos, tc))
            third.append(
                [
                    Ring(rot, three, (one,), two, offset, one, None, gathered, sems, at + 8 + 4 * n, pos, tc)
                    for n, offset in enumerate((0, 1, -1, 2))
                ]
            )
        self.first, self.second = first, second
        self.third = [[rings[n] for rings in third] for n in range(4)]

    def stage(self, number):
        if number == 0:
            for ring in self.first:
                ring.start()
            for copy in self.kept:
                copy.start()
        if number == 1:
            for ring in self.first:
                ring.forward()
            for copy in self.kept:
                copy.wait()
        if number == 2:
            for ring in self.first:
                ring.finish()
            for ring in self.second + self.third[0]:
                ring.start()
        if number == 3:
            for ring in self.second:
                ring.forward()
            for ring in self.third[1] + self.third[2]:
                ring.start()
            for ring in self.third[0]:
                ring.forward()
        if number == 4:
            for ring in self.second:
                ring.finish()
            for ring in self.third[3]:
                ring.start()
        if number == 5:
            for ring in self.third[1] + self.third[2]:
                ring.forward()
        if number == 6:
            for ring in self.third[3]:
                ring.forward()
        if number == 7:
            for rings in self.third:
                for ring in rings:
                    ring.finish()
            for ring in self.first + self.second:
                ring.drain()
            for rings in self.third:
                for ring in rings:
                    ring.drain()


STAGES = 8
GATHER_SEMS = 72


def greet_torus(pos, tc):
    barrier = pltpu.get_barrier_semaphore()
    for axis in ("x", "y", "z"):
        for step in (1, -1):
            pl.semaphore_signal(
                barrier, inc=1, device_id=device_at(moved(pos, axis, step), tc), device_id_type=MESH
            )
    partner = device_at(pos, 1 - tc)
    pl.semaphore_signal(barrier, inc=1, device_id=partner, device_id_type=MESH)
    pl.semaphore_wait(barrier, 7)
    return partner


def gather_kernel(shard, tokens, gains, gathered, other, other_gains, send, recv, local_sem):
    pos, tc = torus_position()
    partner = greet_torus(pos, tc)
    gather = Gather(shard, gathered, send, recv, local_sem, pos, tc)
    swaps = [
        pltpu.make_async_remote_copy(
            src_ref=here,
            dst_ref=there,
            send_sem=send.at[GATHER_SEMS + n],
            recv_sem=recv.at[GATHER_SEMS + n],
            device_id=partner,
            device_id_type=MESH,
        )
        for n, (here, there) in enumerate(((tokens, other), (gains, other_gains)))
    ]
    gather.stage(0)
    for copy in swaps:
        copy.start()
    for number in range(1, STAGES):
        gather.stage(number)
    for copy in swaps:
        copy.wait()


def gather_call(shard, tokens, gains):
    return pl.pallas_call(
        gather_kernel,
        name="gather_weights",
        out_shape=(
            jax.ShapeDtypeStruct((3, 4, 4, 4, 8, IN_COLS), BF16),
            jax.ShapeDtypeStruct(tokens.shape, BF16),
            jax.ShapeDtypeStruct(gains.shape, F32),
        ),
        in_specs=[pl.BlockSpec(memory_space=pltpu.VMEM), ANY, ANY],
        out_specs=(ANY,) * 3,
        scratch_shapes=[
            pltpu.SemaphoreType.DMA((GATHER_SEMS + 2,)),
            pltpu.SemaphoreType.DMA((GATHER_SEMS + 2,)),
            pltpu.SemaphoreType.DMA((3,)),
        ],
        compiler_params=pltpu.CompilerParams(collective_id=0, has_side_effects=True),
    )(shard, tokens, gains)


def silu(value):
    return 0.5 * value * (1.0 + jnp.tanh(0.5 * value))


def project_kernel(
    scalars,
    own_tokens,
    other_tokens,
    own_gains,
    other_gains,
    pick,
    turn,
    left,
    right,
    odd_left,
    odd_right,
    history,
    taps,
    xproj,
    shard,
    conv_out,
    gate_out,
    qkv_out,
    mix_out,
    own_out,
    gathered,
    other_mix,
    normed,
    product,
    sequence,
    mix_send,
    send,
    recv,
    local_sem,
):
    step = pl.program_id(0)
    pos, tc = torus_position()
    gather = Gather(shard, gathered, send, recv, local_sem, pos, tc)
    swap = pltpu.make_async_remote_copy(
        src_ref=mix_send,
        dst_ref=other_mix,
        send_sem=send.at[GATHER_SEMS],
        recv_sem=recv.at[GATHER_SEMS],
        device_id=device_at(pos, 1 - tc),
        device_id_type=MESH,
    )

    @pl.when(step == 0)
    def _():
        greet_torus(pos, tc)
        gather.stage(0)

    for at, number in ((1, 1), (2, 2), (4, 3), (6, 4), (8, 5), (11, 6)):

        @pl.when(step == at)
        def _(number=number):
            gather.stage(number)

    @pl.when(step == 0)
    def _():
        def prepare(group, carry):
            home = scalars[group]
            rows = pl.ds(pl.multiple_of(group * 128, 128), 128)
            values, squares = [], 0.0
            for side, tokens in enumerate((own_tokens, other_tokens)):
                turned = jnp.dot(turn[...], tokens[home], preferred_element_type=F32).astype(BF16)
                value = jnp.dot(turned, pick[side], preferred_element_type=F32)
                squares = squares + jnp.sum(value * value, axis=1, keepdims=True)
                values.append(value)
            own_out[rows, :] = values[0].astype(BF16)
            scale = lax.rsqrt(squares / D + EPSILON)
            mine = values[0] * scale * own_gains[0:1, :]
            theirs = values[1] * scale * other_gains[0:1, :]
            scaled = [jnp.where(tc == 0, mine, theirs), jnp.where(tc == 0, theirs, mine)]
            for rot in range(3):
                for half in range(2):
                    at = rot * 512 + half * 256
                    normed[rows, at : at + 256] = scaled[half][:, rot * 256 : rot * 256 + 256].astype(BF16)
            normed[rows, 1536:1664] = (scaled[0][:, 768:] + scaled[1][:, 768:]).astype(BF16)
            return carry

        lax.fori_loop(0, 8, prepare, 0)
        mix_out[...] = jnp.zeros_like(mix_out)

    block = jnp.concatenate([left[...], right[...]], axis=1)
    odd = jnp.concatenate([odd_left[...], odd_right[...]], axis=1)

    def multiply(part, carry):
        rows = pl.ds(pl.multiple_of(part * 512, 512), 512)
        value = jnp.dot(normed[rows, 0:1536], block, preferred_element_type=F32)
        value = value + jnp.dot(normed[rows, 1536:1664], odd, preferred_element_type=F32)
        product[rows, :] = value
        return carry

    lax.fori_loop(0, 2, multiply, 0)

    @pl.when(step < 7)
    def _():
        def convolve(group, carry):
            home = scalars[group]
            rows = pl.ds(pl.multiple_of(group * 128, 128), 128)
            for k in range(3):
                sequence[16 * k : 16 * k + 16, :] = jnp.broadcast_to(history[home, k : k + 1, :], (16, 256))
            sequence[48:176, :] = product[rows, :]
            total = jnp.broadcast_to(taps[4:5, :], (128, 256))
            for k in range(4):
                total = total + taps[k : k + 1, :] * sequence[16 * k : 16 * k + 128, :]
            result = silu(total).astype(BF16)
            conv_out[rows, :] = result
            mix_out[rows, :] += jnp.dot(result, xproj[...], preferred_element_type=F32)
            return carry

        lax.fori_loop(0, 8, convolve, 0)

    @pl.when((step >= 7) & (step < 14))
    def _():
        def gating(group, carry):
            rows = pl.ds(pl.multiple_of(group * 128, 128), 128)
            gate_out[rows, :] = silu(product[rows, :]).astype(BF16)
            return carry

        lax.fori_loop(0, 8, gating, 0)

    @pl.when(step == 7)
    def _():
        mix_send[...] = mix_out[...].astype(BF16)
        swap.start()

    @pl.when(step >= 14)
    def _():
        def keep(group, carry):
            rows = pl.ds(pl.multiple_of(group * 128, 128), 128)
            qkv_out[rows, :] = product[rows, :].astype(BF16)
            return carry

        lax.fori_loop(0, 8, keep, 0)

    @pl.when(step == 16)
    def _():
        gather.stage(7)
        swap.wait()


def column_block(step):
    return jnp.where(
        step < 7,
        CONV_AT // 128 + 2 * step,
        jnp.where(step < 14, GATE_AT // 128 + 2 * (step - 7), QKV_AT // 128 + 2 * (step - 14)),
    )


def project_call(
    scalars, own, other, own_gains, other_gains, pick, turn, weights, odd, history, taps, xproj, shard
):
    whole = lambda shape: pl.BlockSpec(shape, lambda i, s: (0,) * len(shape), pipeline_mode=pl.Buffered(1))
    conv_at = lambda i: jnp.minimum(i, 6)
    grid_spec = pltpu.PrefetchScalarGridSpec(
        num_scalar_prefetch=1,
        grid=(17,),
        in_specs=[
            whole((8, 128, HALF)),
            whole((8, 128, HALF)),
            whole((8, HP)),
            whole((8, HP)),
            whole((2, HALF, HP)),
            whole((128, 128)),
            pl.BlockSpec((1536, 128), lambda i, s: (0, column_block(i))),
            pl.BlockSpec((1536, 128), lambda i, s: (0, column_block(i) + 1)),
            pl.BlockSpec((128, 128), lambda i, s: (0, column_block(i))),
            pl.BlockSpec((128, 128), lambda i, s: (0, column_block(i) + 1)),
            pl.BlockSpec((8, 3, 256), lambda i, s: (0, 0, conv_at(i))),
            pl.BlockSpec((8, 256), lambda i, s: (0, conv_at(i))),
            pl.BlockSpec((256, 256), lambda i, s: (conv_at(i), 0)),
            whole((3, 8, OUT_COLS)),
        ],
        out_specs=[
            pl.BlockSpec((1024, 256), lambda i, s: (0, conv_at(i))),
            pl.BlockSpec((1024, 256), lambda i, s: (0, jnp.clip(i - 7, 0, 6))),
            pl.BlockSpec((1024, 256), lambda i, s: (0, jnp.clip(i - 14, 0, 2))),
            pl.BlockSpec((1024, 256), lambda i, s: (0, 0)),
            pl.BlockSpec((1024, HP), lambda i, s: (0, 0)),
            ANY,
            ANY,
        ],
        scratch_shapes=[
            pltpu.VMEM((1024, 1664), BF16),
            pltpu.VMEM((1024, 256), F32),
            pltpu.VMEM((176, 256), F32),
            pltpu.VMEM((1024, 256), BF16),
            pltpu.SemaphoreType.DMA((GATHER_SEMS + 1,)),
            pltpu.SemaphoreType.DMA((GATHER_SEMS + 1,)),
            pltpu.SemaphoreType.DMA((3,)),
        ],
    )
    return pl.pallas_call(
        project_kernel,
        name="project",
        grid_spec=grid_spec,
        out_shape=[
            jax.ShapeDtypeStruct((1024, CHT), BF16),
            jax.ShapeDtypeStruct((1024, CHT), BF16),
            jax.ShapeDtypeStruct((1024, 768), BF16),
            jax.ShapeDtypeStruct((1024, 256), F32),
            jax.ShapeDtypeStruct((1024, HP), BF16),
            jax.ShapeDtypeStruct((3, 4, 4, 4, 8, OUT_COLS), BF16),
            jax.ShapeDtypeStruct((1024, 256), BF16),
        ],
        compiler_params=pltpu.CompilerParams(
            collective_id=1, has_side_effects=True, vmem_limit_bytes=50 << 20
        ),
    )(
        scalars, own, other, own_gains, other_gains, pick, turn, weights, weights, odd, odd, history, taps,
        xproj, shard,
    )


def scan_kernel(
    scalars,
    qkv,
    cache,
    mix_own,
    mix_other,
    conv,
    gate,
    start,
    decay,
    dt_weight,
    params,
    spread,
    heads_out,
    gated_out,
    rate,
    mixes,
    step_size,
    drive,
    scan_out,
):
    group = pl.program_id(0)

    @pl.when(group == 0)
    def _():
        value = -jnp.exp(decay[...]) * LOG2E
        for n in range(16):
            rate[n] = jnp.broadcast_to(value[n : n + 1, :], (8, CHP))

    length = scalars[8 + group]
    row = lax.broadcasted_iota(jnp.int32, (128, 384), 0)
    column = lax.broadcasted_iota(jnp.int32, (128, 384), 1)
    own = column - 256
    causal = (column >= 256) & ((own % 16) == (row % 16)) & ((own // 16) <= (row // 16))
    allowed = (causal | ((column < 256) & (column < length)))[None]
    low = lax.broadcasted_iota(jnp.int32, (128, 128), 1) < 64
    for kv in range(2):
        keys = jnp.concatenate(
            [cache[0, :, kv * 128 : kv * 128 + 128], qkv[:, 512 + kv * 128 : 640 + kv * 128]], axis=0
        )
        queries = []
        for pair in range(2):
            at = kv * 256 + pair * 128
            both = qkv[:, at : at + 128].astype(F32)
            queries.append(jnp.where(low, both, 0.0).astype(BF16))
            queries.append(jnp.where(low, pltpu.roll(both, 64, 1), 0.0).astype(BF16))
        query = jnp.concatenate(queries, axis=0)
        scores = lax.dot_general(query, keys, (((1,), (1,)), ((), ())), preferred_element_type=F32)
        scores = scores.reshape(4, 128, 384) * (HD ** (-0.5) * LOG2E)
        scores = jnp.where(allowed, scores, -1e30)
        weights = jnp.exp2(scores - jnp.max(scores, axis=2, keepdims=True))
        totals = jnp.sum(weights, axis=2, keepdims=True)
        weighted = jnp.dot(weights.astype(BF16).reshape(512, 384), keys, preferred_element_type=F32)
        weighted = weighted.reshape(4, 128, 128) / totals
        for pair in range(2):
            at = kv * 256 + pair * 128
            joined = jnp.where(low, pltpu.roll(weighted[2 * pair], 64, 1), weighted[2 * pair + 1])
            heads_out[:, at : at + 128] = joined.astype(BF16)

    projected = mix_own[...] + mix_other[...].astype(F32)
    coarse = projected.astype(BF16)
    fine = (projected - coarse.astype(F32)).astype(BF16)
    lane = lax.broadcasted_iota(jnp.int32, (128, 256), 1)
    moved_fine = pltpu.roll(jnp.where((lane >= 100) & (lane < 132), fine.astype(F32), 0.0), 32, 1)
    joined = jnp.where(lane < 132, coarse.astype(F32), moved_fine).astype(BF16)
    mixes[...] = jnp.dot(joined, spread[...], preferred_element_type=F32)
    raw = jnp.dot(coarse, dt_weight[...], preferred_element_type=F32) + params[0:1, :]
    size = jnp.maximum(raw, 0.0) + jnp.log1p(jnp.exp(-jnp.abs(raw)))
    step_size[...] = size
    drive[...] = size * conv[:, 0:CHP].astype(F32)

    def chunk(index, carry):
        lanes = pl.ds(pl.multiple_of(index * 128, 128), 128)
        first = start[0, :, lanes]
        states = [jnp.broadcast_to(first[n : n + 1, :][None], (2, 8, 128)) for n in range(16)]
        for t in range(8):
            rows = slice(16 * t, 16 * t + 16)
            size = step_size[rows, lanes].reshape(2, 8, 128)
            push = drive[rows, lanes].reshape(2, 8, 128)
            total = None
            for n in range(16):
                mix_in = mixes[rows, 128 * n : 128 * n + 128].reshape(2, 8, 128)
                mix_out = mixes[rows, 2048 + 128 * n : 2176 + 128 * n].reshape(2, 8, 128)
                states[n] = jnp.exp2(size * rate[n, :, lanes][None]) * states[n] + push * mix_in
                term = states[n] * mix_out
                total = term if total is None else total + term
            scan_out[rows, lanes] = total.reshape(16, 128)
        return carry

    lax.fori_loop(0, CHP // 128, chunk, 0)
    value = conv[:, 0:CHP].astype(F32)
    result = (scan_out[...] + params[1:2, :] * value) * gate[:, 0:CHP].astype(F32)
    gated_out[...] = result.astype(BF16)


def scan_call(scalars, qkv, cache, mix_own, mix_other, conv, gate, start, decay, dt_weight, params, spread, interpret=False):
    whole = lambda shape: pl.BlockSpec(shape, lambda i, s: (0,) * len(shape))
    rows = lambda width: pl.BlockSpec((128, width), lambda i, s: (i, 0))
    grid_spec = pltpu.PrefetchScalarGridSpec(
        num_scalar_prefetch=1,
        grid=(8,),
        in_specs=[
            rows(768),
            pl.BlockSpec((1, 256, 256), lambda i, s: (s[i], 0, 0)),
            rows(256),
            rows(256),
            rows(CHT),
            rows(CHT),
            pl.BlockSpec((1, 16, CHP), lambda i, s: (s[i], 0, 0)),
            whole((16, CHP)),
            whole((256, CHP)),
            whole((8, CHP)),
            whole((256, 4096)),
        ],
        out_specs=[rows(512), rows(CHP)],
        scratch_shapes=[
            pltpu.VMEM((16, 8, CHP), F32),
            pltpu.VMEM((128, 4096), F32),
            pltpu.VMEM((128, CHP), F32),
            pltpu.VMEM((128, CHP), F32),
            pltpu.VMEM((128, CHP), F32),
        ],
    )
    return pl.pallas_call(
        scan_kernel,
        name="attend_scan",
        grid_spec=grid_spec,
        out_shape=[jax.ShapeDtypeStruct((1024, 512), BF16), jax.ShapeDtypeStruct((1024, CHP), BF16)],
        compiler_params=pltpu.CompilerParams(vmem_limit_bytes=50 << 20),
        interpret=interpret,
    )(scalars, qkv, cache, mix_own, mix_other, conv, gate, start, decay, dt_weight, params, spread)


def output_kernel(heads, gated, weights, odd, out):
    contract = (((1,), (1,)), ((), ()))
    sources = (heads, gated)
    spans = (slice(ATT_AT, ATT_AT + 512), slice(SSM_AT, SSM_AT + CHP))
    lane = lax.broadcasted_iota(jnp.int32, (512, 128), 1)
    for branch in range(2):
        source = sources[branch][...]

        def columns(index, carry, branch=branch, source=source):
            rot, half = index // 2, index % 2
            block = weights[pl.ds(pl.multiple_of(index * 256, 256), 256), spans[branch]]
            part = lax.dot_general(source, block, contract, preferred_element_type=F32).astype(BF16)
            lanes = pl.ds(pl.multiple_of(rot * 256, 256), 256)
            out[half, :, branch, :, lanes] = part.reshape(4, 128, 256)
            return carry

        lax.fori_loop(0, 6, columns, 0)
        part = lax.dot_general(source, odd[:, spans[branch]], contract, preferred_element_type=F32)
        out[0, :, branch, :, 768:896] = jnp.where(lane < 32, part, 0.0).astype(BF16).reshape(4, 128, 128)
        part = jnp.where((lane >= 32) & (lane < 64), part, 0.0)
        out[1, :, branch, :, 768:896] = part.astype(BF16).reshape(4, 128, 128)


def output_call(heads, gated, weights, odd, interpret=False):
    return pl.pallas_call(
        output_kernel,
        name="output_products",
        grid=(2,),
        in_specs=[
            pl.BlockSpec((512, 512), lambda i: (i, 0)),
            pl.BlockSpec((512, CHP), lambda i: (i, 0)),
            pl.BlockSpec((1536, 2176), lambda i: (0, 0), pipeline_mode=pl.Buffered(1)),
            pl.BlockSpec((128, 2176), lambda i: (0, 0)),
        ],
        out_specs=pl.BlockSpec((2, 4, 2, 128, HP), lambda i: (0, i, 0, 0, 0)),
        out_shape=jax.ShapeDtypeStruct((2, 8, 2, 128, HP), BF16),
        compiler_params=pltpu.CompilerParams(vmem_limit_bytes=50 << 20),
        interpret=interpret,
    )(heads, gated, weights, odd)


def combine(mine, theirs):
    return mine.astype(F32) + theirs.astype(F32)


def deliver_kernel(
    parts, own, gains, live, served, mine, theirs, squares, other_squares, mixed, send, recv, local_sem
):
    pos, tc = torus_position()
    rep, tr = lax.axis_index("rep"), lax.axis_index("tr")
    partner = (rep, tr, 1 - tc)
    barrier = pltpu.get_barrier_semaphore()
    pl.semaphore_signal(barrier, inc=1, device_id=partner, device_id_type=MESH)
    for k in range(1, 8):
        pl.semaphore_signal(barrier, inc=1, device_id=((rep + k) % 8, tr, tc), device_id_type=MESH)
    pl.semaphore_wait(barrier, 8)

    def part_copy(k):
        return pltpu.make_async_remote_copy(
            src_ref=parts.at[1 - tc, k],
            dst_ref=theirs.at[k],
            send_sem=send.at[k],
            recv_sem=recv.at[k],
            device_id=partner,
            device_id_type=MESH,
        )

    def square_copy(k):
        return pltpu.make_async_remote_copy(
            src_ref=squares.at[k],
            dst_ref=other_squares.at[k],
            send_sem=send.at[8 + k],
            recv_sem=recv.at[8 + k],
            device_id=partner,
            device_id_type=MESH,
        )

    def result_copy(k):
        return pltpu.make_async_remote_copy(
            src_ref=mixed.at[k],
            dst_ref=served.at[rep],
            send_sem=send.at[16 + k],
            recv_sem=recv.at[16 + k],
            device_id=((rep + k) % 8, tr, tc),
            device_id_type=MESH,
        )

    for k in range(8):
        part_copy(k).start()
    keep = pltpu.make_async_copy(parts.at[tc], mine, local_sem.at[0])
    keep.start()
    keep.wait()
    lane = lax.broadcasted_iota(jnp.int32, (128, 128), 1)

    def sums(k, carry):
        part_copy(k).wait_recv()
        attn = combine(mine[k, 0], theirs[k, 0])
        ssm = combine(mine[k, 1], theirs[k, 1])
        attn_sq = jnp.sum(attn * attn, axis=1, keepdims=True)
        ssm_sq = jnp.sum(ssm * ssm, axis=1, keepdims=True)
        squares[k] = jnp.where(lane < 64, attn_sq, ssm_sq)
        square_copy(k).start()
        return carry

    lax.fori_loop(0, 8, sums, 0)

    def finish(k):
        square_copy(k).wait_recv()
        total = squares[k] + other_squares[k]
        attn_rms = lax.rsqrt(total[:, 0:1] / D + EPSILON)
        ssm_rms = lax.rsqrt(total[:, 64:65] / D + EPSILON)
        attn = combine(mine[k, 0], theirs[k, 0]) * attn_rms * gains[1:2, :]
        ssm = combine(mine[k, 1], theirs[k, 1]) * ssm_rms * gains[2:3, :]
        value = own[k].astype(F32) + 0.5 * (attn + ssm)
        mixed[k] = jnp.where(live[k, :, 0:1] > 0.0, value, 0.0).astype(BF16)

    finish(0)
    stay = pltpu.make_async_copy(mixed.at[0], served.at[rep], local_sem.at[1])
    stay.start()

    def results(k, carry):
        finish(k)
        result_copy(k).start()
        return carry

    lax.fori_loop(1, 8, results, 0)
    stay.wait()
    for k in range(1, 8):
        result_copy(k).wait()
    for k in range(8):
        part_copy(k).wait_send()
        square_copy(k).wait_send()


def deliver_call(parts, own, gains, live):
    vmem = pl.BlockSpec(memory_space=pltpu.VMEM)
    return pl.pallas_call(
        deliver_kernel,
        name="deliver",
        out_shape=jax.ShapeDtypeStruct((8, 128, HP), BF16),
        in_specs=[ANY, vmem, vmem, vmem],
        out_specs=ANY,
        scratch_shapes=[
            pltpu.VMEM((8, 2, 128, HP), BF16),
            pltpu.VMEM((8, 2, 128, HP), BF16),
            pltpu.VMEM((8, 128, 128), F32),
            pltpu.VMEM((8, 128, 128), F32),
            pltpu.VMEM((8, 128, HP), BF16),
            pltpu.SemaphoreType.DMA((24,)),
            pltpu.SemaphoreType.DMA((24,)),
            pltpu.SemaphoreType.DMA((2,)),
        ],
        compiler_params=pltpu.CompilerParams(
            collective_id=2, has_side_effects=True, vmem_limit_bytes=50 << 20
        ),
    )(parts, own, gains, live)


def restore_kernel(served, pick, turn, out):
    value = lax.dot_general(
        served[0], pick[...], (((1,), (1,)), ((), ())), preferred_element_type=F32
    ).astype(BF16)
    value = lax.dot_general(turn[...], value, (((0,), (0,)), ((), ())), preferred_element_type=F32)
    out[0] = value.astype(BF16)


def restore_call(served, pick, turn, interpret=False):
    return pl.pallas_call(
        restore_kernel,
        name="restore",
        grid=(8,),
        in_specs=[
            pl.BlockSpec((1, 128, HP), lambda i: (i, 0, 0)),
            pl.BlockSpec((HALF, HP), lambda i: (0, 0)),
            pl.BlockSpec((128, 128), lambda i: (0, 0)),
        ],
        out_specs=pl.BlockSpec((1, 128, HALF), lambda i: (i, 0, 0)),
        out_shape=jax.ShapeDtypeStruct((8, 128, HALF), BF16),
        compiler_params=pltpu.CompilerParams(vmem_limit_bytes=50 << 20),
        interpret=interpret,
    )(served, pick, turn)


def pad_to(value, axis, size):
    widths = [(0, 0)] * value.ndim
    widths[axis] = (0, size - value.shape[axis])
    return jnp.pad(value, widths)


def pack_shard(pieces, odd_columns):
    rows = jnp.concatenate(pieces, axis=1)
    odd = pad_to(rows[24], 0, 24 * odd_columns).reshape(8, 3, odd_columns).swapaxes(0, 1)
    return jnp.concatenate([rows[:24].reshape(3, 8, rows.shape[1]), odd], axis=2)


def unpack_odd(gathered, at):
    odd = gathered[..., at:].transpose(1, 2, 3, 4, 0, 5).reshape(64, -1)
    return pad_to(odd[:, :at], 0, 128)


def picks():
    table = jnp.asarray(feature_table())
    return (table[:, None, :] == jnp.arange(HALF, dtype=jnp.int32)[None, :, None]).astype(BF16)


def turning():
    row = jnp.arange(128, dtype=jnp.int32)
    return (((row % 16) * 8 + row // 16)[:, None] == row[None, :]).astype(BF16)


def spreading():
    row = jnp.arange(256, dtype=jnp.int32)[:, None]
    target = jnp.arange(4096, dtype=jnp.int32)[None, :] // 128
    return ((row == 100 + target) | (row == 132 + target)).astype(BF16)


def local(
    tokens,
    prefix_kv,
    ssm_state,
    conv_state,
    prefix_len,
    group_size,
    serve_replica,
    in_gain,
    w_query,
    w_keyval,
    w_inner,
    conv_weight,
    conv_bias,
    w_xproj,
    dt_weight,
    dt_bias,
    decay_log,
    skip_gain,
    w_attn_out,
    w_ssm_out,
    attn_gain,
    ssm_gain,
):
    rep, tr, tc = lax.axis_index("rep"), lax.axis_index("tr"), lax.axis_index("tc")
    block = (rep * 8 + tr) * 8
    table = jnp.stack([serve_replica, prefix_len, group_size])
    mine = lax.dynamic_slice(table, (0, block), (3, 8))
    hits = mine[0][None, :] == ((rep + jnp.arange(8, dtype=jnp.int32)) % 8)[:, None]
    values = jnp.stack([jnp.arange(8, dtype=jnp.int32), mine[1], mine[2]])
    picked = jnp.sum(jnp.where(hits[None], values[:, None, :], 0), axis=2)
    scalars = picked.reshape(24)

    pick = picks()
    pick = jnp.where(tc == 0, pick, pick[::-1])
    turn = turning()
    gains = jnp.stack(
        [
            in_gain,
            lax.dynamic_slice_in_dim(attn_gain, tc * HALF, HALF),
            lax.dynamic_slice_in_dim(ssm_gain, tc * HALF, HALF),
        ]
    )
    gains = jnp.dot(pad_to(gains, 0, 8), pick[0].astype(F32), precision=lax.Precision.HIGHEST)
    gap = jnp.zeros((SHARD, CHP - CH), BF16)
    in_shard = pack_shard([w_inner[:, 0], gap, w_inner[:, 1], gap, w_query, w_keyval], 256)
    out_shard = pack_shard([w_ssm_out.T, gap, w_attn_out.T], 128)
    x_rows = tokens.reshape(8, 128, HALF)
    gathered, other_rows, other_gains = gather_call(in_shard, x_rows, gains)
    odd = unpack_odd(gathered, IN_ODD)
    history = pad_to(conv_state, 2, CHT)
    taps = pad_to(pad_to(jnp.concatenate([conv_weight, conv_bias[None]]), 0, 8), 1, CHT)
    xproj = pad_to(pad_to(w_xproj, 0, CHT), 1, 256)
    conv, gate, qkv, mix, own, out_gathered, other_mix = project_call(
        scalars,
        x_rows,
        other_rows,
        gains,
        other_gains,
        pick,
        turn,
        gathered.reshape(1536, IN_COLS),
        odd,
        history,
        taps,
        xproj,
        out_shard,
    )
    params = pad_to(pad_to(jnp.stack([dt_bias, skip_gain]), 0, 8), 1, CHP)
    heads, gated = scan_call(
        scalars,
        qkv,
        prefix_kv,
        mix,
        other_mix,
        conv,
        gate,
        pad_to(ssm_state, 2, CHP),
        pad_to(decay_log, 1, CHP),
        pad_to(pad_to(dt_weight, 0, 256), 1, CHP),
        params,
        spreading(),
    )
    parts = output_call(
        heads, gated, out_gathered.reshape(1536, OUT_COLS), unpack_odd(out_gathered, OUT_ODD)
    )
    live = (jnp.arange(128, dtype=jnp.int32) % 16)[None, :] < picked[2][:, None]
    live = jnp.broadcast_to(live[:, :, None], (8, 128, 128)).astype(F32)
    served = deliver_call(parts, own.reshape(8, 128, HP), gains, live)
    out = restore_call(served, pick[0], turn)
    return out.reshape(8, 16, 8, HALF)


def solution(mesh):
    placed = (
        P(("rep", "tr"), None, None, "tc"),
        P(("rep", "tr"), None, "tc"),
        P(("rep", "tr"), None, "tc"),
        P(("rep", "tr"), None, "tc"),
        P(),
        P(),
        P(),
        P("tc"),
        P(("rep", "tr"), "tc"),
        P(("rep", "tr"), "tc"),
        P(("rep", "tr"), None, "tc"),
        P(None, "tc"),
        P("tc"),
        P("tc", None),
        P(None, "tc"),
        P("tc"),
        P(None, "tc"),
        P("tc"),
        P("tc", ("rep", "tr")),
        P("tc", ("rep", "tr")),
        P(),
        P(),
    )
    return jax.shard_map(
        local,
        mesh=mesh,
        in_specs=placed,
        out_specs=P(("rep", "tr"), None, None, "tc"),
        check_vma=False,
    )
```

time: 1660 us -> 252 us (0.15)
  waiting for transfers between devices: 963 us -> 0 us
  Pallas kernels: 0 us -> 232 us
  blocking collectives: 225 us -> 0 us
  local copies, waits for them, and re-layouts: 186 us -> 10 us
  other arithmetic: 177 us -> 6.27 us
  matrix products: 71.2 us -> 1.32 us
    all_gather x5 -> x0, waiting for transfers between devices: 948 us -> none  [the longest x1 331 us: local(): lax.all_gather(w_attn_out, ('rep', 'tr'), axis=1, tiled=True)]
    pallas_call x0 -> x6, Pallas kernels: none -> 232 us  [the longest x1 61.9 us: gather_call(): pl.pallas_call(gather_kernel, name='gather_weights', out_shape=(jax.Shape...]
    all_gather x1 -> x0, blocking collectives: 187 us -> none  [local(): lax.all_gather(w_keyval, ('rep', 'tr'), axis=0, tiled=True)]
    reduce_sum x28 -> x1, other arithmetic: 109 us -> 0.15 us  [local(): picked = jnp.sum(jnp.where(hits[None], values[:, None, :], 0), axis=2)]
    dot_general x39 -> x1, matrix products: 71.2 us -> 1.32 us  [local(): jnp.dot(pad_to(gains, 0, 8), pick[0].astype(F32), precision=lax.Precision...]
    dynamic_slice x60 -> x2, local copies, waits for them, and re-layouts: 51.1 us -> 1.54 us  [the longest x1 0.77 us: local(): lax.dynamic_slice_in_dim(attn_gain, tc * HALF, HALF)]
    unnamed x50 -> x48, local copies, waits for them, and re-layouts: 40.4 us -> 2.21 us
    all_to_all x1 -> x0, blocking collectives: 32.8 us -> none  [local(): lax.all_to_all(jnp.take(tokens, send_order, axis=0), 'rep', split_axis=0,...]
  transfers between devices with their start and end apart: 11 -> 0, of which waited for: 7 -> 0; matrix products, arithmetic and copies ran while one was open for 26% -> 0% of each run, Pallas kernels for 0% -> 0%
where the time goes in v1:
time: 252 us; the launch traced here: 250 us
  Pallas kernels  232 us (92%)
  local copies, waits for them, and re-layouts  10 us (4%)
  other arithmetic  6.27 us (2%)
    pallas_call x1, Pallas kernels, gather_call(): pl.pallas_call(gather_kernel, name='gather_weights', out_shape=(jax.Shape...  61.9 us
    pallas_call x1, Pallas kernels, project_call(): pl.pallas_call(project_kernel, name='project', grid_spec=grid_spec, out_s...  61.8 us
    pallas_call x1, Pallas kernels, scan_call(): pl.pallas_call(scan_kernel, name='attend_scan', grid_spec=grid_spec, out_...  47.2 us
    pallas_call x1, Pallas kernels, deliver_call(): pl.pallas_call(deliver_kernel, name='deliver', out_shape=jax.ShapeDtypeSt...  33.9 us
    pallas_call x1, Pallas kernels, output_call(): pl.pallas_call(output_kernel, name='output_products', grid=(2,), in_specs...  19.7 us
    pallas_call x1, Pallas kernels, restore_call(): pl.pallas_call(restore_kernel, name='restore', grid=(8,), in_specs=[pl.Bl...  7.5 us

profile of v1, /device:TPU:0, one launch (start us, length us, event | category | flops | bytes accessed | tf_op | source)
XLA Modules:
  0.0 250.3 jit_solution(7537912477563790055)
XLA Ops:
  0.0 0.8 dynamic_slice.10
  0.8 0.8 dynamic_slice.11
  1.6 1.7 fusion
  3.3 0.6 reverse_select_fusion.pick
  4.0 1.7 copy-done.3
  5.7 1.3 fusion.4.gains.own_gains
  7.0 0.2 fusion.23
  7.3 0.1 concatenate.15
  7.5 0.7 pad_maximum_fusion.shard
  8.2 61.9 %gather_weights.1 = (bf16[3,4,4,4,8,4352]{5,4,3,2,1,0:T(8,128)(2,1)}, bf16[8,128,800]{2,1,0:T(8,128)(2,1)}, f32[8,896]{1,0:T(8,128)}) custom-call(bf16[3,8,4352]{2,1,0:T(8,128)(2,1)} %pad_maximum_fusion.shard, bf16[8,128,800]{2,1,0:T(8,128)(2,1)} %bitcast.38, f32[8,896]{1,0:T(8,128)} %fusion.4.gains.own_gains), custom_call_target="tpu_custom_call" | custom-call | tf_op jit(solution)/shard_map/gather_weights/pallas_call | solution.py:240
  70.1 1.2 slice_bitcast_fusion.1
  71.4 0.7 copy.40
  72.1 1.1 reshape.191
  73.4 0.1 fusion.17
  73.5 0.1 broadcast_compare_fusion
  73.6 0.1 select_reduce_fusion
  73.8 0.1 reshape.186.scalars
  73.9 0.1 concatenate.18
  74.1 0.1 fusion.3.turn
  74.2 0.3 copy.42
  74.5 0.1 pad.101.xproj
  74.9 61.8 %project.1 = (bf16[1024,1792]{1,0:T(8,128)(2,1)}, bf16[1024,1792]{1,0:T(8,128)(2,1)}, bf16[1024,768]{1,0:T(8,128)(2,1)}, f32[1024,256]{1,0:T(8,128)S(1)}, bf16[1...) custom-call(s32[24]{0:T(128)S(1)} %reshape.186.scalars, ...), custom_call_target="tpu_custom_call" | custom-call | tf_op jit(solution)/shard_map/project/pallas_call | solution.py:453
  136.8 2.7 %fusion.2.spread = bf16[256,4096]{1,0:T(8,128)(2,1)} fusion(s32[4096]{0:T(1024)S(1)} %get-tuple-element.35, s32[4096]{0:T(1024)S(1)} %get-tuple-element.36), kind=kLoop, calls=%fused_computation.6 | loop fusion | flops 4194304 | bytes 2129920 | tf_op jit(solution)/shard_map/convert_element_type | solution.py:821
  139.7 47.2 %attend_scan.1 = (bf16[1024,512]{1,0:T(8,128)(2,1)S(1)}, bf16[1024,1664]{1,0:T(8,128)(2,1)}) custom-call(s32[24]{0:T(128)S(1)} %reshape.186.scalars, bf16[1024,768]{1,0:T(8,128)(2,1)} %get-tuple-element.20.qkv, bf16[8,256,256]{2,1,0:T(8,128)(2,1)} %cache.1, f32[1024,256]{1,0:T(8,128)} %copy-done, bf16[1024,256]{1,0:T(8,128)(2,1)S(1)} %get-tuple-element.22.mix_other, ...), custom_call_target="tpu_custom_call" | custom-call | tf_op jit(solution)/shard_map/attend_scan/pallas_call | solution.py:598
  187.0 1.0 slice_bitcast_fusion.2
  188.0 0.3 copy.44
  188.3 0.3 reshape.195
  188.7 19.7 %output_products.1.parts = bf16[2,8,2,128,896]{4,3,2,1,0:T(8,128)(2,1)} custom-call(bf16[1024,512]{1,0:T(8,128)(2,1)S(1)} %get-tuple-element.25.heads, bf16[1024,1664]{1,0:T(8,128)(2,1)} %get-tuple-element.26.gated, bf16[1536,2304]{1,0:T(8,128)(2,1)} %bitcast.37, bf16[128,2176]{1,0:T(8,128)(2,1)S(1)} %pad.79.odd), custom_call_target="tpu_custom_call" | custom-call | tf_op jit(solution)/shard_map/output_products/pallas_call | solution.py:632
  208.6 0.2 broadcast_in_dim.47.live
  208.8 33.9 %deliver.1.served = bf16[8,128,896]{2,1,0:T(8,128)(2,1)S(1)} custom-call(bf16[2,8,2,128,896]{4,3,2,1,0:T(8,128)(2,1)} %output_products.1.parts, bf16[8,128,896]{2,1,0:T(8,128)(2,1)} %bitcast.40, f32[8,896]{1,0:T(8,128)S(1)} %copy-done.1, f32[8,128,128]{2,1,0:T(8,128)S(1)} %broadcast_in_dim.47.live), custom_call_target="tpu_custom_call" | custom-call | tf_op jit(solution)/shard_map/deliver/pallas_call | solution.py:744
  242.7 0.1 slice_bitcast_fusion.pick
  242.8 7.5 %restore.1 = bf16[8,128,800]{2,1,0:T(8,128)(2,1)} custom-call(bf16[8,128,896]{2,1,0:T(8,128)(2,1)S(1)} %deliver.1.served, bf16[800,896]{1,0:T(8,128)(2,1)S(1)} %slice_bitcast_fusion.pick, bf16[128,128]{1,0:T(8,128)(2,1)S(1)} %fusion.3.turn), custom_call_target="tpu_custom_call" | custom-call | tf_op jit(solution)/shard_map/restore/pallas_call | solution.py:775
  (86 shorter events, 1.0 us)
Async XLA Ops:
  3.3 0.7 copy-start.19
  3.3 3.7 %copy-start.6 = (bf16[25,2,1600]{2,1,0:T(2,128)(2,1)S(1)}, bf16[25,2,1600]{2,1,0:T(2,128)(2,1)}, u32[]{:S(2)}) copy-start(bf16[25,2,1600]{2,1,0:T(2,128)(2,1)} %param.33) | copy-start | bytes 480004
  3.3 4.0 %copy-start.12 = (bf16[25,512]{1,0:T(8,128)(2,1)S(1)}, bf16[25,512]{1,0:T(8,128)(2,1)}, u32[]{:S(2)}) copy-start(bf16[25,512]{1,0:T(8,128)(2,1)} %param.31) | copy-start | bytes 76804
  3.3 3.9 %copy-start.15 = (bf16[25,256]{1,0:T(8,128)(2,1)S(1)}, bf16[25,256]{1,0:T(8,128)(2,1)}, u32[]{:S(2)}) copy-start(bf16[25,256]{1,0:T(8,128)(2,1)} %param.32) | copy-start | bytes 38404
  4.0 1.7 copy-start.3
  71.3 2.1 copy-start.20
  71.3 2.1 copy-start.21
  71.3 2.1 copy-start.22
  71.4 2.5 copy-start.10
  71.4 2.5 copy-start.13
  72.1 2.1 copy-start.7
  73.3 1.4 copy-start.9
  73.3 1.5 copy-start.16
  73.3 1.5 copy-start.14
  73.3 1.5 copy-start.1
  73.3 1.5 copy-start.2
  74.9 64.6 %copy-start.8 = (bf16[100,1600]{1,0:T(8,128)(2,1)S(1)}, bf16[100,1600]{1,0:T(8,128)(2,1)}, u32[]{:S(2)}) copy-start(bf16[100,1600]{1,0:T(8,128)(2,1)} %param.37) | copy-start | bytes 960004
  136.7 2.8 %copy-start = (f32[1024,256]{1,0:T(8,128)}, f32[1024,256]{1,0:T(8,128)S(1)}, u32[]{:S(2)}) copy-start(f32[1024,256]{1,0:T(8,128)S(1)} %get-tuple-element.21.mix_own) | copy-start | bytes 3145732
  136.7 2.8 %copy-start.5 = (f32[8,16,1600]{2,1,0:T(8,128)S(1)}, f32[8,16,1600]{2,1,0:T(8,128)}, u32[]{:S(2)}) copy-start(f32[8,16,1600]{2,1,0:T(8,128)} %param.25) | copy-start | bytes 2457604
  136.7 2.9 %copy-start.17 = (f32[1600]{0:T(1024)S(1)}, f32[1600]{0:T(1024)}, u32[]{:S(2)}) copy-start(f32[1600]{0:T(1024)} %param.38) | copy-start | bytes 19204
  136.7 2.9 %copy-start.18 = (f32[1600]{0:T(1024)S(1)}, f32[1600]{0:T(1024)}, u32[]{:S(2)}) copy-start(f32[1600]{0:T(1024)} %param.40) | copy-start | bytes 19204
  136.7 3.0 %copy-start.11 = (f32[16,1600]{1,0:T(8,128)S(1)}, f32[16,1600]{1,0:T(8,128)}, u32[]{:S(2)}) copy-start(f32[16,1600]{1,0:T(8,128)} %param.39) | copy-start | bytes 307204
  208.8 33.9 %copy-start.4 = (bf16[2,800,896]{2,1,0:T(8,128)(2,1)S(1)}, bf16[2,800,896]{2,1,0:T(8,128)(2,1)}, u32[]{:S(2)}) copy-start(bf16[2,800,896]{2,1,0:T(8,128)(2,1)} %copy-done.3) | copy-start | bytes 8601604

commit v2 on v1

v2 whole, which is shorter than its diff:
```python
import functools

import jax
import jax.numpy as jnp
import numpy as np
from jax import lax
from jax.experimental import pallas as pl
from jax.experimental.pallas import tpu as pltpu
from jax.sharding import PartitionSpec as P

D = 1600
HD = 64
QH = 16
KVH = 4
EPSILON = 1e-06
LOG2E = 1.4426950408889634

SHARD = 25
CONV_AT, GATE_AT, QKV_AT, IN_ODD, IN_COLS = 0, 1664, 3328, 4096, 4352
SSM_AT, ATT_AT, OUT_ODD, OUT_COLS = 0, 1664, 2176, 2304
CH = 1600
CHP = 1664
CHT = 1792
HALF = 800
HP = 896
MESH = pl.DeviceIdType.MESH
ANY = pl.BlockSpec(memory_space=pl.ANY)
F32 = jnp.float32
BF16 = jnp.bfloat16


def feature_table():
    table = np.full((2, HP), -1, np.int32)
    for half in range(2):
        at = 0
        for rot in range(3):
            for ylo in range(2):
                for x in range(4):
                    for z in range(4):
                        device = x * 8 + ylo * 4 + z
                        for j in range(8):
                            table[half, at] = device * SHARD + rot * 8 + j
                            at += 1
        for ylo in range(2):
            for x in range(4):
                for z in range(4):
                    device = x * 8 + ylo * 4 + z
                    table[half, 768 + 32 * half + ylo * 16 + x * 4 + z] = device * SHARD + 24
    return table


def torus_position():
    rep, tr, tc = lax.axis_index("rep"), lax.axis_index("tr"), lax.axis_index("tc")
    return {"x": rep % 4, "y": (rep // 4) * 2 + tr // 4, "z": tr % 4}, tc


def device_at(pos, tc):
    return ((pos["y"] // 2) * 4 + pos["x"], (pos["y"] % 2) * 4 + pos["z"], tc)


def moved(pos, axis, step):
    out = dict(pos)
    out[axis] = (pos[axis] + step + 4) % 4
    return out


ORDERS = (("x", "y", "z"), ("y", "z", "x"), ("z", "x", "y"))


class Ring:
    def __init__(self, rot, axis, span, offset_axis, offset, split, source, gathered, sems, slot, pos, tc):
        self.pos, self.tc, self.axis = pos, tc, axis
        self.rot, self.span, self.offset_axis, self.offset, self.split = rot, span, offset_axis, offset, split
        self.source, self.gathered = source, gathered
        self.send, self.recv, self.slot = sems[0], sems[1], slot

    def view(self, home, part=None):
        index = [self.rot]
        for name in ("y", "x", "z"):
            if name in self.span:
                if part is not None and self.split == name:
                    index.append(pl.ds(2 * part, 2))
                else:
                    index.append(pl.ds(0, 4))
            else:
                at = home[name]
                if name == self.offset_axis:
                    at = (at + self.offset + 4) % 4
                index.append(at)
        if part is not None and self.split is None:
            columns = self.gathered.shape[-1]
            middle = columns // 256 * 128
            index += [slice(None), pl.ds(0, middle) if part == 0 else pl.ds(middle, columns - middle)]
        return self.gathered.at[tuple(index)]

    def copy(self, number):
        step = 1 if number % 2 == 0 else -1
        if number < 2:
            home, part, source = self.pos, None, self.source
        else:
            home, part, source = moved(self.pos, self.axis, -step), number - 2, None
        there = self.view(home, part)
        return pltpu.make_async_remote_copy(
            src_ref=there if source is None else source,
            dst_ref=there,
            send_sem=self.send.at[self.slot + number],
            recv_sem=self.recv.at[self.slot + number],
            device_id=device_at(moved(self.pos, self.axis, step), self.tc),
            device_id_type=MESH,
        )

    def start(self):
        self.copy(0).start()
        self.copy(1).start()

    def forward(self):
        for number in (0, 1):
            self.copy(number).wait_recv()
            self.copy(number + 2).start()

    def finish(self):
        self.copy(2).wait_recv()
        self.copy(3).wait_recv()

    def drain(self):
        for number in range(4):
            self.copy(number).wait_send()


class Gather:
    def __init__(self, shard, gathered, send, recv, local_sem, pos, tc):
        sems = (send, recv)
        self.kept = [
            pltpu.make_async_copy(
                shard.at[rot], gathered.at[rot, pos["y"], pos["x"], pos["z"]], local_sem.at[rot]
            )
            for rot in range(3)
        ]
        first, second, third = [], [], []
        for rot, (one, two, three) in enumerate(ORDERS):
            at = rot * 24
            first.append(Ring(rot, one, (), None, 0, None, shard.at[rot], gathered, sems, at, pos, tc))
            second.append(Ring(rot, two, (one,), None, 0, one, None, gathered, sems, at + 4, pos, tc))
            third.append(
                [
                    Ring(rot, three, (one,), two, offset, one, None, gathered, sems, at + 8 + 4 * n, pos, tc)
                    for n, offset in enumerate((0, 1, -1, 2))
                ]
            )
        self.first, self.second = first, second
        self.third = [[rings[n] for rings in third] for n in range(4)]

    def stage(self, number):
        if number == 0:
            for ring in self.first:
                ring.start()
            for copy in self.kept:
                copy.start()
        if number == 1:
            for ring in self.first:
                ring.forward()
            for copy in self.kept:
                copy.wait()
        if number == 2:
            for ring in self.first:
                ring.finish()
            for ring in self.second + self.third[0]:
                ring.start()
        if number == 3:
            for ring in self.second:
                ring.forward()
            for ring in self.third[1] + self.third[2]:
                ring.start()
            for ring in self.third[0]:
                ring.forward()
        if number == 4:
            for ring in self.second:
                ring.finish()
            for ring in self.third[3]:
                ring.start()
        if number == 5:
            for ring in self.third[1] + self.third[2]:
                ring.forward()
        if number == 6:
            for ring in self.third[3]:
                ring.forward()
        if number == 7:
            for rings in self.third:
                for ring in rings:
                    ring.finish()
            for ring in self.first + self.second:
                ring.drain()
            for rings in self.third:
                for ring in rings:
                    ring.drain()


STAGES = 8
GATHER_SEMS = 72


def greet_torus(pos, tc):
    barrier = pltpu.get_barrier_semaphore()
    for axis in ("x", "y", "z"):
        for step in (1, -1):
            pl.semaphore_signal(
                barrier, inc=1, device_id=device_at(moved(pos, axis, step), tc), device_id_type=MESH
            )
    partner = device_at(pos, 1 - tc)
    pl.semaphore_signal(barrier, inc=1, device_id=partner, device_id_type=MESH)
    pl.semaphore_wait(barrier, 7)
    return partner


def split_gain(gain):
    high = gain.astype(BF16)
    rest = gain - high.astype(F32)
    middle = rest.astype(BF16)
    low = (rest - middle.astype(F32)).astype(BF16)
    return [high, middle, low]


def gather_kernel(
    scalars,
    shard,
    tokens,
    gain,
    pick,
    turn,
    gathered,
    normed,
    other_tokens,
    other_gain,
    turned,
    send,
    recv,
    local_sem,
):
    pos, tc = torus_position()
    partner = greet_torus(pos, tc)
    gather = Gather(shard, gathered, send, recv, local_sem, pos, tc)
    swaps = [
        pltpu.make_async_remote_copy(
            src_ref=here,
            dst_ref=there,
            send_sem=send.at[GATHER_SEMS + n],
            recv_sem=recv.at[GATHER_SEMS + n],
            device_id=partner,
            device_id_type=MESH,
        )
        for n, (here, there) in enumerate(((tokens, other_tokens), (gain, other_gain)))
    ]

    def turn_rows(side, source):
        def body(group, carry):
            value = jnp.dot(turn[...], source[scalars[group]], preferred_element_type=F32)
            turned[side, pl.ds(pl.multiple_of(group * 128, 128), 128), :] = value.astype(BF16)
            return carry

        lax.fori_loop(0, 8, body, 0)

    def prepare(part, carry):
        rows = pl.ds(pl.multiple_of(part * 256, 256), 256)
        values, squares = [], 0.0
        for side, gains in enumerate((gain, other_gain)):
            half = (tc + side) % 2
            value = jnp.dot(turned[side, rows, :], pick[half], preferred_element_type=F32)
            squares = squares + jnp.sum(value * value, axis=1, keepdims=True)
            terms = jnp.concatenate(split_gain(jnp.broadcast_to(gains[0:1, :], (8, HALF))), axis=0)
            placed = jnp.dot(terms, pick[half], preferred_element_type=F32)
            values.append(value * (placed[0:1] + placed[8:9] + placed[16:17]))
        scale = lax.rsqrt(squares / D + EPSILON)
        mine, theirs = values[0] * scale, values[1] * scale
        scaled = [jnp.where(tc == 0, mine, theirs), jnp.where(tc == 0, theirs, mine)]
        for rot in range(3):
            for half in range(2):
                at = rot * 512 + half * 256
                normed[rows, at : at + 256] = scaled[half][:, rot * 256 : rot * 256 + 256].astype(BF16)
        normed[rows, 1536:1664] = (scaled[0][:, 768:] + scaled[1][:, 768:]).astype(BF16)
        return carry

    gather.stage(0)
    for copy in swaps:
        copy.start()
    turn_rows(0, tokens)
    gather.stage(1)
    for copy in swaps:
        copy.wait_recv()
    gather.stage(2)
    turn_rows(1, other_tokens)
    lax.fori_loop(0, 1, prepare, 0)
    gather.stage(3)
    lax.fori_loop(1, 3, prepare, 0)
    gather.stage(4)
    lax.fori_loop(3, 4, prepare, 0)
    for number in range(5, STAGES):
        gather.stage(number)
    for copy in swaps:
        copy.wait_send()


def gather_call(scalars, shard, tokens, gain, pick, turn):
    vmem = pl.BlockSpec(memory_space=pltpu.VMEM)
    return pl.pallas_call(
        gather_kernel,
        name="gather_weights",
        out_shape=(
            jax.ShapeDtypeStruct((3, 4, 4, 4, 8, IN_COLS), BF16),
            jax.ShapeDtypeStruct((1024, 1664), BF16),
        ),
        in_specs=[pl.BlockSpec(memory_space=pltpu.SMEM), vmem, vmem, vmem, vmem, vmem],
        out_specs=(ANY, vmem),
        scratch_shapes=[
            pltpu.VMEM((8, 128, HALF), BF16),
            pltpu.VMEM((8, HALF), F32),
            pltpu.VMEM((2, 1024, HALF), BF16),
            pltpu.SemaphoreType.DMA((GATHER_SEMS + 2,)),
            pltpu.SemaphoreType.DMA((GATHER_SEMS + 2,)),
            pltpu.SemaphoreType.DMA((3,)),
        ],
        compiler_params=pltpu.CompilerParams(
            collective_id=0, has_side_effects=True, vmem_limit_bytes=50 << 20
        ),
    )(scalars, shard, tokens, gain, pick, turn)


def silu(value):
    return 0.5 * value * (1.0 + jnp.tanh(0.5 * value))


def project_kernel(
    normed,
    left,
    right,
    odd_left,
    odd_right,
    history,
    taps,
    xproj,
    shard,
    conv_out,
    gate_out,
    qkv_out,
    mix_out,
    gathered,
    other_mix,
    product,
    sequence,
    mix_send,
    send,
    recv,
    local_sem,
):
    step = pl.program_id(0)
    pos, tc = torus_position()
    gather = Gather(shard, gathered, send, recv, local_sem, pos, tc)
    swap = pltpu.make_async_remote_copy(
        src_ref=mix_send,
        dst_ref=other_mix,
        send_sem=send.at[GATHER_SEMS],
        recv_sem=recv.at[GATHER_SEMS],
        device_id=device_at(pos, 1 - tc),
        device_id_type=MESH,
    )

    @pl.when(step == 0)
    def _():
        greet_torus(pos, tc)
        gather.stage(0)

    for at, number in ((1, 1), (2, 2), (4, 3), (6, 4), (8, 5), (11, 6)):

        @pl.when(step == at)
        def _(number=number):
            gather.stage(number)

    @pl.when(step == 0)
    def _():
        mix_out[...] = jnp.zeros_like(mix_out)

    block = jnp.concatenate([left[...], right[...]], axis=1)
    odd = jnp.concatenate([odd_left[...], odd_right[...]], axis=1)

    def multiply(part, carry):
        rows = pl.ds(pl.multiple_of(part * 512, 512), 512)
        value = jnp.dot(normed[rows, 0:1536], block, preferred_element_type=F32)
        value = value + jnp.dot(normed[rows, 1536:1664], odd, preferred_element_type=F32)
        product[rows, :] = value
        return carry

    lax.fori_loop(0, 2, multiply, 0)

    @pl.when(step < 7)
    def _():
        def convolve(group, carry):
            rows = pl.ds(pl.multiple_of(group * 128, 128), 128)
            for k in range(3):
                sequence[16 * k : 16 * k + 16, :] = jnp.broadcast_to(history[group, k : k + 1, :], (16, 256))
            sequence[48:176, :] = product[rows, :]
            total = jnp.broadcast_to(taps[4:5, :], (128, 256))
            for k in range(4):
                total = total + taps[k : k + 1, :] * sequence[16 * k : 16 * k + 128, :]
            result = silu(total).astype(BF16)
            conv_out[rows, :] = result
            mix_out[rows, :] += jnp.dot(result, xproj[...], preferred_element_type=F32)
            return carry

        lax.fori_loop(0, 8, convolve, 0)

    @pl.when((step >= 7) & (step < 14))
    def _():
        def gating(group, carry):
            rows = pl.ds(pl.multiple_of(group * 128, 128), 128)
            gate_out[rows, :] = silu(product[rows, :]).astype(BF16)
            return carry

        lax.fori_loop(0, 8, gating, 0)

    @pl.when(step == 7)
    def _():
        mix_send[...] = mix_out[...].astype(BF16)
        swap.start()

    @pl.when(step >= 14)
    def _():
        def keep(group, carry):
            rows = pl.ds(pl.multiple_of(group * 128, 128), 128)
            qkv_out[rows, :] = product[rows, :].astype(BF16)
            return carry

        lax.fori_loop(0, 8, keep, 0)

    @pl.when(step == 16)
    def _():
        gather.stage(7)
        swap.wait()


def column_block(step):
    return jnp.where(
        step < 7,
        CONV_AT // 128 + 2 * step,
        jnp.where(step < 14, GATE_AT // 128 + 2 * (step - 7), QKV_AT // 128 + 2 * (step - 14)),
    )


def project_call(normed, weights, odd, history, taps, xproj, shard):
    whole = lambda shape: pl.BlockSpec(shape, lambda i: (0,) * len(shape), pipeline_mode=pl.Buffered(1))
    conv_at = lambda i: jnp.minimum(i, 6)
    return pl.pallas_call(
        project_kernel,
        name="project",
        grid=(17,),
        in_specs=[
            whole((1024, 1664)),
            pl.BlockSpec((1536, 128), lambda i: (0, column_block(i))),
            pl.BlockSpec((1536, 128), lambda i: (0, column_block(i) + 1)),
            pl.BlockSpec((128, 128), lambda i: (0, column_block(i))),
            pl.BlockSpec((128, 128), lambda i: (0, column_block(i) + 1)),
            pl.BlockSpec((8, 3, 256), lambda i: (0, 0, conv_at(i))),
            pl.BlockSpec((8, 256), lambda i: (0, conv_at(i))),
            pl.BlockSpec((256, 256), lambda i: (conv_at(i), 0)),
            whole((3, 8, OUT_COLS)),
        ],
        out_specs=[
            pl.BlockSpec((1024, 256), lambda i: (0, conv_at(i))),
            pl.BlockSpec((1024, 256), lambda i: (0, jnp.clip(i - 7, 0, 6))),
            pl.BlockSpec((1024, 256), lambda i: (0, jnp.clip(i - 14, 0, 2))),
            pl.BlockSpec((1024, 256), lambda i: (0, 0)),
            ANY,
            ANY,
        ],
        scratch_shapes=[
            pltpu.VMEM((1024, 256), F32),
            pltpu.VMEM((176, 256), F32),
            pltpu.VMEM((1024, 256), BF16),
            pltpu.SemaphoreType.DMA((GATHER_SEMS + 1,)),
            pltpu.SemaphoreType.DMA((GATHER_SEMS + 1,)),
            pltpu.SemaphoreType.DMA((3,)),
        ],
        out_shape=[
            jax.ShapeDtypeStruct((1024, CHT), BF16),
            jax.ShapeDtypeStruct((1024, CHT), BF16),
            jax.ShapeDtypeStruct((1024, 768), BF16),
            jax.ShapeDtypeStruct((1024, 256), F32),
            jax.ShapeDtypeStruct((3, 4, 4, 4, 8, OUT_COLS), BF16),
            jax.ShapeDtypeStruct((1024, 256), BF16),
        ],
        compiler_params=pltpu.CompilerParams(
            collective_id=1, has_side_effects=True, vmem_limit_bytes=50 << 20
        ),
    )(normed, weights, weights, odd, odd, history, taps, xproj, shard)


def final_kernel(
    scalars,
    qkv,
    cache,
    mix_own,
    mix_other,
    conv,
    gate,
    start,
    decay,
    dt_weight,
    params,
    weights,
    odd,
    tokens,
    gains,
    unpick,
    turn,
    out,
    rate,
    spread,
    mixes,
    step_size,
    drive,
    scan_out,
    stacked,
    parts,
    theirs,
    squares,
    other_squares,
    wide,
    staged,
    send,
    recv,
    local_sem,
):
    step = pl.program_id(0)
    rep, tr, tc = lax.axis_index("rep"), lax.axis_index("tr"), lax.axis_index("tc")
    partner = (rep, tr, 1 - tc)

    def part_copy(pair):
        return pltpu.make_async_remote_copy(
            src_ref=parts.at[pair, 1],
            dst_ref=theirs.at[pair],
            send_sem=send.at[pair],
            recv_sem=recv.at[pair],
            device_id=partner,
            device_id_type=MESH,
        )

    def square_copy(pair):
        return pltpu.make_async_remote_copy(
            src_ref=squares.at[pair],
            dst_ref=other_squares.at[pair],
            send_sem=send.at[4 + pair],
            recv_sem=recv.at[4 + pair],
            device_id=partner,
            device_id_type=MESH,
        )

    def result_copy(group):
        return pltpu.make_async_remote_copy(
            src_ref=staged.at[group],
            dst_ref=out.at[rep],
            send_sem=send.at[8 + group],
            recv_sem=recv.at[8 + group],
            device_id=((rep + 7 - group) % 8, tr, tc),
            device_id_type=MESH,
        )

    @pl.when(step == 0)
    def _():
        barrier = pltpu.get_barrier_semaphore()
        pl.semaphore_signal(barrier, inc=1, device_id=partner, device_id_type=MESH)
        for k in range(1, 8):
            pl.semaphore_signal(barrier, inc=1, device_id=((rep + k) % 8, tr, tc), device_id_type=MESH)
        pl.semaphore_wait(barrier, 8)
        value = -jnp.exp(decay[...]) * LOG2E
        for n in range(16):
            rate[n] = jnp.broadcast_to(value[n : n + 1, :], (8, CHP))
        row = lax.broadcasted_iota(jnp.int32, (256, 128), 0)
        for n in range(32):
            spread[:, 128 * n : 128 * n + 128] = jnp.where(
                (row == 100 + n) | (row == 132 + n), 1.0, 0.0
            ).astype(BF16)
        squares[...] = jnp.zeros_like(squares)
        terms = [jnp.broadcast_to(gains[n : n + 1, :], (8, HALF)) for n in range(2)]
        terms = jnp.concatenate(split_gain(terms[0]) + split_gain(terms[1]), axis=0)
        placed = lax.dot_general(
            unpick[0, :, 0:HALF], terms, (((0,), (1,)), ((), ())), preferred_element_type=F32
        )
        for n in range(2):
            at = 24 * n
            column = placed[:, at : at + 1] + placed[:, at + 8 : at + 9] + placed[:, at + 16 : at + 17]
            wide[n] = jnp.broadcast_to(0.5 * column, (HALF, 256))

    def joined(pair, branch):
        return parts[pair, 0, branch].astype(F32) + theirs[pair, branch].astype(F32)

    def sums(pair):
        part_copy(pair).wait_recv()
        for branch in range(2):
            value = joined(pair, branch)
            squares[pair, branch : branch + 1, :] = jnp.sum(value * value, axis=0, keepdims=True)
        square_copy(pair).start()

    def finish(pair):
        square_copy(pair).wait_recv()
        total = squares[pair] + other_squares[pair]
        scale = lax.rsqrt(total / D + EPSILON)
        value = joined(pair, 0) * scale[0:1, :] * wide[0] + joined(pair, 1) * scale[1:2, :] * wide[1]
        value = jnp.dot(unpick[0, :, 0:HALF], value.astype(BF16), preferred_element_type=F32).astype(BF16)
        row = lax.broadcasted_iota(jnp.int32, (128, HALF), 0)
        for member in range(2):
            group = 2 * pair + member
            branch = lax.dot_general(
                turn[...],
                value[:, 128 * member : 128 * member + 128],
                (((0,), (1,)), ((), ())),
                preferred_element_type=F32,
            )
            result = tokens[scalars[group]].astype(F32) + branch
            staged[group] = jnp.where(row < 8 * scalars[16 + group], result, 0.0).astype(BF16)

    @pl.when((step % 2 == 0) & (step >= 2))
    def _():
        sums(step // 2 - 1)

    home = scalars[step]
    length = scalars[8 + step]
    column_at = pl.ds(pl.multiple_of((step % 2) * 128, 128), 128)
    row = lax.broadcasted_iota(jnp.int32, (128, 384), 0)
    column = lax.broadcasted_iota(jnp.int32, (128, 384), 1)
    own = column - 256
    causal = (column >= 256) & ((own % 16) == (row % 16)) & ((own // 16) <= (row // 16))
    allowed = (causal | ((column < 256) & (column < length)))[None]
    low = lax.broadcasted_iota(jnp.int32, (128, 128), 1) < 64
    for kv in range(2):
        keys = jnp.concatenate(
            [cache[home, :, kv * 128 : kv * 128 + 128], qkv[:, 512 + kv * 128 : 640 + kv * 128]], axis=0
        )
        queries = []
        for pair in range(2):
            at = kv * 256 + pair * 128
            both = qkv[:, at : at + 128].astype(F32)
            queries.append(jnp.where(low, both, 0.0).astype(BF16))
            queries.append(jnp.where(low, pltpu.roll(both, 64, 1), 0.0).astype(BF16))
        query = jnp.concatenate(queries, axis=0)
        scores = lax.dot_general(query, keys, (((1,), (1,)), ((), ())), preferred_element_type=F32)
        scores = scores.reshape(4, 128, 384) * (HD ** (-0.5) * LOG2E)
        scores = jnp.where(allowed, scores, -1e30)
        probs = jnp.exp2(scores - jnp.max(scores, axis=2, keepdims=True))
        totals = jnp.sum(probs, axis=2, keepdims=True)
        weighted = jnp.dot(probs.astype(BF16).reshape(512, 384), keys, preferred_element_type=F32)
        weighted = weighted.reshape(4, 128, 128) / totals
        for pair in range(2):
            at = ATT_AT + kv * 256 + pair * 128
            heads = jnp.where(low, pltpu.roll(weighted[2 * pair], 64, 1), weighted[2 * pair + 1])
            stacked[at : at + 128, column_at] = heads.T.astype(BF16)

    projected = mix_own[...] + mix_other[...].astype(F32)
    coarse = projected.astype(BF16)
    fine = (projected - coarse.astype(F32)).astype(BF16)
    lane = lax.broadcasted_iota(jnp.int32, (128, 256), 1)
    moved_fine = pltpu.roll(jnp.where((lane >= 100) & (lane < 132), fine.astype(F32), 0.0), 32, 1)
    mix_terms = jnp.where(lane < 132, coarse.astype(F32), moved_fine).astype(BF16)
    mixes[...] = jnp.dot(mix_terms, spread[...], preferred_element_type=F32)
    raw = jnp.dot(coarse, dt_weight[...], preferred_element_type=F32) + params[0:1, :]
    size = jnp.maximum(raw, 0.0) + jnp.log1p(jnp.exp(-jnp.abs(raw)))
    step_size[...] = size
    drive[...] = size * conv[:, 0:CHP].astype(F32)

    def chunk(index, carry):
        at = pl.multiple_of(index * 128, 128)
        lanes = pl.ds(at, 128)
        first = start[home, :, lanes]
        states = [jnp.broadcast_to(first[n : n + 1, :][None], (2, 8, 128)) for n in range(16)]
        for t in range(8):
            rows = slice(16 * t, 16 * t + 16)
            size = step_size[rows, lanes].reshape(2, 8, 128)
            push = drive[rows, lanes].reshape(2, 8, 128)
            total = None
            for n in range(16):
                mix_in = mixes[rows, 128 * n : 128 * n + 128].reshape(2, 8, 128)
                mix_out = mixes[rows, 2048 + 128 * n : 2176 + 128 * n].reshape(2, 8, 128)
                states[n] = jnp.exp2(size * rate[n, :, lanes][None]) * states[n] + push * mix_in
                term = states[n] * mix_out
                total = term if total is None else total + term
            scan_out[rows, :] = total.reshape(16, 128)
        value = conv[:, lanes].astype(F32)
        gated = (scan_out[...] + params[1:2, lanes] * value) * gate[:, lanes].astype(F32)
        stacked[pl.ds(at, 128), column_at] = gated.T.astype(BF16)
        return carry

    lax.fori_loop(0, CHP // 128, chunk, 0)

    @pl.when((step % 2 == 0) & (step >= 2))
    def _():
        pair = step // 2 - 1
        finish(pair)
        result_copy(2 * pair).start()
        result_copy(2 * pair + 1).start()

    @pl.when(step % 2 == 1)
    def _():
        pair = step // 2

        def products(rot, carry):
            rows = pl.ds(pl.multiple_of(rot * 512, 512), 512)
            place = pl.ds(pl.multiple_of(rot * 256, 256), 256)
            for branch, (low_at, high_at) in enumerate(((ATT_AT, ATT_AT + 512), (SSM_AT, SSM_AT + CHP))):
                value = jnp.dot(
                    weights[rows, low_at:high_at], stacked[low_at:high_at, :], preferred_element_type=F32
                ).astype(BF16)
                for half in range(2):
                    parts[pair, (half + tc) % 2, branch, place, :] = value[256 * half : 256 * half + 256]
            return carry

        lax.fori_loop(0, 3, products, 0)
        for branch, (low_at, high_at) in enumerate(((ATT_AT, ATT_AT + 512), (SSM_AT, SSM_AT + CHP))):
            value = jnp.dot(
                odd[0:64, low_at:high_at], stacked[low_at:high_at, :], preferred_element_type=F32
            ).astype(BF16)
            for half in range(2):
                parts[pair, (half + tc) % 2, branch, 768:800, :] = value[32 * half : 32 * half + 32]
        part_copy(pair).start()

    @pl.when(step == 7)
    def _():
        sums(3)
        finish(3)
        result_copy(6).start()
        stay = pltpu.make_async_copy(staged.at[7], out.at[rep], local_sem)
        stay.start()
        for group in range(7):
            result_copy(group).wait()
        stay.wait()
        for pair in range(4):
            part_copy(pair).wait_send()
            square_copy(pair).wait_send()


def final_call(
    scalars, qkv, cache, mix_own, mix_other, conv, gate, start, decay, dt_weight, params, weights, odd,
    tokens, gains, unpick, turn,
):
    whole = lambda shape: pl.BlockSpec(shape, lambda i: (0,) * len(shape), pipeline_mode=pl.Buffered(1))
    rows = lambda width: pl.BlockSpec((128, width), lambda i: (i, 0))
    return pl.pallas_call(
        final_kernel,
        name="attend_scan_deliver",
        grid=(8,),
        in_specs=[
            pl.BlockSpec(memory_space=pltpu.SMEM),
            rows(768),
            whole((8, 256, 256)),
            rows(256),
            rows(256),
            rows(CHT),
            rows(CHT),
            whole((8, 16, CHP)),
            whole((16, CHP)),
            whole((256, CHP)),
            whole((8, CHP)),
            whole((1536, 2176)),
            whole((128, 2176)),
            whole((8, 128, HALF)),
            whole((8, HALF)),
            whole((1, HALF, HP)),
            whole((128, 128)),
        ],
        out_specs=ANY,
        out_shape=jax.ShapeDtypeStruct((8, 128, HALF), BF16),
        scratch_shapes=[
            pltpu.VMEM((16, 8, CHP), F32),
            pltpu.VMEM((256, 4096), BF16),
            pltpu.VMEM((128, 4096), F32),
            pltpu.VMEM((128, CHP), F32),
            pltpu.VMEM((128, CHP), F32),
            pltpu.VMEM((128, 128), F32),
            pltpu.VMEM((2176, 256), BF16),
            pltpu.VMEM((4, 2, 2, HALF, 256), BF16),
            pltpu.VMEM((4, 2, HALF, 256), BF16),
            pltpu.VMEM((4, 8, 256), F32),
            pltpu.VMEM((4, 8, 256), F32),
            pltpu.VMEM((2, HALF, 256), F32),
            pltpu.VMEM((8, 128, HALF), BF16),
            pltpu.SemaphoreType.DMA((16,)),
            pltpu.SemaphoreType.DMA((16,)),
            pltpu.SemaphoreType.DMA,
        ],
        compiler_params=pltpu.CompilerParams(
            collective_id=2, has_side_effects=True, vmem_limit_bytes=58 << 20
        ),
    )(
        scalars, qkv, cache, mix_own, mix_other, conv, gate, start, decay, dt_weight, params, weights, odd,
        tokens, gains, unpick, turn,
    )


def pad_to(value, axis, size):
    widths = [(0, 0)] * value.ndim
    widths[axis] = (0, size - value.shape[axis])
    return jnp.pad(value, widths)


def pack_shard(pieces, odd_columns):
    rows = jnp.concatenate(pieces, axis=1)
    odd = pad_to(rows[24], 0, 24 * odd_columns).reshape(8, 3, odd_columns).swapaxes(0, 1)
    return jnp.concatenate([rows[:24].reshape(3, 8, rows.shape[1]), odd], axis=2)


def unpack_odd(gathered, at):
    odd = gathered[..., at:].transpose(1, 2, 3, 4, 0, 5).reshape(64, -1)
    return pad_to(odd[:, :at], 0, 128)


def picks():
    table = jnp.asarray(feature_table())
    return (table[:, None, :] == jnp.arange(HALF, dtype=jnp.int32)[None, :, None]).astype(BF16)


def turning():
    row = jnp.arange(128, dtype=jnp.int32)
    return (((row % 16) * 8 + row // 16)[:, None] == row[None, :]).astype(BF16)


def local(
    tokens,
    prefix_kv,
    ssm_state,
    conv_state,
    prefix_len,
    group_size,
    serve_replica,
    in_gain,
    w_query,
    w_keyval,
    w_inner,
    conv_weight,
    conv_bias,
    w_xproj,
    dt_weight,
    dt_bias,
    decay_log,
    skip_gain,
    w_attn_out,
    w_ssm_out,
    attn_gain,
    ssm_gain,
):
    rep, tr, tc = lax.axis_index("rep"), lax.axis_index("tr"), lax.axis_index("tc")
    block = (rep * 8 + tr) * 8
    table = jnp.stack([serve_replica, prefix_len, group_size])
    mine = lax.dynamic_slice(table, (0, block), (3, 8))
    hits = mine[0][None, :] == ((rep + 7 - jnp.arange(8, dtype=jnp.int32)) % 8)[:, None]
    values = jnp.stack([jnp.arange(8, dtype=jnp.int32), mine[1], mine[2]])
    picked = jnp.sum(jnp.where(hits[None], values[:, None, :], 0), axis=2)
    scalars = picked.reshape(24)

    order = picked[0]
    pick = picks()
    turn = turning()
    gap = jnp.zeros((SHARD, CHP - CH), BF16)
    in_shard = pack_shard([w_inner[:, 0], gap, w_inner[:, 1], gap, w_query, w_keyval], 256)
    out_shard = pack_shard([w_ssm_out.T, gap, w_attn_out.T], 128)
    x_rows = tokens.reshape(8, 128, HALF)
    in_gains = pad_to(in_gain[None], 0, 8)
    gathered, normed = gather_call(scalars, in_shard, x_rows, in_gains, pick, turn)
    history = pad_to(jnp.take(conv_state, order, axis=0), 2, CHT)
    taps = pad_to(pad_to(jnp.concatenate([conv_weight, conv_bias[None]]), 0, 8), 1, CHT)
    xproj = pad_to(pad_to(w_xproj, 0, CHT), 1, 256)
    conv, gate, qkv, mix, out_gathered, other_mix = project_call(
        normed,
        gathered.reshape(1536, IN_COLS),
        unpack_odd(gathered, IN_ODD),
        history,
        taps,
        xproj,
        out_shard,
    )
    params = pad_to(pad_to(jnp.stack([dt_bias, skip_gain]), 0, 8), 1, CHP)
    gains = jnp.stack(
        [
            lax.dynamic_slice_in_dim(attn_gain, tc * HALF, HALF),
            lax.dynamic_slice_in_dim(ssm_gain, tc * HALF, HALF),
        ]
    )
    out = final_call(
        scalars,
        qkv,
        prefix_kv,
        mix,
        other_mix,
        conv,
        gate,
        pad_to(ssm_state, 2, CHP),
        pad_to(decay_log, 1, CHP),
        pad_to(pad_to(dt_weight, 0, 256), 1, CHP),
        params,
        out_gathered.reshape(1536, OUT_COLS),
        unpack_odd(out_gathered, OUT_ODD),
        x_rows,
        pad_to(gains, 0, 8),
        pick,
        turn,
    )
    return out.reshape(8, 16, 8, HALF)


def solution(mesh):
    placed = (
        P(("rep", "tr"), None, None, "tc"),
        P(("rep", "tr"), None, "tc"),
        P(("rep", "tr"), None, "tc"),
        P(("rep", "tr"), None, "tc"),
        P(),
        P(),
        P(),
        P("tc"),
        P(("rep", "tr"), "tc"),
        P(("rep", "tr"), "tc"),
        P(("rep", "tr"), None, "tc"),
        P(None, "tc"),
        P("tc"),
        P("tc", None),
        P(None, "tc"),
        P("tc"),
        P(None, "tc"),
        P("tc"),
        P("tc", ("rep", "tr")),
        P("tc", ("rep", "tr")),
        P(),
        P(),
    )
    return jax.shard_map(
        local,
        mesh=mesh,
        in_specs=placed,
        out_specs=P(("rep", "tr"), None, None, "tc"),
        check_vma=False,
    )
```

time: 252 us -> 233 us (0.925)
  Pallas kernels: 232 us -> 210 us
  local copies, waits for them, and re-layouts: 10 us -> 16.3 us
    pallas_call x5 -> x2, Pallas kernels: 170 us -> 145 us  [the longest x1 94.2 us: final_call(): pl.pallas_call(final_kernel, name='attend_scan_deliver', grid=(8,), in_sp...]
    pad x11 -> x12, local copies, waits for them, and re-layouts: 0.45 us -> 4.36 us  [pad_to(): return jnp.pad(value, widths)]
    pallas_call x1, Pallas kernels: 61.9 us -> 64.8 us  [gather_call(): pl.pallas_call(gather_kernel, name='gather_weights', out_shape=(jax.Shape...]
    convert_element_type x2 -> x0, other arithmetic: 2.79 us -> none  [the longest x1 2.71 us: spreading(): return ((row == 100 + target) | (row == 132 + target)).astype(BF16)]
where the time goes in v2:
time: 233 us; the launch traced here: 231 us
  Pallas kernels  210 us (90%)
  local copies, waits for them, and re-layouts  16.3 us (7%)
  other arithmetic  4.58 us (2%)
    pallas_call x1, Pallas kernels, final_call(): pl.pallas_call(final_kernel, name='attend_scan_deliver', grid=(8,), in_sp...  94.2 us
    pallas_call x1, Pallas kernels, gather_call(): pl.pallas_call(gather_kernel, name='gather_weights', out_shape=(jax.Shape...  64.8 us
    pallas_call x1, Pallas kernels, project_call(): pl.pallas_call(project_kernel, name='project', grid=(17,), in_specs=[whol...  50.7 us

profile of v2, /device:TPU:0, one launch (start us, length us, event | category | flops | bytes accessed | tf_op | source)
XLA Modules:
  0.0 231.2 jit_solution(709314550679648512)
XLA Ops:
  0.0 0.8 fusion.3
  0.9 0.1 broadcast_compare_fusion
  0.9 0.1 select_reduce_fusion
  1.1 0.8 gather_fusion
  2.0 0.1 copy_select_fusion
  2.1 0.1 reshape.135.scalars
  2.2 1.4 fusion.8
  3.7 0.1 concatenate.15
  4.0 2.6 %fusion.pick.unpick = bf16[2,800,896]{2,1,0:T(8,128)(2,1)} fusion(s32[2,896]{1,0:T(2,128)S(1)} %copy-done.18), kind=kLoop, calls=%fused_computation.2 | loop fusion | flops 2867200 | bytes 2874368 | tf_op jit(solution)/shard_map/convert_element_type | solution.py:814
  6.6 0.1 fusion.1.turn
  6.7 64.8 %gather_weights.1 = (bf16[3,4,4,4,8,4352]{5,4,3,2,1,0:T(8,128)(2,1)}, bf16[1024,1664]{1,0:T(8,128)(2,1)}) custom-call(s32[24]{0:T(128)S(1)} %reshape.135.scalars, bf16[3,8,4352]{2,1,0:T(8,128)(2,1)S(1)} %pad_maximum_fusion.shard, bf16[8,128,800]{2,1,0:T(8,128)(2,1)S(1)} %bitcast.36, f32[8,800]{1,0:T(8,128)S(1)} %pad.69.gain, ...), custom_call_target="tpu_custom_call" | custom-call | tf_op jit(solution)/shard_map/gather_weights/pallas_call | solution.py:304
  71.6 1.2 slice_bitcast_fusion
  72.9 0.7 copy.39
  73.6 0.9 reshape.140
  74.7 0.1 concatenate.18
  74.9 0.3 copy.41
  75.2 0.1 pad.103.xproj
  75.4 50.7 %project.1 = (bf16[1024,1792]{1,0:T(8,128)(2,1)}, bf16[1024,1792]{1,0:T(8,128)(2,1)}, bf16[1024,768]{1,0:T(8,128)(2,1)}, f32[1024,256]{1,0:T(8,128)S(1)}, bf16[3...) custom-call(bf16[1024,1664]{1,0:T(8,128)(2,1)} %get-tuple-element.13.normed, ...), custom_call_target="tpu_custom_call" | custom-call | tf_op jit(solution)/shard_map/project/pallas_call | solution.py:450
  126.1 1.0 copy-done.2
  127.1 1.3 slice_bitcast_fusion.1
  128.4 0.3 copy.43
  128.8 0.3 reshape.144
  129.1 0.9 pad.83.odd
  130.0 0.1 dynamic_slice.10
  130.1 0.1 dynamic_slice.11
  130.2 0.6 select_maximum_fusion.2.gains
  130.8 1.0 pad.104.dt_weight
  131.7 1.0 pad.77.start
  132.8 0.6 pad.82.params
  133.4 0.6 pad.78.decay
  134.1 94.2 %attend_scan_deliver.1 = bf16[8,128,800]{2,1,0:T(8,128)(2,1)} custom-call(s32[24]{0:T(128)} %copy-done.5, bf16[1024,768]{1,0:T(8,128)(2,1)} %get-tuple-element.15.qkv, bf16[8,256,256]{2,1,0:T(8,128)(2,1)} %cache.1, f32[1024,256]{1,0:T(8,128)} %copy-done.2, bf16[1024,256]{1,0:T(8,128)(2,1)} %copy-done.3, bf16[1024,1792]{1,0:T(8,128)(2,1)} %get-tuple-element.18.conv, ...), custom_call_target="tpu_custom_call" | custom-call | tf_op jit(solution)/shard_map/attend_scan_deliver/pallas_call | solution.py:743
  228.3 2.9 %copy.54 = bf16[8,16,8,800]{3,2,1,0:T(8,128)(2,1)} copy(bf16[8,16,8,800]{3,2,1,0:T(8,128)(2,1)} %bitcast.40) | data formatting | bytes 3276800
  (80 shorter events, 0.7 us)
Async XLA Ops:
  0.0 1.1 copy-start
  0.0 4.0 %copy-start.18 = (s32[2,896]{1,0:T(2,128)S(1)}, s32[2,896]{1,0:T(2,128)}, u32[]{:S(2)}) copy-start(s32[2,896]{1,0:T(2,128)} %constant.86.clone) | copy-start | bytes 21508
  0.0 3.7 %copy-start.11 = (bf16[25,512]{1,0:T(8,128)(2,1)S(1)}, bf16[25,512]{1,0:T(8,128)(2,1)}, u32[]{:S(2)}) copy-start(bf16[25,512]{1,0:T(8,128)(2,1)} %param.31) | copy-start | bytes 76804
  0.0 3.7 %copy-start.14 = (bf16[25,256]{1,0:T(8,128)(2,1)S(1)}, bf16[25,256]{1,0:T(8,128)(2,1)}, u32[]{:S(2)}) copy-start(bf16[25,256]{1,0:T(8,128)(2,1)} %param.32) | copy-start | bytes 38404
  1.9 4.8 %copy-start.19 = (f32[800]{0:T(1024)S(1)}, f32[800]{0:T(1024)}, u32[]{:S(2)}) copy-start(f32[800]{0:T(1024)} %param.30) | copy-start | bytes 9604
  1.9 4.8 %copy-start.1 = (bf16[8,16,8,800]{3,2,1,0:T(8,128)(2,1)S(1)}, bf16[8,16,8,800]{3,2,1,0:T(8,128)(2,1)}, u32[]{:S(2)}) copy-start(bf16[8,16,8,800]{3,2,1,0:T(8,128)(2,1)} %param.23) | copy-start | bytes 4915204
  2.2 69.4 %copy-start.5 = (s32[24]{0:T(128)}, s32[24]{0:T(128)S(1)}, u32[]{:S(2)}) copy-start(s32[24]{0:T(128)S(1)} %reshape.135.scalars) | copy-start | bytes 292
  6.7 66.9 %copy-start.4 = (bf16[128,128]{1,0:T(8,128)(2,1)}, bf16[128,128]{1,0:T(8,128)(2,1)S(1)}, u32[]{:S(2)}) copy-start(bf16[128,128]{1,0:T(8,128)(2,1)S(1)} %fusion.1.turn) | copy-start | bytes 98308
  71.6 3.1 %copy-start.9 = (bf16[1600,25]{0,1:T(8,128)(2,1)S(1)}, bf16[1600,25]{0,1:T(8,128)(2,1)}, u32[]{:S(2)}) copy-start(bf16[1600,25]{0,1:T(8,128)(2,1)} %param.42) | copy-start | bytes 240004
  71.6 3.1 %copy-start.12 = (bf16[512,25]{0,1:T(8,128)(2,1)S(1)}, bf16[512,25]{0,1:T(8,128)(2,1)}, u32[]{:S(2)}) copy-start(bf16[512,25]{0,1:T(8,128)(2,1)} %param.41) | copy-start | bytes 76804
  72.9 2.0 copy-start.7
  73.6 1.8 copy-start.15
  74.5 0.8 copy-start.13
  126.1 1.0 copy-start.2
  127.1 7.0 %copy-start.3 = (bf16[1024,256]{1,0:T(8,128)(2,1)}, bf16[1024,256]{1,0:T(8,128)(2,1)S(1)}, u32[]{:S(2)}) copy-start(bf16[1024,256]{1,0:T(8,128)(2,1)S(1)} %get-tuple-element.17.mix_other) | copy-start | bytes 1572868
  127.1 2.9 %copy-start.20 = (f32[1600]{0:T(1024)S(1)}, f32[1600]{0:T(1024)}, u32[]{:S(2)}) copy-start(f32[1600]{0:T(1024)} %param.43) | copy-start | bytes 19204
  127.1 3.0 %copy-start.21 = (f32[1600]{0:T(1024)S(1)}, f32[1600]{0:T(1024)}, u32[]{:S(2)}) copy-start(f32[1600]{0:T(1024)} %param.44) | copy-start | bytes 19204
  127.1 3.7 %copy-start.8 = (bf16[100,1600]{1,0:T(8,128)(2,1)S(1)}, bf16[100,1600]{1,0:T(8,128)(2,1)}, u32[]{:S(2)}) copy-start(bf16[100,1600]{1,0:T(8,128)(2,1)} %param.37) | copy-start | bytes 960004
  127.1 4.7 %copy-start.6 = (f32[8,16,1600]{2,1,0:T(8,128)S(1)}, f32[8,16,1600]{2,1,0:T(8,128)}, u32[]{:S(2)}) copy-start(f32[8,16,1600]{2,1,0:T(8,128)} %param.25) | copy-start | bytes 2457604
  127.1 5.6 %copy-start.16 = (f32[1600]{0:T(1024)S(1)}, f32[1600]{0:T(1024)}, u32[]{:S(2)}) copy-start(f32[1600]{0:T(1024)} %param.38) | copy-start | bytes 19204
  127.1 5.6 %copy-start.17 = (f32[1600]{0:T(1024)S(1)}, f32[1600]{0:T(1024)}, u32[]{:S(2)}) copy-start(f32[1600]{0:T(1024)} %param.40) | copy-start | bytes 19204
  127.1 6.3 %copy-start.10 = (f32[16,1600]{1,0:T(8,128)S(1)}, f32[16,1600]{1,0:T(8,128)}, u32[]{:S(2)}) copy-start(f32[16,1600]{1,0:T(8,128)} %param.39) | copy-start | bytes 307204

commit v3 on v2

--- a/solution.py
+++ b/solution.py
@@ -16,7 +16,10 @@
 LOG2E = 1.4426950408889634
 
 SHARD = 25
-CONV_AT, GATE_AT, QKV_AT, IN_ODD, IN_COLS = 0, 1664, 3328, 4096, 4352
+GATE_TILES = 5
+FIRST_GATE, FIRST_ODD, FIRST_COLS = 1664, 1664 + 256 * GATE_TILES, 1792 + 256 * GATE_TILES
+SECOND_QKV = 1664 - 256 * GATE_TILES
+SECOND_ODD, SECOND_COLS = SECOND_QKV + 768, SECOND_QKV + 896
 SSM_AT, ATT_AT, OUT_ODD, OUT_COLS = 0, 1664, 2176, 2304
 CH = 1600
 CHP = 1664
@@ -128,17 +131,17 @@
 
 
 class Gather:
-    def __init__(self, shard, gathered, send, recv, local_sem, pos, tc):
+    def __init__(self, shard, gathered, send, recv, local_sem, pos, tc, base=0):
         sems = (send, recv)
         self.kept = [
             pltpu.make_async_copy(
-                shard.at[rot], gathered.at[rot, pos["y"], pos["x"], pos["z"]], local_sem.at[rot]
+                shard.at[rot], gathered.at[rot, pos["y"], pos["x"], pos["z"]], local_sem.at[base // 24 + rot]
             )
             for rot in range(3)
         ]
         first, second, third = [], [], []
         for rot, (one, two, three) in enumerate(ORDERS):
-            at = rot * 24
+            at = base + rot * 24
             first.append(Ring(rot, one, (), None, 0, None, shard.at[rot], gathered, sems, at, pos, tc))
             second.append(Ring(rot, two, (one,), None, 0, one, None, gathered, sems, at + 4, pos, tc))
             third.append(
@@ -199,7 +202,7 @@
 GATHER_SEMS = 72
 
 
-def greet_torus(pos, tc):
+def greet_torus(pos, tc, others=0):
     barrier = pltpu.get_barrier_semaphore()
     for axis in ("x", "y", "z"):
         for step in (1, -1):
@@ -208,7 +211,7 @@
             )
     partner = device_at(pos, 1 - tc)
     pl.semaphore_signal(barrier, inc=1, device_id=partner, device_id_type=MESH)
-    pl.semaphore_wait(barrier, 7)
+    pl.semaphore_wait(barrier, 7 + others)
     return partner
 
 
@@ -220,35 +223,90 @@
     return [high, middle, low]
 
 
-def gather_kernel(
+def silu(value):
+    return 0.5 * value * (1.0 + jnp.tanh(0.5 * value))
+
+
+def odd_permutation():
+    row = lax.broadcasted_iota(jnp.int32, (512, 512), 0)
+    column = lax.broadcasted_iota(jnp.int32, (512, 512), 1)
+    return jnp.where(column == (row % 64) * 8 + row // 64, 1.0, 0.0).astype(BF16)
+
+
+def unpack_odd(weights, at, order, odd):
+    odd[...] = jnp.zeros_like(odd)
+    for rot in range(3):
+        block = weights[rot * 512 : rot * 512 + 512, at : at + 128]
+        rows = jnp.dot(order[...], block, preferred_element_type=F32).astype(BF16)
+        for r in range(8):
+            tile = (r * 3 + rot) * 128
+            odd[0:64, tile : tile + 128] = rows[64 * r : 64 * r + 64]
+
+
+def project_kernel(
     scalars,
-    shard,
+    first_shard,
+    second_shard,
     tokens,
     gain,
     pick,
     turn,
-    gathered,
-    normed,
+    history,
+    taps,
+    xproj,
+    first_gathered,
+    second_gathered,
+    conv_out,
+    gate_out,
+    qkv_out,
+    mix_out,
+    other_mix,
     other_tokens,
     other_gain,
     turned,
+    normed,
+    first_weights,
+    second_weights,
+    first_odd,
+    second_odd,
+    odd_order,
+    product,
+    sequence,
+    conv,
+    gate,
+    qkv,
+    mix,
+    mix_send,
     send,
     recv,
     local_sem,
 ):
     pos, tc = torus_position()
     partner = greet_torus(pos, tc)
-    gather = Gather(shard, gathered, send, recv, local_sem, pos, tc)
+    one = Gather(first_shard, first_gathered, send, recv, local_sem, pos, tc)
+    two = Gather(second_shard, second_gathered, send, recv, local_sem, pos, tc, GATHER_SEMS)
     swaps = [
         pltpu.make_async_remote_copy(
             src_ref=here,
             dst_ref=there,
-            send_sem=send.at[GATHER_SEMS + n],
-            recv_sem=recv.at[GATHER_SEMS + n],
+            send_sem=send.at[2 * GATHER_SEMS + n],
+            recv_sem=recv.at[2 * GATHER_SEMS + n],
             device_id=partner,
             device_id_type=MESH,
         )
-        for n, (here, there) in enumerate(((tokens, other_tokens), (gain, other_gain)))
+        for n, (here, there) in enumerate(
+            ((tokens, other_tokens), (gain, other_gain), (mix_send, other_mix))
+        )
+    ]
+    loads = [
+        pltpu.make_async_copy(source.reshape(1536, source.shape[-1]), target, local_sem.at[6 + n])
+        for n, (source, target) in enumerate(
+            ((first_gathered, first_weights), (second_gathered, second_weights))
+        )
+    ]
+    stores = [
+        pltpu.make_async_copy(source, target, local_sem.at[8 + n])
+        for n, (source, target) in enumerate(((conv, conv_out), (mix, mix_out), (gate, gate_out), (qkv, qkv_out)))
     ]
 
     def turn_rows(side, source):
@@ -279,217 +337,164 @@
         normed[rows, 1536:1664] = (scaled[0][:, 768:] + scaled[1][:, 768:]).astype(BF16)
         return carry
 
-    gather.stage(0)
-    for copy in swaps:
-        copy.start()
+    def multiply(weights, odd, at):
+        columns = pl.ds(pl.multiple_of(at, 128), 256)
+
+        def body(part, carry):
+            rows = pl.ds(pl.multiple_of(part * 512, 512), 512)
+            value = jnp.dot(normed[rows, 0:1536], weights[:, columns], preferred_element_type=F32)
+            value = value + jnp.dot(normed[rows, 1536:1664], odd[:, columns], preferred_element_type=F32)
+            product[rows, :] = value
+            return carry
+
+        lax.fori_loop(0, 2, body, 0)
+
+    def conv_tile(tile, carry):
+        at = pl.multiple_of(tile * 256, 256)
+        columns = pl.ds(at, 256)
+        multiply(first_weights, first_odd, at)
+
+        def convolve(group, carry):
+            rows = pl.ds(pl.multiple_of(group * 128, 128), 128)
+            for k in range(3):
+                sequence[16 * k : 16 * k + 16, :] = jnp.broadcast_to(
+                    history[scalars[group], k : k + 1, columns], (16, 256)
+                )
+            sequence[48:176, :] = product[rows, :]
+            total = jnp.broadcast_to(taps[4:5, columns], (128, 256))
+            for k in range(4):
+                total = total + taps[k : k + 1, columns] * sequence[16 * k : 16 * k + 128, :]
+            result = silu(total).astype(BF16)
+            conv[rows, columns] = result
+            mix[rows, :] += jnp.dot(result, xproj[columns, :], preferred_element_type=F32)
+            return carry
+
+        lax.fori_loop(0, 8, convolve, 0)
+        return carry
+
+    def gate_tile(weights, odd, start):
+        def tile(index, carry):
+            multiply(weights, odd, start + index * 256 - (0 if start else GATE_TILES * 256))
+
+            def body(group, carry):
+                rows = pl.ds(pl.multiple_of(group * 128, 128), 128)
+                columns = pl.ds(pl.multiple_of(index * 256, 256), 256)
+                gate[rows, columns] = silu(product[rows, :]).astype(BF16)
+                return carry
+
+            lax.fori_loop(0, 8, body, 0)
+            return carry
+
+        return tile
+
+    def qkv_tile(index, carry):
+        multiply(second_weights, second_odd, SECOND_QKV + index * 256)
+        columns = pl.ds(pl.multiple_of(index * 256, 256), 256)
+        qkv[:, columns] = product[...].astype(BF16)
+        return carry
+
+    one.stage(0)
+    swaps[0].start()
+    swaps[1].start()
+    odd_order[...] = odd_permutation()
+    mix[...] = jnp.zeros_like(mix)
     turn_rows(0, tokens)
-    gather.stage(1)
-    for copy in swaps:
-        copy.wait_recv()
-    gather.stage(2)
+    one.stage(1)
+    swaps[0].wait_recv()
+    swaps[1].wait_recv()
+    one.stage(2)
     turn_rows(1, other_tokens)
     lax.fori_loop(0, 1, prepare, 0)
-    gather.stage(3)
+    one.stage(3)
     lax.fori_loop(1, 3, prepare, 0)
-    gather.stage(4)
+    one.stage(4)
     lax.fori_loop(3, 4, prepare, 0)
-    for number in range(5, STAGES):
-        gather.stage(number)
-    for copy in swaps:
-        copy.wait_send()
-
-
-def gather_call(scalars, shard, tokens, gain, pick, turn):
+    one.stage(5)
+    two.stage(0)
+    one.stage(6)
+    two.stage(1)
+    two.stage(2)
+    one.stage(7)
+    loads[0].start()
+    two.stage(3)
+    loads[0].wait()
+    unpack_odd(first_weights, FIRST_ODD, odd_order, first_odd)
+    lax.fori_loop(0, 3, conv_tile, 0)
+    two.stage(4)
+    lax.fori_loop(3, 6, conv_tile, 0)
+    two.stage(5)
+    lax.fori_loop(6, 7, conv_tile, 0)
+    mix_send[...] = mix[...].astype(BF16)
+    swaps[2].start()
+    stores[0].start()
+    stores[1].start()
+    lax.fori_loop(0, 2, gate_tile(first_weights, first_odd, FIRST_GATE), 0)
+    two.stage(6)
+    lax.fori_loop(2, GATE_TILES, gate_tile(first_weights, first_odd, FIRST_GATE), 0)
+    two.stage(7)
+    loads[1].start()
+    loads[1].wait()
+    unpack_odd(second_weights, SECOND_ODD, odd_order, second_odd)
+    lax.fori_loop(GATE_TILES, 7, gate_tile(second_weights, second_odd, 0), 0)
+    stores[2].start()
+    lax.fori_loop(0, 3, qkv_tile, 0)
+    stores[3].start()
+    swaps[0].wait_send()
+    swaps[1].wait_send()
+    swaps[2].wait()
+    for store in stores:
+        store.wait()
+
+
+def project_call(scalars, first_shard, second_shard, tokens, gain, pick, turn, history, taps, xproj):
     vmem = pl.BlockSpec(memory_space=pltpu.VMEM)
     return pl.pallas_call(
-        gather_kernel,
-        name="gather_weights",
+        project_kernel,
+        name="gather_project",
         out_shape=(
-            jax.ShapeDtypeStruct((3, 4, 4, 4, 8, IN_COLS), BF16),
-            jax.ShapeDtypeStruct((1024, 1664), BF16),
+            jax.ShapeDtypeStruct((3, 4, 4, 4, 8, FIRST_COLS), BF16),
+            jax.ShapeDtypeStruct((3, 4, 4, 4, 8, SECOND_COLS), BF16),
+            jax.ShapeDtypeStruct((1024, CHT), BF16),
+            jax.ShapeDtypeStruct((1024, CHT), BF16),
+            jax.ShapeDtypeStruct((1024, 768), BF16),
+            jax.ShapeDtypeStruct((1024, 256), F32),
+            jax.ShapeDtypeStruct((1024, 256), BF16),
         ),
-        in_specs=[pl.BlockSpec(memory_space=pltpu.SMEM), vmem, vmem, vmem, vmem, vmem],
-        out_specs=(ANY, vmem),
+        in_specs=[pl.BlockSpec(memory_space=pltpu.SMEM)] + [vmem] * 9,
+        out_specs=(ANY,) * 7,
         scratch_shapes=[
             pltpu.VMEM((8, 128, HALF), BF16),
             pltpu.VMEM((8, HALF), F32),
             pltpu.VMEM((2, 1024, HALF), BF16),
-            pltpu.SemaphoreType.DMA((GATHER_SEMS + 2,)),
-            pltpu.SemaphoreType.DMA((GATHER_SEMS + 2,)),
-            pltpu.SemaphoreType.DMA((3,)),
+            pltpu.VMEM((1024, 1664), BF16),
+            pltpu.VMEM((1536, FIRST_COLS), BF16),
+            pltpu.VMEM((1536, SECOND_COLS), BF16),
+            pltpu.VMEM((128, 3072), BF16),
+            pltpu.VMEM((128, 3072), BF16),
+            pltpu.VMEM((512, 512), BF16),
+            pltpu.VMEM((1024, 256), F32),
+            pltpu.VMEM((176, 256), F32),
+            pltpu.VMEM((1024, CHT), BF16),
+            pltpu.VMEM((1024, CHT), BF16),
+            pltpu.VMEM((1024, 768), BF16),
+            pltpu.VMEM((1024, 256), F32),
+            pltpu.VMEM((1024, 256), BF16),
+            pltpu.SemaphoreType.DMA((2 * GATHER_SEMS + 3,)),
+            pltpu.SemaphoreType.DMA((2 * GATHER_SEMS + 3,)),
+            pltpu.SemaphoreType.DMA((12,)),
         ],
         compiler_params=pltpu.CompilerParams(
-            collective_id=0, has_side_effects=True, vmem_limit_bytes=50 << 20
+            collective_id=0, has_side_effects=True, vmem_limit_bytes=60 << 20
         ),
-    )(scalars, shard, tokens, gain, pick, turn)
-
-
-def silu(value):
-    return 0.5 * value * (1.0 + jnp.tanh(0.5 * value))
-
-
-def project_kernel(
-    normed,
-    left,
-    right,
-    odd_left,
-    odd_right,
-    history,
-    taps,
-    xproj,
-    shard,
-    conv_out,
-    gate_out,
-    qkv_out,
-    mix_out,
-    gathered,
-    other_mix,
-    product,
-    sequence,
-    mix_send,
-    send,
-    recv,
-    local_sem,
-):
-    step = pl.program_id(0)
-    pos, tc = torus_position()
-    gather = Gather(shard, gathered, send, recv, local_sem, pos, tc)
-    swap = pltpu.make_async_remote_copy(
-        src_ref=mix_send,
-        dst_ref=other_mix,
-        send_sem=send.at[GATHER_SEMS],
-        recv_sem=recv.at[GATHER_SEMS],
-        device_id=device_at(pos, 1 - tc),
-        device_id_type=MESH,
-    )
-
-    @pl.when(step == 0)
-    def _():
-        greet_torus(pos, tc)
-        gather.stage(0)
-
-    for at, number in ((1, 1), (2, 2), (4, 3), (6, 4), (8, 5), (11, 6)):
-
-        @pl.when(step == at)
-        def _(number=number):
-            gather.stage(number)
-
-    @pl.when(step == 0)
-    def _():
-        mix_out[...] = jnp.zeros_like(mix_out)
-
-    block = jnp.concatenate([left[...], right[...]], axis=1)
-    odd = jnp.concatenate([odd_left[...], odd_right[...]], axis=1)
-
-    def multiply(part, carry):
-        rows = pl.ds(pl.multiple_of(part * 512, 512), 512)
-        value = jnp.dot(normed[rows, 0:1536], block, preferred_element_type=F32)
-        value = value + jnp.dot(normed[rows, 1536:1664], odd, preferred_element_type=F32)
-        product[rows, :] = value
-        return carry
-
-    lax.fori_loop(0, 2, multiply, 0)
-
-    @pl.when(step < 7)
-    def _():
-        def convolve(group, carry):
-            rows = pl.ds(pl.multiple_of(group * 128, 128), 128)
-            for k in range(3):
-                sequence[16 * k : 16 * k + 16, :] = jnp.broadcast_to(history[group, k : k + 1, :], (16, 256))
-            sequence[48:176, :] = product[rows, :]
-            total = jnp.broadcast_to(taps[4:5, :], (128, 256))
-            for k in range(4):
-                total = total + taps[k : k + 1, :] * sequence[16 * k : 16 * k + 128, :]
-            result = silu(total).astype(BF16)
-            conv_out[rows, :] = result
-            mix_out[rows, :] += jnp.dot(result, xproj[...], preferred_element_type=F32)
-            return carry
-
-        lax.fori_loop(0, 8, convolve, 0)
-
-    @pl.when((step >= 7) & (step < 14))
-    def _():
-        def gating(group, carry):
-            rows = pl.ds(pl.multiple_of(group * 128, 128), 128)
-            gate_out[rows, :] = silu(product[rows, :]).astype(BF16)
-            return carry
-
-        lax.fori_loop(0, 8, gating, 0)
-
-    @pl.when(step == 7)
-    def _():
-        mix_send[...] = mix_out[...].astype(BF16)
-        swap.start()
-
-    @pl.when(step >= 14)
-    def _():
-        def keep(group, carry):
-            rows = pl.ds(pl.multiple_of(group * 128, 128), 128)
-            qkv_out[rows, :] = product[rows, :].astype(BF16)
-            return carry
-
-        lax.fori_loop(0, 8, keep, 0)
-
-    @pl.when(step == 16)
-    def _():
-        gather.stage(7)
-        swap.wait()
-
-
-def column_block(step):
-    return jnp.where(
-        step < 7,
-        CONV_AT // 128 + 2 * step,
-        jnp.where(step < 14, GATE_AT // 128 + 2 * (step - 7), QKV_AT // 128 + 2 * (step - 14)),
-    )
-
-
-def project_call(normed, weights, odd, history, taps, xproj, shard):
-    whole = lambda shape: pl.BlockSpec(shape, lambda i: (0,) * len(shape), pipeline_mode=pl.Buffered(1))
-    conv_at = lambda i: jnp.minimum(i, 6)
-    return pl.pallas_call(
-        project_kernel,
-        name="project",
-        grid=(17,),
-        in_specs=[
-            whole((1024, 1664)),
-            pl.BlockSpec((1536, 128), lambda i: (0, column_block(i))),
-            pl.BlockSpec((1536, 128), lambda i: (0, column_block(i) + 1)),
-            pl.BlockSpec((128, 128), lambda i: (0, column_block(i))),
-            pl.BlockSpec((128, 128), lambda i: (0, column_block(i) + 1)),
-            pl.BlockSpec((8, 3, 256), lambda i: (0, 0, conv_at(i))),
-            pl.BlockSpec((8, 256), lambda i: (0, conv_at(i))),
-            pl.BlockSpec((256, 256), lambda i: (conv_at(i), 0)),
-            whole((3, 8, OUT_COLS)),
-        ],
-        out_specs=[
-            pl.BlockSpec((1024, 256), lambda i: (0, conv_at(i))),
-            pl.BlockSpec((1024, 256), lambda i: (0, jnp.clip(i - 7, 0, 6))),
-            pl.BlockSpec((1024, 256), lambda i: (0, jnp.clip(i - 14, 0, 2))),
-            pl.BlockSpec((1024, 256), lambda i: (0, 0)),
-            ANY,
-            ANY,
-        ],
-        scratch_shapes=[
-            pltpu.VMEM((1024, 256), F32),
-            pltpu.VMEM((176, 256), F32),
-            pltpu.VMEM((1024, 256), BF16),
-            pltpu.SemaphoreType.DMA((GATHER_SEMS + 1,)),
-            pltpu.SemaphoreType.DMA((GATHER_SEMS + 1,)),
-            pltpu.SemaphoreType.DMA((3,)),
-        ],
-        out_shape=[
-            jax.ShapeDtypeStruct((1024, CHT), BF16),
-            jax.ShapeDtypeStruct((1024, CHT), BF16),
-            jax.ShapeDtypeStruct((1024, 768), BF16),
-            jax.ShapeDtypeStruct((1024, 256), F32),
-            jax.ShapeDtypeStruct((3, 4, 4, 4, 8, OUT_COLS), BF16),
-            jax.ShapeDtypeStruct((1024, 256), BF16),
-        ],
-        compiler_params=pltpu.CompilerParams(
-            collective_id=1, has_side_effects=True, vmem_limit_bytes=50 << 20
-        ),
-    )(normed, weights, weights, odd, odd, history, taps, xproj, shard)
+    )(scalars, first_shard, second_shard, tokens, gain, pick, turn, history, taps, xproj)
+
+
+def split_gain(gain):
+    high = gain.astype(BF16)
+    rest = gain - high.astype(F32)
+    middle = rest.astype(BF16)
+    low = (rest - middle.astype(F32)).astype(BF16)
+    return [high, middle, low]
 
 
 def final_kernel(
@@ -504,13 +509,16 @@
     decay,
     dt_weight,
     params,
-    weights,
-    odd,
+    shard,
     tokens,
     gains,
     unpick,
     turn,
     out,
+    gathered,
+    weights,
+    odd,
+    odd_order,
     rate,
     spread,
     mixes,
@@ -531,13 +539,17 @@
     step = pl.program_id(0)
     rep, tr, tc = lax.axis_index("rep"), lax.axis_index("tr"), lax.axis_index("tc")
     partner = (rep, tr, 1 - tc)
+    pos, _ = torus_position()
+    gather = Gather(shard, gathered, send, recv, local_sem, pos, tc)
+    load = pltpu.make_async_copy(gathered.reshape(1536, OUT_COLS), weights, local_sem.at[3])
+    base = GATHER_SEMS
 
     def part_copy(pair):
         return pltpu.make_async_remote_copy(
             src_ref=parts.at[pair, 1],
             dst_ref=theirs.at[pair],
-            send_sem=send.at[pair],
-            recv_sem=recv.at[pair],
+            send_sem=send.at[base + pair],
+            recv_sem=recv.at[base + pair],
             device_id=partner,
             device_id_type=MESH,
         )
@@ -546,8 +558,8 @@
         return pltpu.make_async_remote_copy(
             src_ref=squares.at[pair],
             dst_ref=other_squares.at[pair],
-            send_sem=send.at[4 + pair],
-            recv_sem=recv.at[4 + pair],
+            send_sem=send.at[base + 4 + pair],
+            recv_sem=recv.at[base + 4 + pair],
             device_id=partner,
             device_id_type=MESH,
         )
@@ -556,8 +568,8 @@
         return pltpu.make_async_remote_copy(
             src_ref=staged.at[group],
             dst_ref=out.at[rep],
-            send_sem=send.at[8 + group],
-            recv_sem=recv.at[8 + group],
+            send_sem=send.at[base + 8 + group],
+            recv_sem=recv.at[base + 8 + group],
             device_id=((rep + 7 - group) % 8, tr, tc),
             device_id_type=MESH,
         )
@@ -565,10 +577,11 @@
     @pl.when(step == 0)
     def _():
         barrier = pltpu.get_barrier_semaphore()
-        pl.semaphore_signal(barrier, inc=1, device_id=partner, device_id_type=MESH)
         for k in range(1, 8):
             pl.semaphore_signal(barrier, inc=1, device_id=((rep + k) % 8, tr, tc), device_id_type=MESH)
-        pl.semaphore_wait(barrier, 8)
+        greet_torus(pos, tc, 7)
+        gather.stage(0)
+        odd_order[...] = odd_permutation()
         value = -jnp.exp(decay[...]) * LOG2E
         for n in range(16):
             rate[n] = jnp.broadcast_to(value[n : n + 1, :], (8, CHP))
@@ -616,12 +629,49 @@
             result = tokens[scalars[group]].astype(F32) + branch
             staged[group] = jnp.where(row < 8 * scalars[16 + group], result, 0.0).astype(BF16)
 
-    @pl.when((step % 2 == 0) & (step >= 2))
+    def products(pair):
+        source = stacked.at[pair % 2]
+        spans = ((ATT_AT, ATT_AT + 512), (SSM_AT, SSM_AT + CHP))
+
+        def body(rot, carry):
+            rows = pl.ds(pl.multiple_of(rot * 512, 512), 512)
+            place = pl.ds(pl.multiple_of(rot * 256, 256), 256)
+            for branch, (low_at, high_at) in enumerate(spans):
+                value = jnp.dot(
+                    weights[rows, low_at:high_at], source[low_at:high_at, :], preferred_element_type=F32
+                ).astype(BF16)
+                for half in range(2):
+                    parts[pair, (half + tc) % 2, branch, place, :] = value[256 * half : 256 * half + 256]
+            return carry
+
+        lax.fori_loop(0, 3, body, 0)
+        for branch, (low_at, high_at) in enumerate(spans):
+            value = jnp.dot(
+                odd[0:64, low_at:high_at], source[low_at:high_at, :], preferred_element_type=F32
+            ).astype(BF16)
+            for half in range(2):
+                parts[pair, (half + tc) % 2, branch, 768:800, :] = value[32 * half : 32 * half + 32]
+        part_copy(pair).start()
+
+    @pl.when(step == 4)
     def _():
-        sums(step // 2 - 1)
+        load.wait()
+        unpack_odd(weights, OUT_ODD, odd_order, odd)
+        products(0)
+
+    @pl.when(step == 5)
+    def _():
+        finish(step - 5)
+        result_copy(0).start()
+        result_copy(1).start()
+
+    @pl.when((step == 5) | (step == 6))
+    def _():
+        sums(step - 4)
 
     home = scalars[step]
     length = scalars[8 + step]
+    here = (step // 2) % 2
     column_at = pl.ds(pl.multiple_of((step % 2) * 128, 128), 128)
     row = lax.broadcasted_iota(jnp.int32, (128, 384), 0)
     column = lax.broadcasted_iota(jnp.int32, (128, 384), 1)
@@ -650,7 +700,7 @@
         for pair in range(2):
             at = ATT_AT + kv * 256 + pair * 128
             heads = jnp.where(low, pltpu.roll(weighted[2 * pair], 64, 1), weighted[2 * pair + 1])
-            stacked[at : at + 128, column_at] = heads.T.astype(BF16)
+            stacked[here, at : at + 128, column_at] = heads.T.astype(BF16)
 
     projected = mix_own[...] + mix_other[...].astype(F32)
     coarse = projected.astype(BF16)
@@ -683,48 +733,43 @@
             scan_out[rows, :] = total.reshape(16, 128)
         value = conv[:, lanes].astype(F32)
         gated = (scan_out[...] + params[1:2, lanes] * value) * gate[:, lanes].astype(F32)
-        stacked[pl.ds(at, 128), column_at] = gated.T.astype(BF16)
+        stacked[here, pl.ds(at, 128), column_at] = gated.T.astype(BF16)
         return carry
 
     lax.fori_loop(0, CHP // 128, chunk, 0)
 
-    @pl.when((step % 2 == 0) & (step >= 2))
+    for at, numbers in ((0, (1, 2)), (1, (3, 4)), (2, (5, 6)), (3, (7,))):
+
+        @pl.when(step == at)
+        def _(numbers=numbers):
+            for number in numbers:
+                gather.stage(number)
+
+    @pl.when(step == 3)
     def _():
-        pair = step // 2 - 1
-        finish(pair)
-        result_copy(2 * pair).start()
-        result_copy(2 * pair + 1).start()
-
-    @pl.when(step % 2 == 1)
+        load.start()
+
+    @pl.when((step == 4) | (step == 5) | (step == 7))
     def _():
-        pair = step // 2
-
-        def products(rot, carry):
-            rows = pl.ds(pl.multiple_of(rot * 512, 512), 512)
-            place = pl.ds(pl.multiple_of(rot * 256, 256), 256)
-            for branch, (low_at, high_at) in enumerate(((ATT_AT, ATT_AT + 512), (SSM_AT, SSM_AT + CHP))):
-                value = jnp.dot(
-                    weights[rows, low_at:high_at], stacked[low_at:high_at, :], preferred_element_type=F32
-                ).astype(BF16)
-                for half in range(2):
-                    parts[pair, (half + tc) % 2, branch, place, :] = value[256 * half : 256 * half + 256]
-            return carry
-
-        lax.fori_loop(0, 3, products, 0)
-        for branch, (low_at, high_at) in enumerate(((ATT_AT, ATT_AT + 512), (SSM_AT, SSM_AT + CHP))):
-            value = jnp.dot(
-                odd[0:64, low_at:high_at], stacked[low_at:high_at, :], preferred_element_type=F32
-            ).astype(BF16)
-            for half in range(2):
-                parts[pair, (half + tc) % 2, branch, 768:800, :] = value[32 * half : 32 * half + 32]
-        part_copy(pair).start()
+        products((step + 1) // 2 - 1)
+
+    @pl.when((step == 4) | (step == 7))
+    def _():
+        sums(step - 4)
+
+    @pl.when(step >= 5)
+    def _():
+        finish(step - 4)
+
+    @pl.when((step == 5) | (step == 6))
+    def _():
+        result_copy(2 * step - 8).start()
+        result_copy(2 * step - 7).start()
 
     @pl.when(step == 7)
     def _():
-        sums(3)
-        finish(3)
         result_copy(6).start()
-        stay = pltpu.make_async_copy(staged.at[7], out.at[rep], local_sem)
+        stay = pltpu.make_async_copy(staged.at[7], out.at[rep], local_sem.at[4])
         stay.start()
         for group in range(7):
             result_copy(group).wait()
@@ -735,8 +780,8 @@
 
 
 def final_call(
-    scalars, qkv, cache, mix_own, mix_other, conv, gate, start, decay, dt_weight, params, weights, odd,
-    tokens, gains, unpick, turn,
+    scalars, qkv, cache, mix_own, mix_other, conv, gate, start, decay, dt_weight, params, shard, tokens,
+    gains, unpick, turn,
 ):
     whole = lambda shape: pl.BlockSpec(shape, lambda i: (0,) * len(shape), pipeline_mode=pl.Buffered(1))
     rows = lambda width: pl.BlockSpec((128, width), lambda i: (i, 0))
@@ -756,40 +801,45 @@
             whole((16, CHP)),
             whole((256, CHP)),
             whole((8, CHP)),
-            whole((1536, 2176)),
-            whole((128, 2176)),
+            whole((3, 8, OUT_COLS)),
             whole((8, 128, HALF)),
             whole((8, HALF)),
             whole((1, HALF, HP)),
             whole((128, 128)),
         ],
-        out_specs=ANY,
-        out_shape=jax.ShapeDtypeStruct((8, 128, HALF), BF16),
+        out_specs=(ANY, ANY),
+        out_shape=(
+            jax.ShapeDtypeStruct((8, 128, HALF), BF16),
+            jax.ShapeDtypeStruct((3, 4, 4, 4, 8, OUT_COLS), BF16),
+        ),
         scratch_shapes=[
+            pltpu.VMEM((1536, OUT_COLS), BF16),
+            pltpu.VMEM((128, 3072), BF16),
+            pltpu.VMEM((512, 512), BF16),
             pltpu.VMEM((16, 8, CHP), F32),
             pltpu.VMEM((256, 4096), BF16),
             pltpu.VMEM((128, 4096), F32),
             pltpu.VMEM((128, CHP), F32),
             pltpu.VMEM((128, CHP), F32),
             pltpu.VMEM((128, 128), F32),
-            pltpu.VMEM((2176, 256), BF16),
+            pltpu.VMEM((2, 2176, 256), BF16),
             pltpu.VMEM((4, 2, 2, HALF, 256), BF16),
             pltpu.VMEM((4, 2, HALF, 256), BF16),
             pltpu.VMEM((4, 8, 256), F32),
             pltpu.VMEM((4, 8, 256), F32),
             pltpu.VMEM((2, HALF, 256), F32),
             pltpu.VMEM((8, 128, HALF), BF16),
-            pltpu.SemaphoreType.DMA((16,)),
-            pltpu.SemaphoreType.DMA((16,)),
-            pltpu.SemaphoreType.DMA,
+            pltpu.SemaphoreType.DMA((GATHER_SEMS + 16,)),
+            pltpu.SemaphoreType.DMA((GATHER_SEMS + 16,)),
+            pltpu.SemaphoreType.DMA((5,)),
         ],
         compiler_params=pltpu.CompilerParams(
             collective_id=2, has_side_effects=True, vmem_limit_bytes=58 << 20
         ),
     )(
-        scalars, qkv, cache, mix_own, mix_other, conv, gate, start, decay, dt_weight, params, weights, odd,
-        tokens, gains, unpick, turn,
-    )
+        scalars, qkv, cache, mix_own, mix_other, conv, gate, start, decay, dt_weight, params, shard, tokens,
+        gains, unpick, turn,
+    )[0]
 
 
 def pad_to(value, axis, size):
@@ -802,11 +852,6 @@
     rows = jnp.concatenate(pieces, axis=1)
     odd = pad_to(rows[24], 0, 24 * odd_columns).reshape(8, 3, odd_columns).swapaxes(0, 1)
     return jnp.concatenate([rows[:24].reshape(3, 8, rows.shape[1]), odd], axis=2)
-
-
-def unpack_odd(gathered, at):
-    odd = gathered[..., at:].transpose(1, 2, 3, 4, 0, 5).reshape(64, -1)
-    return pad_to(odd[:, :at], 0, 128)
 
 
 def picks():
@@ -852,26 +897,20 @@
     picked = jnp.sum(jnp.where(hits[None], values[:, None, :], 0), axis=2)
     scalars = picked.reshape(24)
 
-    order = picked[0]
     pick = picks()
     turn = turning()
     gap = jnp.zeros((SHARD, CHP - CH), BF16)
-    in_shard = pack_shard([w_inner[:, 0], gap, w_inner[:, 1], gap, w_query, w_keyval], 256)
+    split = GATE_TILES * 256
+    first_shard = pack_shard([w_inner[:, 0], gap, w_inner[:, 1, :split]], 128)
+    second_shard = pack_shard([w_inner[:, 1, split:], gap, w_query, w_keyval], 128)
     out_shard = pack_shard([w_ssm_out.T, gap, w_attn_out.T], 128)
     x_rows = tokens.reshape(8, 128, HALF)
     in_gains = pad_to(in_gain[None], 0, 8)
-    gathered, normed = gather_call(scalars, in_shard, x_rows, in_gains, pick, turn)
-    history = pad_to(jnp.take(conv_state, order, axis=0), 2, CHT)
+    history = pad_to(conv_state, 2, CHT)
     taps = pad_to(pad_to(jnp.concatenate([conv_weight, conv_bias[None]]), 0, 8), 1, CHT)
     xproj = pad_to(pad_to(w_xproj, 0, CHT), 1, 256)
-    conv, gate, qkv, mix, out_gathered, other_mix = project_call(
-        normed,
-        gathered.reshape(1536, IN_COLS),
-        unpack_odd(gathered, IN_ODD),
-        history,
-        taps,
-        xproj,
-        out_shard,
+    _, _, conv, gate, qkv, mix, other_mix = project_call(
+        scalars, first_shard, second_shard, x_rows, in_gains, pick, turn, history, taps, xproj
     )
     params = pad_to(pad_to(jnp.stack([dt_bias, skip_gain]), 0, 8), 1, CHP)
     gains = jnp.stack(
@@ -892,8 +931,7 @@
         pad_to(decay_log, 1, CHP),
         pad_to(pad_to(dt_weight, 0, 256), 1, CHP),
         params,
-        out_gathered.reshape(1536, OUT_COLS),
-        unpack_odd(out_gathered, OUT_ODD),
+        out_shard,
         x_rows,
         pad_to(gains, 0, 8),
         pick,

time: 233 us -> 231 us (level)
  other arithmetic: 4.58 us -> 7.72 us
    pallas_call x2 -> x1, Pallas kernels: 116 us -> 101 us  [project_call(): pl.pallas_call(project_kernel, name='gather_project', out_shape=(jax.Shap...]
    pallas_call x1, Pallas kernels: 94.2 us -> 107 us  [final_call(): pl.pallas_call(final_kernel, name='attend_scan_deliver', grid=(8,), in_sp...]
    transpose x4 -> x0, local copies, waits for them, and re-layouts: 3.53 us -> none  [unpack_odd(): odd = gathered[..., at:].transpose(1, 2, 3, 4, 0, 5).reshape(64, -1)]
    pad x12 -> x11, local copies, waits for them, and re-layouts: 4.36 us -> 6.31 us  [pad_to(): return jnp.pad(value, widths)]
where the time goes in v3:
time: 231 us
  Pallas kernels  208 us (90%)
  local copies, waits for them, and re-layouts  14.5 us (6%)
  other arithmetic  7.72 us (3%)
    pallas_call x1, Pallas kernels, final_call(): pl.pallas_call(final_kernel, name='attend_scan_deliver', grid=(8,), in_sp...  107 us
    pallas_call x1, Pallas kernels, project_call(): pl.pallas_call(project_kernel, name='gather_project', out_shape=(jax.Shap...  101 us
    pad x11, local copies, waits for them, and re-layouts, pad_to(): return jnp.pad(value, widths)  6.31 us

profile of v3, /device:TPU:0, one launch (start us, length us, event | category | flops | bytes accessed | tf_op | source)
XLA Modules:
  0.0 230.9 jit_solution(1200321310409600767)
XLA Ops:
  0.0 0.8 fusion.3
  0.8 0.1 broadcast_compare_fusion
  0.9 0.1 select_reduce_fusion
  1.1 0.6 reshape.95.scalars
  1.7 1.0 slice.41
  2.8 0.9 copy.52
  3.7 0.0 copy-start.3
  3.7 0.1 concatenate.21
  3.9 0.7 pad_maximum_fusion.first_shard
  4.6 0.8 slice.44
  5.5 0.9 concatenate.23
  6.4 0.6 pad_maximum_fusion.2.second_shard
  7.0 3.3 %fusion.pick.unpick = bf16[2,800,896]{2,1,0:T(8,128)(2,1)} fusion(s32[2,896]{1,0:T(2,128)} %constant.73.clone), kind=kLoop, calls=%fused_computation.1 | loop fusion | flops 2867200 | bytes 2874368 | tf_op jit(solution)/shard_map/convert_element_type | solution.py:859
  10.4 0.7 fusion.1.turn
  11.1 0.3 copy.41
  11.4 1.1 pad.99.xproj
  12.5 0.1 copy.40
  12.5 0.7 pad.67.history
  13.3 0.6 pad.69.taps
  14.0 0.6 pad.66.gain
  14.6 101.3 %gather_project.1 = (bf16[3,4,4,4,8,3072]{5,4,3,2,1,0:T(8,128)(2,1)}, bf16[3,4,4,4,8,1280]{5,4,3,2,1,0:T(8,128)(2,1)}, bf16[1024,1792]{1,0:T(8,128)(2,1)}, bf16[...) custom-call(s32[24]{0:T(128)} %reshape.95.scalars, ...), custom_call_target="tpu_custom_call" | custom-call | tf_op jit(solution)/shard_map/gather_project/pallas_call | solution.py:451
  115.9 0.1 dynamic_slice.10
  116.0 0.1 dynamic_slice.11
  116.1 0.6 select_maximum_fusion.2.gains
  116.7 0.1 concatenate.26
  116.9 0.7 pad_maximum_fusion.1.shard
  117.5 1.0 pad.100.dt_weight
  118.5 1.0 pad.72.start
  119.6 0.6 pad.77.params
  120.2 0.6 pad.73.decay
  120.8 107.2 %attend_scan_deliver.1 = (bf16[8,128,800]{2,1,0:T(8,128)(2,1)}, bf16[3,4,4,4,8,2304]{5,4,3,2,1,0:T(8,128)(2,1)}) custom-call(s32[24]{0:T(128)} %reshape.95.scalars, bf16[1024,768]{1,0:T(8,128)(2,1)} %get-tuple-element.11.qkv, bf16[8,256,256]{2,1,0:T(8,128)(2,1)} %cache.1, f32[1024,256]{1,0:T(8,128)} %get-tuple-element.12.mix_own, ...), custom_call_target="tpu_custom_call" | custom-call | tf_op jit(solution)/shard_map/attend_scan_deliver/pallas_call | solution.py:788
  228.0 2.9 %copy.59 = bf16[8,16,8,800]{3,2,1,0:T(8,128)(2,1)} copy(bf16[8,16,8,800]{3,2,1,0:T(8,128)(2,1)} %bitcast.36) | data formatting | bytes 3276800
  (59 shorter events, 0.4 us)
Async XLA Ops:
  0.0 11.1 %copy-start.1 = (bf16[1600,132]{0,1:T(8,128)(2,1)S(1)}, bf16[1600,132]{0,1:T(8,128)(2,1)}, u32[]{:S(2)}) copy-start(bf16[1600,132]{0,1:T(8,128)(2,1)} %param.36) | copy-start | bytes 1267204
  3.7 8.7 %copy-start.3 = (f32[8,3,1600]{2,0,1:T(8,128)S(1)}, f32[8,3,1600]{2,0,1:T(8,128)}, u32[]{:S(2)}) copy-start(f32[8,3,1600]{2,0,1:T(8,128)} %param.26) | copy-start | bytes 460804
  4.6 8.7 %copy-start.8 = (f32[1600]{0:T(1024)S(1)}, f32[1600]{0:T(1024)}, u32[]{:S(2)}) copy-start(f32[1600]{0:T(1024)} %param.35) | copy-start | bytes 19204
  4.6 8.7 %copy-start.7 = (f32[4,1600]{1,0:T(4,128)S(1)}, f32[4,1600]{1,0:T(4,128)}, u32[]{:S(2)}) copy-start(f32[4,1600]{1,0:T(4,128)} %param.34) | copy-start | bytes 76804
  5.5 8.5 %copy-start.11 = (f32[800]{0:T(1024)S(1)}, f32[800]{0:T(1024)}, u32[]{:S(2)}) copy-start(f32[800]{0:T(1024)} %param.30) | copy-start | bytes 9604
  12.4 103.4 %copy-start.12 = (f32[1600]{0:T(1024)S(1)}, f32[1600]{0:T(1024)}, u32[]{:S(2)}) copy-start(f32[1600]{0:T(1024)} %param.43) | copy-start | bytes 19204
  12.4 103.5 %copy-start.13 = (f32[1600]{0:T(1024)S(1)}, f32[1600]{0:T(1024)}, u32[]{:S(2)}) copy-start(f32[1600]{0:T(1024)} %param.44) | copy-start | bytes 19204
  12.4 104.2 %copy-start.4 = (bf16[1600,25]{0,1:T(8,128)(2,1)S(1)}, bf16[1600,25]{0,1:T(8,128)(2,1)}, u32[]{:S(2)}) copy-start(bf16[1600,25]{0,1:T(8,128)(2,1)} %param.42) | copy-start | bytes 240004
  12.4 104.2 %copy-start.6 = (bf16[512,25]{0,1:T(8,128)(2,1)S(1)}, bf16[512,25]{0,1:T(8,128)(2,1)}, u32[]{:S(2)}) copy-start(bf16[512,25]{0,1:T(8,128)(2,1)} %param.41) | copy-start | bytes 76804
  13.3 104.3 %copy-start.2 = (bf16[100,1600]{1,0:T(8,128)(2,1)S(1)}, bf16[100,1600]{1,0:T(8,128)(2,1)}, u32[]{:S(2)}) copy-start(bf16[100,1600]{1,0:T(8,128)(2,1)} %param.37) | copy-start | bytes 960004
  14.6 104.0 %copy-start = (f32[8,16,1600]{2,1,0:T(8,128)S(1)}, f32[8,16,1600]{2,1,0:T(8,128)}, u32[]{:S(2)}) copy-start(f32[8,16,1600]{2,1,0:T(8,128)} %param.25) | copy-start | bytes 2457604
  14.6 104.9 %copy-start.9 = (f32[1600]{0:T(1024)S(1)}, f32[1600]{0:T(1024)}, u32[]{:S(2)}) copy-start(f32[1600]{0:T(1024)} %param.38) | copy-start | bytes 19204
  14.6 104.9 %copy-start.10 = (f32[1600]{0:T(1024)S(1)}, f32[1600]{0:T(1024)}, u32[]{:S(2)}) copy-start(f32[1600]{0:T(1024)} %param.40) | copy-start | bytes 19204
  14.6 105.6 %copy-start.5 = (f32[16,1600]{1,0:T(8,128)S(1)}, f32[16,1600]{1,0:T(8,128)}, u32[]{:S(2)}) copy-start(f32[16,1600]{1,0:T(8,128)} %param.39) | copy-start | bytes 307204

commit v4 on v3

--- a/solution.py
+++ b/solution.py
@@ -235,12 +235,14 @@
 
 def unpack_odd(weights, at, order, odd):
     odd[...] = jnp.zeros_like(odd)
+    tiles = at // 128
     for rot in range(3):
         block = weights[rot * 512 : rot * 512 + 512, at : at + 128]
         rows = jnp.dot(order[...], block, preferred_element_type=F32).astype(BF16)
         for r in range(8):
             tile = (r * 3 + rot) * 128
-            odd[0:64, tile : tile + 128] = rows[64 * r : 64 * r + 64]
+            if r * 3 + rot < tiles:
+                odd[0:64, tile : tile + 128] = rows[64 * r : 64 * r + 64]
 
 
 def project_kernel(
@@ -267,11 +269,7 @@
     normed,
     first_weights,
     second_weights,
-    first_odd,
-    second_odd,
     odd_order,
-    product,
-    sequence,
     conv,
     gate,
     qkv,
@@ -299,7 +297,9 @@
         )
     ]
     loads = [
-        pltpu.make_async_copy(source.reshape(1536, source.shape[-1]), target, local_sem.at[6 + n])
+        pltpu.make_async_copy(
+            source.reshape(1536, source.shape[-1]), target.at[0:1536], local_sem.at[6 + n]
+        )
         for n, (source, target) in enumerate(
             ((first_gathered, first_weights), (second_gathered, second_weights))
         )
@@ -337,67 +337,57 @@
         normed[rows, 1536:1664] = (scaled[0][:, 768:] + scaled[1][:, 768:]).astype(BF16)
         return carry
 
-    def multiply(weights, odd, at):
+    def multiply(weights, at, part):
         columns = pl.ds(pl.multiple_of(at, 128), 256)
-
-        def body(part, carry):
-            rows = pl.ds(pl.multiple_of(part * 512, 512), 512)
-            value = jnp.dot(normed[rows, 0:1536], weights[:, columns], preferred_element_type=F32)
-            value = value + jnp.dot(normed[rows, 1536:1664], odd[:, columns], preferred_element_type=F32)
-            product[rows, :] = value
-            return carry
-
-        lax.fori_loop(0, 2, body, 0)
+        return jnp.dot(
+            normed[256 * part : 256 * part + 256, :], weights[:, columns], preferred_element_type=F32
+        )
 
     def conv_tile(tile, carry):
         at = pl.multiple_of(tile * 256, 256)
         columns = pl.ds(at, 256)
-        multiply(first_weights, first_odd, at)
-
-        def convolve(group, carry):
-            rows = pl.ds(pl.multiple_of(group * 128, 128), 128)
-            for k in range(3):
-                sequence[16 * k : 16 * k + 16, :] = jnp.broadcast_to(
-                    history[scalars[group], k : k + 1, columns], (16, 256)
+        for part in range(4):
+            value = multiply(first_weights, at, part)
+            for member in range(2):
+                group = 2 * part + member
+                past = history[scalars[group], :, columns]
+                sequence = jnp.concatenate(
+                    [jnp.broadcast_to(past[k : k + 1], (16, 256)) for k in range(3)]
+                    + [value[128 * member : 128 * member + 128]],
+                    axis=0,
                 )
-            sequence[48:176, :] = product[rows, :]
-            total = jnp.broadcast_to(taps[4:5, columns], (128, 256))
-            for k in range(4):
-                total = total + taps[k : k + 1, columns] * sequence[16 * k : 16 * k + 128, :]
-            result = silu(total).astype(BF16)
-            conv[rows, columns] = result
-            mix[rows, :] += jnp.dot(result, xproj[columns, :], preferred_element_type=F32)
+                total = taps[4:5, columns]
+                for k in range(4):
+                    total = total + taps[k : k + 1, columns] * sequence[16 * k : 16 * k + 128, :]
+                conv[128 * group : 128 * group + 128, columns] = silu(total).astype(BF16)
+        return carry
+
+    def mixing(part, carry):
+        rows = pl.ds(pl.multiple_of(part * 256, 256), 256)
+        mix[rows, :] = jnp.dot(conv[rows, :], xproj[...], preferred_element_type=F32)
+        return carry
+
+    def gate_tile(weights, start):
+        def tile(index, carry):
+            columns = pl.ds(pl.multiple_of(index * 256, 256), 256)
+            for part in range(4):
+                value = multiply(weights, start + index * 256, part)
+                gate[256 * part : 256 * part + 256, columns] = silu(value).astype(BF16)
             return carry
 
-        lax.fori_loop(0, 8, convolve, 0)
-        return carry
-
-    def gate_tile(weights, odd, start):
-        def tile(index, carry):
-            multiply(weights, odd, start + index * 256 - (0 if start else GATE_TILES * 256))
-
-            def body(group, carry):
-                rows = pl.ds(pl.multiple_of(group * 128, 128), 128)
-                columns = pl.ds(pl.multiple_of(index * 256, 256), 256)
-                gate[rows, columns] = silu(product[rows, :]).astype(BF16)
-                return carry
-
-            lax.fori_loop(0, 8, body, 0)
-            return carry
-
         return tile
 
     def qkv_tile(index, carry):
-        multiply(second_weights, second_odd, SECOND_QKV + index * 256)
         columns = pl.ds(pl.multiple_of(index * 256, 256), 256)
-        qkv[:, columns] = product[...].astype(BF16)
+        for part in range(4):
+            value = multiply(second_weights, SECOND_QKV + index * 256, part)
+            qkv[256 * part : 256 * part + 256, columns] = value.astype(BF16)
         return carry
 
     one.stage(0)
     swaps[0].start()
     swaps[1].start()
     odd_order[...] = odd_permutation()
-    mix[...] = jnp.zeros_like(mix)
     turn_rows(0, tokens)
     one.stage(1)
     swaps[0].wait_recv()
@@ -418,24 +408,25 @@
     loads[0].start()
     two.stage(3)
     loads[0].wait()
-    unpack_odd(first_weights, FIRST_ODD, odd_order, first_odd)
+    unpack_odd(first_weights, FIRST_ODD, odd_order, first_weights.at[1536:1664])
     lax.fori_loop(0, 3, conv_tile, 0)
     two.stage(4)
     lax.fori_loop(3, 6, conv_tile, 0)
     two.stage(5)
     lax.fori_loop(6, 7, conv_tile, 0)
+    lax.fori_loop(0, 4, mixing, 0)
     mix_send[...] = mix[...].astype(BF16)
     swaps[2].start()
     stores[0].start()
     stores[1].start()
-    lax.fori_loop(0, 2, gate_tile(first_weights, first_odd, FIRST_GATE), 0)
+    lax.fori_loop(0, 2, gate_tile(first_weights, FIRST_GATE), 0)
     two.stage(6)
-    lax.fori_loop(2, GATE_TILES, gate_tile(first_weights, first_odd, FIRST_GATE), 0)
+    lax.fori_loop(2, GATE_TILES, gate_tile(first_weights, FIRST_GATE), 0)
     two.stage(7)
     loads[1].start()
     loads[1].wait()
-    unpack_odd(second_weights, SECOND_ODD, odd_order, second_odd)
-    lax.fori_loop(GATE_TILES, 7, gate_tile(second_weights, second_odd, 0), 0)
+    unpack_odd(second_weights, SECOND_ODD, odd_order, second_weights.at[1536:1664])
+    lax.fori_loop(GATE_TILES, 7, gate_tile(second_weights, -256 * GATE_TILES), 0)
     stores[2].start()
     lax.fori_loop(0, 3, qkv_tile, 0)
     stores[3].start()
@@ -467,13 +458,9 @@
             pltpu.VMEM((8, HALF), F32),
             pltpu.VMEM((2, 1024, HALF), BF16),
             pltpu.VMEM((1024, 1664), BF16),
-            pltpu.VMEM((1536, FIRST_COLS), BF16),
-            pltpu.VMEM((1536, SECOND_COLS), BF16),
-            pltpu.VMEM((128, 3072), BF16),
-            pltpu.VMEM((128, 3072), BF16),
+            pltpu.VMEM((1664, FIRST_COLS), BF16),
+            pltpu.VMEM((1664, SECOND_COLS), BF16),
             pltpu.VMEM((512, 512), BF16),
-            pltpu.VMEM((1024, 256), F32),
-            pltpu.VMEM((176, 256), F32),
             pltpu.VMEM((1024, CHT), BF16),
             pltpu.VMEM((1024, CHT), BF16),
             pltpu.VMEM((1024, 768), BF16),
@@ -497,6 +484,9 @@
     return [high, middle, low]
 
 
+POLLS = ((0, 0, 1), (0, 1, 2), (1, 1, 3), (2, 0, 4), (2, 1, 5), (3, 0, 6), (3, 1, 7))
+
+
 def final_kernel(
     scalars,
     qkv,
@@ -505,9 +495,9 @@
     mix_other,
     conv,
     gate,
-    start,
+    start_in,
     decay,
-    dt_weight,
+    dt_in,
     params,
     shard,
     tokens,
@@ -516,6 +506,8 @@
     turn,
     out,
     gathered,
+    start,
+    dt_weight,
     weights,
     odd,
     odd_order,
@@ -582,13 +574,18 @@
         greet_torus(pos, tc, 7)
         gather.stage(0)
         odd_order[...] = odd_permutation()
+        start[...] = jnp.zeros_like(start)
+        start[:, :, 0:CH] = start_in[...]
+        dt_weight[...] = jnp.zeros_like(dt_weight)
+        dt_weight[0:100, 0:CH] = dt_in[...]
         value = -jnp.exp(decay[...]) * LOG2E
+        rate[...] = jnp.zeros_like(rate)
         for n in range(16):
-            rate[n] = jnp.broadcast_to(value[n : n + 1, :], (8, CHP))
+            rate[n, :, 0:CH] = jnp.broadcast_to(value[n : n + 1, :], (8, CH))
         row = lax.broadcasted_iota(jnp.int32, (256, 128), 0)
         for n in range(32):
             spread[:, 128 * n : 128 * n + 128] = jnp.where(
-                (row == 100 + n) | (row == 132 + n), 1.0, 0.0
+                row == 100 + n, 1.0, 0.0
             ).astype(BF16)
         squares[...] = jnp.zeros_like(squares)
         terms = [jnp.broadcast_to(gains[n : n + 1, :], (8, HALF)) for n in range(2)]
@@ -630,7 +627,7 @@
             staged[group] = jnp.where(row < 8 * scalars[16 + group], result, 0.0).astype(BF16)
 
     def products(pair):
-        source = stacked.at[pair % 2]
+        source = stacked.at[pair]
         spans = ((ATT_AT, ATT_AT + 512), (SSM_AT, SSM_AT + CHP))
 
         def body(rot, carry):
@@ -653,12 +650,6 @@
                 parts[pair, (half + tc) % 2, branch, 768:800, :] = value[32 * half : 32 * half + 32]
         part_copy(pair).start()
 
-    @pl.when(step == 4)
-    def _():
-        load.wait()
-        unpack_odd(weights, OUT_ODD, odd_order, odd)
-        products(0)
-
     @pl.when(step == 5)
     def _():
         finish(step - 5)
@@ -671,7 +662,7 @@
 
     home = scalars[step]
     length = scalars[8 + step]
-    here = (step // 2) % 2
+    here = step // 2
     column_at = pl.ds(pl.multiple_of((step % 2) * 128, 128), 128)
     row = lax.broadcasted_iota(jnp.int32, (128, 384), 0)
     column = lax.broadcasted_iota(jnp.int32, (128, 384), 1)
@@ -702,15 +693,10 @@
             heads = jnp.where(low, pltpu.roll(weighted[2 * pair], 64, 1), weighted[2 * pair + 1])
             stacked[here, at : at + 128, column_at] = heads.T.astype(BF16)
 
-    projected = mix_own[...] + mix_other[...].astype(F32)
-    coarse = projected.astype(BF16)
-    fine = (projected - coarse.astype(F32)).astype(BF16)
-    lane = lax.broadcasted_iota(jnp.int32, (128, 256), 1)
-    moved_fine = pltpu.roll(jnp.where((lane >= 100) & (lane < 132), fine.astype(F32), 0.0), 32, 1)
-    mix_terms = jnp.where(lane < 132, coarse.astype(F32), moved_fine).astype(BF16)
-    mixes[...] = jnp.dot(mix_terms, spread[...], preferred_element_type=F32)
-    raw = jnp.dot(coarse, dt_weight[...], preferred_element_type=F32) + params[0:1, :]
-    size = jnp.maximum(raw, 0.0) + jnp.log1p(jnp.exp(-jnp.abs(raw)))
+    projected = (mix_own[...] + mix_other[...].astype(F32)).astype(BF16)
+    mixes[...] = jnp.dot(projected, spread[...], preferred_element_type=F32)
+    raw = jnp.dot(projected, dt_weight[...], preferred_element_type=F32) + params[0:1, :]
+    size = jnp.maximum(raw, 0.0) + jnp.log(1.0 + jnp.exp(-jnp.abs(raw)))
     step_size[...] = size
     drive[...] = size * conv[:, 0:CHP].astype(F32)
 
@@ -736,18 +722,23 @@
         stacked[here, pl.ds(at, 128), column_at] = gated.T.astype(BF16)
         return carry
 
-    lax.fori_loop(0, CHP // 128, chunk, 0)
-
-    for at, numbers in ((0, (1, 2)), (1, (3, 4)), (2, (5, 6)), (3, (7,))):
-
-        @pl.when(step == at)
-        def _(numbers=numbers):
-            for number in numbers:
-                gather.stage(number)
-
-    @pl.when(step == 3)
+    for half, (low_chunk, high_chunk) in enumerate(((0, 6), (6, 13))):
+        lax.fori_loop(low_chunk, high_chunk, chunk, 0)
+        for at_step, at_half, number in POLLS:
+            if at_half == half:
+
+                @pl.when(step == at_step)
+                def _(number=number):
+                    gather.stage(number)
+                    if number == STAGES - 1:
+                        load.start()
+
+
+    @pl.when(step == 4)
     def _():
-        load.start()
+        load.wait()
+        unpack_odd(weights, OUT_ODD, odd_order, odd)
+        products(0)
 
     @pl.when((step == 4) | (step == 5) | (step == 7))
     def _():
@@ -797,9 +788,9 @@
             rows(256),
             rows(CHT),
             rows(CHT),
-            whole((8, 16, CHP)),
-            whole((16, CHP)),
-            whole((256, CHP)),
+            whole((8, 16, CH)),
+            whole((16, CH)),
+            whole((100, CH)),
             whole((8, CHP)),
             whole((3, 8, OUT_COLS)),
             whole((8, 128, HALF)),
@@ -813,6 +804,8 @@
             jax.ShapeDtypeStruct((3, 4, 4, 4, 8, OUT_COLS), BF16),
         ),
         scratch_shapes=[
+            pltpu.VMEM((8, 16, CHP), F32),
+            pltpu.VMEM((256, CHP), BF16),
             pltpu.VMEM((1536, OUT_COLS), BF16),
             pltpu.VMEM((128, 3072), BF16),
             pltpu.VMEM((512, 512), BF16),
@@ -822,7 +815,7 @@
             pltpu.VMEM((128, CHP), F32),
             pltpu.VMEM((128, CHP), F32),
             pltpu.VMEM((128, 128), F32),
-            pltpu.VMEM((2, 2176, 256), BF16),
+            pltpu.VMEM((4, 2176, 256), BF16),
             pltpu.VMEM((4, 2, 2, HALF, 256), BF16),
             pltpu.VMEM((4, 2, HALF, 256), BF16),
             pltpu.VMEM((4, 8, 256), F32),
@@ -927,9 +920,9 @@
         other_mix,
         conv,
         gate,
-        pad_to(ssm_state, 2, CHP),
-        pad_to(decay_log, 1, CHP),
-        pad_to(pad_to(dt_weight, 0, 256), 1, CHP),
+        ssm_state,
+        decay_log,
+        dt_weight,
         params,
         out_shard,
         x_rows,

time: 231 us -> 210 us (0.909)
  Pallas kernels: 208 us -> 190 us
  local copies, waits for them, and re-layouts: 14.5 us -> 11.8 us
    pallas_call x1, Pallas kernels: 101 us -> 90.1 us  [project_call(): pl.pallas_call(project_kernel, name='gather_project', out_shape=(jax.Shap...]
    pallas_call x1, Pallas kernels: 107 us -> 99.9 us  [final_call(): pl.pallas_call(final_kernel, name='attend_scan_deliver', grid=(8,), in_sp...]
    pad x11 -> x8, local copies, waits for them, and re-layouts: 6.31 us -> 3.67 us  [pad_to(): return jnp.pad(value, widths)]
where the time goes in v4:
time: 210 us
  Pallas kernels  190 us (90%)
  local copies, waits for them, and re-layouts  11.8 us (6%)
  other arithmetic  7.69 us (4%)
    pallas_call x1, Pallas kernels, final_call(): pl.pallas_call(final_kernel, name='attend_scan_deliver', grid=(8,), in_sp...  99.9 us
    pallas_call x1, Pallas kernels, project_call(): pl.pallas_call(project_kernel, name='gather_project', out_shape=(jax.Shap...  90.1 us
    unnamed x28, local copies, waits for them, and re-layouts  4.23 us

profile of v4, /device:TPU:0, one launch (start us, length us, event | category | flops | bytes accessed | tf_op | source)
XLA Modules:
  0.0 209.8 jit_solution(17825701721504799973)
XLA Ops:
  0.0 0.8 fusion.3
  0.8 0.1 broadcast_compare_fusion
  0.9 0.1 select_reduce_fusion
  1.1 0.6 reshape.95.scalars
  1.7 1.0 slice.41
  2.7 0.9 copy.52
  3.7 0.0 copy-start.1
  3.7 0.1 concatenate.21
  3.9 0.7 pad_maximum_fusion.first_shard
  4.6 0.8 slice.44
  5.4 0.0 copy-start.8
  5.4 0.9 concatenate.23
  6.4 0.6 pad_maximum_fusion.2.second_shard
  7.0 3.3 %fusion.pick.unpick = bf16[2,800,896]{2,1,0:T(8,128)(2,1)} fusion(s32[2,896]{1,0:T(2,128)} %constant.73.clone), kind=kLoop, calls=%fused_computation.1 | loop fusion | flops 2867200 | bytes 2874368 | tf_op jit(solution)/shard_map/convert_element_type | solution.py:852
  10.3 0.7 fusion.1.turn
  11.0 0.0 copy-done
  11.0 0.3 copy.41
  11.3 1.1 pad.79.xproj
  12.4 0.0 copy-start.3
  12.4 0.1 copy.40
  12.5 0.7 pad.51.history
  13.2 0.6 pad.53.taps
  13.9 0.6 pad.50.gain
  14.5 90.1 %gather_project.1 = (bf16[3,4,4,4,8,3072]{5,4,3,2,1,0:T(8,128)(2,1)}, bf16[3,4,4,4,8,1280]{5,4,3,2,1,0:T(8,128)(2,1)}, bf16[1024,1792]{1,0:T(8,128)(2,1)}, bf16[...) custom-call(s32[24]{0:T(128)} %reshape.95.scalars, ...), custom_call_target="tpu_custom_call" | custom-call | tf_op jit(solution)/shard_map/gather_project/pallas_call | solution.py:442
  104.6 0.1 dynamic_slice.10
  104.7 0.1 dynamic_slice.11
  104.8 0.6 select_maximum_fusion.2.gains
  105.4 0.1 concatenate.26
  105.6 0.7 pad_maximum_fusion.1.shard
  106.3 0.6 pad.57.params
  107.0 99.9 %attend_scan_deliver.1 = (bf16[8,128,800]{2,1,0:T(8,128)(2,1)}, bf16[3,4,4,4,8,2304]{5,4,3,2,1,0:T(8,128)(2,1)}) custom-call(s32[24]{0:T(128)} %reshape.95.scalars, bf16[1024,768]{1,0:T(8,128)(2,1)} %get-tuple-element.11.qkv, bf16[8,256,256]{2,1,0:T(8,128)(2,1)} %cache.1, f32[1024,256]{1,0:T(8,128)} %get-tuple-element.12.mix_own, ...), custom_call_target="tpu_custom_call" | custom-call | tf_op jit(solution)/shard_map/attend_scan_deliver/pallas_call | solution.py:779
  206.9 2.9 %copy.59 = bf16[8,16,8,800]{3,2,1,0:T(8,128)(2,1)} copy(bf16[8,16,8,800]{3,2,1,0:T(8,128)(2,1)} %bitcast.36) | data formatting | bytes 3276800
  (50 shorter events, 0.4 us)
Async XLA Ops:
  0.0 11.0 %copy-start = (bf16[1600,132]{0,1:T(8,128)(2,1)S(1)}, bf16[1600,132]{0,1:T(8,128)(2,1)}, u32[]{:S(2)}) copy-start(bf16[1600,132]{0,1:T(8,128)(2,1)} %param.36) | copy-start | bytes 1267204
  3.7 8.7 %copy-start.1 = (f32[8,3,1600]{2,0,1:T(8,128)S(1)}, f32[8,3,1600]{2,0,1:T(8,128)}, u32[]{:S(2)}) copy-start(f32[8,3,1600]{2,0,1:T(8,128)} %param.26) | copy-start | bytes 460804
  4.6 8.6 %copy-start.5 = (f32[1600]{0:T(1024)S(1)}, f32[1600]{0:T(1024)}, u32[]{:S(2)}) copy-start(f32[1600]{0:T(1024)} %param.35) | copy-start | bytes 19204
  4.6 8.6 %copy-start.4 = (f32[4,1600]{1,0:T(4,128)S(1)}, f32[4,1600]{1,0:T(4,128)}, u32[]{:S(2)}) copy-start(f32[4,1600]{1,0:T(4,128)} %param.34) | copy-start | bytes 76804
  5.4 8.4 %copy-start.8 = (f32[800]{0:T(1024)S(1)}, f32[800]{0:T(1024)}, u32[]{:S(2)}) copy-start(f32[800]{0:T(1024)} %param.30) | copy-start | bytes 9604
  12.4 92.3 %copy-start.9 = (f32[1600]{0:T(1024)S(1)}, f32[1600]{0:T(1024)}, u32[]{:S(2)}) copy-start(f32[1600]{0:T(1024)} %param.43) | copy-start | bytes 19204
  12.4 92.4 %copy-start.10 = (f32[1600]{0:T(1024)S(1)}, f32[1600]{0:T(1024)}, u32[]{:S(2)}) copy-start(f32[1600]{0:T(1024)} %param.44) | copy-start | bytes 19204
  12.4 93.1 %copy-start.2 = (bf16[1600,25]{0,1:T(8,128)(2,1)S(1)}, bf16[1600,25]{0,1:T(8,128)(2,1)}, u32[]{:S(2)}) copy-start(bf16[1600,25]{0,1:T(8,128)(2,1)} %param.42) | copy-start | bytes 240004
  12.4 93.1 %copy-start.3 = (bf16[512,25]{0,1:T(8,128)(2,1)S(1)}, bf16[512,25]{0,1:T(8,128)(2,1)}, u32[]{:S(2)}) copy-start(bf16[512,25]{0,1:T(8,128)(2,1)} %param.41) | copy-start | bytes 76804
  13.2 93.1 %copy-start.6 = (f32[1600]{0:T(1024)S(1)}, f32[1600]{0:T(1024)}, u32[]{:S(2)}) copy-start(f32[1600]{0:T(1024)} %param.38) | copy-start | bytes 19204
  13.2 93.1 %copy-start.7 = (f32[1600]{0:T(1024)S(1)}, f32[1600]{0:T(1024)}, u32[]{:S(2)}) copy-start(f32[1600]{0:T(1024)} %param.40) | copy-start | bytes 19204

commit v5 on v4

--- a/solution.py
+++ b/solution.py
@@ -227,6 +227,12 @@
     return 0.5 * value * (1.0 + jnp.tanh(0.5 * value))
 
 
+def row_turn():
+    row = lax.broadcasted_iota(jnp.int32, (128, 128), 0)
+    column = lax.broadcasted_iota(jnp.int32, (128, 128), 1)
+    return jnp.where(column == (row % 16) * 8 + row // 16, 1.0, 0.0).astype(BF16)
+
+
 def odd_permutation():
     row = lax.broadcasted_iota(jnp.int32, (512, 512), 0)
     column = lax.broadcasted_iota(jnp.int32, (512, 512), 1)
@@ -251,11 +257,10 @@
     second_shard,
     tokens,
     gain,
-    pick,
-    turn,
-    history,
+    table,
+    history_in,
     taps,
-    xproj,
+    xproj_in,
     first_gathered,
     second_gathered,
     conv_out,
@@ -263,6 +268,11 @@
     qkv_out,
     mix_out,
     other_mix,
+    unpick,
+    pick,
+    turn,
+    history,
+    xproj,
     other_tokens,
     other_gain,
     turned,
@@ -309,6 +319,8 @@
         for n, (source, target) in enumerate(((conv, conv_out), (mix, mix_out), (gate, gate_out), (qkv, qkv_out)))
     ]
 
+    keep_pick = pltpu.make_async_copy(pick.at[0], unpick, local_sem.at[12])
+
     def turn_rows(side, source):
         def body(group, carry):
             value = jnp.dot(turn[...], source[scalars[group]], preferred_element_type=F32)
@@ -387,9 +399,18 @@
     one.stage(0)
     swaps[0].start()
     swaps[1].start()
+    turn[...] = row_turn()
     odd_order[...] = odd_permutation()
     turn_rows(0, tokens)
     one.stage(1)
+    natural = lax.broadcasted_iota(jnp.int32, (HALF, HP), 0)
+    for half in range(2):
+        pick[half] = jnp.where(natural == table[8 * half : 8 * half + 1, :], 1.0, 0.0).astype(BF16)
+    keep_pick.start()
+    history[...] = jnp.zeros_like(history)
+    history[:, :, 0:CH] = history_in[...]
+    xproj[...] = jnp.zeros_like(xproj)
+    xproj[0:CH, 0:132] = xproj_in[...]
     swaps[0].wait_recv()
     swaps[1].wait_recv()
     one.stage(2)
@@ -435,9 +456,10 @@
     swaps[2].wait()
     for store in stores:
         store.wait()
-
-
-def project_call(scalars, first_shard, second_shard, tokens, gain, pick, turn, history, taps, xproj):
+    keep_pick.wait()
+
+
+def project_call(scalars, first_shard, second_shard, tokens, gain, table, history, taps, xproj):
     vmem = pl.BlockSpec(memory_space=pltpu.VMEM)
     return pl.pallas_call(
         project_kernel,
@@ -450,10 +472,15 @@
             jax.ShapeDtypeStruct((1024, 768), BF16),
             jax.ShapeDtypeStruct((1024, 256), F32),
             jax.ShapeDtypeStruct((1024, 256), BF16),
+            jax.ShapeDtypeStruct((HALF, HP), BF16),
         ),
-        in_specs=[pl.BlockSpec(memory_space=pltpu.SMEM)] + [vmem] * 9,
-        out_specs=(ANY,) * 7,
+        in_specs=[pl.BlockSpec(memory_space=pltpu.SMEM)] + [vmem] * 8,
+        out_specs=(ANY,) * 8,
         scratch_shapes=[
+            pltpu.VMEM((2, HALF, HP), BF16),
+            pltpu.VMEM((128, 128), BF16),
+            pltpu.VMEM((8, 3, CHT), F32),
+            pltpu.VMEM((CHT, 256), BF16),
             pltpu.VMEM((8, 128, HALF), BF16),
             pltpu.VMEM((8, HALF), F32),
             pltpu.VMEM((2, 1024, HALF), BF16),
@@ -468,12 +495,12 @@
             pltpu.VMEM((1024, 256), BF16),
             pltpu.SemaphoreType.DMA((2 * GATHER_SEMS + 3,)),
             pltpu.SemaphoreType.DMA((2 * GATHER_SEMS + 3,)),
-            pltpu.SemaphoreType.DMA((12,)),
+            pltpu.SemaphoreType.DMA((13,)),
         ],
         compiler_params=pltpu.CompilerParams(
             collective_id=0, has_side_effects=True, vmem_limit_bytes=60 << 20
         ),
-    )(scalars, first_shard, second_shard, tokens, gain, pick, turn, history, taps, xproj)
+    )(scalars, first_shard, second_shard, tokens, gain, table, history, taps, xproj)
 
 
 def split_gain(gain):
@@ -503,9 +530,9 @@
     tokens,
     gains,
     unpick,
-    turn,
     out,
     gathered,
+    turn,
     start,
     dt_weight,
     weights,
@@ -574,6 +601,7 @@
         greet_torus(pos, tc, 7)
         gather.stage(0)
         odd_order[...] = odd_permutation()
+        turn[...] = row_turn()
         start[...] = jnp.zeros_like(start)
         start[:, :, 0:CH] = start_in[...]
         dt_weight[...] = jnp.zeros_like(dt_weight)
@@ -591,7 +619,7 @@
         terms = [jnp.broadcast_to(gains[n : n + 1, :], (8, HALF)) for n in range(2)]
         terms = jnp.concatenate(split_gain(terms[0]) + split_gain(terms[1]), axis=0)
         placed = lax.dot_general(
-            unpick[0, :, 0:HALF], terms, (((0,), (1,)), ((), ())), preferred_element_type=F32
+            unpick[:, 0:HALF], terms, (((0,), (1,)), ((), ())), preferred_element_type=F32
         )
         for n in range(2):
             at = 24 * n
@@ -613,7 +641,7 @@
         total = squares[pair] + other_squares[pair]
         scale = lax.rsqrt(total / D + EPSILON)
         value = joined(pair, 0) * scale[0:1, :] * wide[0] + joined(pair, 1) * scale[1:2, :] * wide[1]
-        value = jnp.dot(unpick[0, :, 0:HALF], value.astype(BF16), preferred_element_type=F32).astype(BF16)
+        value = jnp.dot(unpick[:, 0:HALF], value.astype(BF16), preferred_element_type=F32).astype(BF16)
         row = lax.broadcasted_iota(jnp.int32, (128, HALF), 0)
         for member in range(2):
             group = 2 * pair + member
@@ -700,30 +728,49 @@
     step_size[...] = size
     drive[...] = size * conv[:, 0:CHP].astype(F32)
 
-    def chunk(index, carry):
-        at = pl.multiple_of(index * 128, 128)
-        lanes = pl.ds(at, 128)
-        first = start[home, :, lanes]
-        states = [jnp.broadcast_to(first[n : n + 1, :][None], (2, 8, 128)) for n in range(16)]
-        for t in range(8):
-            rows = slice(16 * t, 16 * t + 16)
-            size = step_size[rows, lanes].reshape(2, 8, 128)
-            push = drive[rows, lanes].reshape(2, 8, 128)
-            total = None
-            for n in range(16):
-                mix_in = mixes[rows, 128 * n : 128 * n + 128].reshape(2, 8, 128)
-                mix_out = mixes[rows, 2048 + 128 * n : 2176 + 128 * n].reshape(2, 8, 128)
-                states[n] = jnp.exp2(size * rate[n, :, lanes][None]) * states[n] + push * mix_in
-                term = states[n] * mix_out
-                total = term if total is None else total + term
-            scan_out[rows, :] = total.reshape(16, 128)
-        value = conv[:, lanes].astype(F32)
-        gated = (scan_out[...] + params[1:2, lanes] * value) * gate[:, lanes].astype(F32)
-        stacked[here, pl.ds(at, 128), column_at] = gated.T.astype(BF16)
-        return carry
-
-    for half, (low_chunk, high_chunk) in enumerate(((0, 6), (6, 13))):
-        lax.fori_loop(low_chunk, high_chunk, chunk, 0)
+    def chunk(width):
+        def body(index, carry):
+            at = pl.multiple_of(index * (128 * width), 128)
+            blocks = [pl.ds(pl.multiple_of(at + 128 * b, 128), 128) for b in range(width)]
+            for half in range(2):
+                names = range(8 * half, 8 * half + 8)
+                firsts = [start[home, :, lanes] for lanes in blocks]
+                states = [
+                    [jnp.broadcast_to(first[n : n + 1, :][None], (2, 8, 128)) for first in firsts]
+                    for n in names
+                ]
+                for t in range(8):
+                    rows = slice(16 * t, 16 * t + 16)
+                    size = [step_size[rows, lanes].reshape(2, 8, 128) for lanes in blocks]
+                    push = [drive[rows, lanes].reshape(2, 8, 128) for lanes in blocks]
+                    total = [None] * width
+                    for k, n in enumerate(names):
+                        mix_in = mixes[rows, 128 * n : 128 * n + 128].reshape(2, 8, 128)
+                        mix_out = mixes[rows, 2048 + 128 * n : 2176 + 128 * n].reshape(2, 8, 128)
+                        for b, lanes in enumerate(blocks):
+                            decayed = jnp.exp2(size[b] * rate[n, :, lanes][None]) * states[k][b]
+                            states[k][b] = decayed + push[b] * mix_in
+                            term = states[k][b] * mix_out
+                            total[b] = term if total[b] is None else total[b] + term
+                    for b in range(width):
+                        columns = slice(128 * b, 128 * b + 128)
+                        value = total[b].reshape(16, 128)
+                        if half:
+                            value = value + scan_out[rows, columns]
+                        scan_out[rows, columns] = value
+            for b, lanes in enumerate(blocks):
+                value = conv[:, lanes].astype(F32)
+                result = scan_out[:, 128 * b : 128 * b + 128] + params[1:2, lanes] * value
+                gated = result * gate[:, lanes].astype(F32)
+                stacked[here, lanes, column_at] = gated.T.astype(BF16)
+            return carry
+
+        return body
+
+    for half, (low_chunk, high_chunk) in enumerate(((0, 3), (3, 6))):
+        lax.fori_loop(low_chunk, high_chunk, chunk(2), 0)
+        if half:
+            lax.fori_loop(12, 13, chunk(1), 0)
         for at_step, at_half, number in POLLS:
             if at_half == half:
 
@@ -772,7 +819,7 @@
 
 def final_call(
     scalars, qkv, cache, mix_own, mix_other, conv, gate, start, decay, dt_weight, params, shard, tokens,
-    gains, unpick, turn,
+    gains, unpick,
 ):
     whole = lambda shape: pl.BlockSpec(shape, lambda i: (0,) * len(shape), pipeline_mode=pl.Buffered(1))
     rows = lambda width: pl.BlockSpec((128, width), lambda i: (i, 0))
@@ -795,8 +842,7 @@
             whole((3, 8, OUT_COLS)),
             whole((8, 128, HALF)),
             whole((8, HALF)),
-            whole((1, HALF, HP)),
-            whole((128, 128)),
+            whole((HALF, HP)),
         ],
         out_specs=(ANY, ANY),
         out_shape=(
@@ -804,6 +850,7 @@
             jax.ShapeDtypeStruct((3, 4, 4, 4, 8, OUT_COLS), BF16),
         ),
         scratch_shapes=[
+            pltpu.VMEM((128, 128), BF16),
             pltpu.VMEM((8, 16, CHP), F32),
             pltpu.VMEM((256, CHP), BF16),
             pltpu.VMEM((1536, OUT_COLS), BF16),
@@ -814,7 +861,7 @@
             pltpu.VMEM((128, 4096), F32),
             pltpu.VMEM((128, CHP), F32),
             pltpu.VMEM((128, CHP), F32),
-            pltpu.VMEM((128, 128), F32),
+            pltpu.VMEM((128, 256), F32),
             pltpu.VMEM((4, 2176, 256), BF16),
             pltpu.VMEM((4, 2, 2, HALF, 256), BF16),
             pltpu.VMEM((4, 2, HALF, 256), BF16),
@@ -831,7 +878,7 @@
         ),
     )(
         scalars, qkv, cache, mix_own, mix_other, conv, gate, start, decay, dt_weight, params, shard, tokens,
-        gains, unpick, turn,
+        gains, unpick,
     )[0]
 
 
@@ -845,16 +892,6 @@
     rows = jnp.concatenate(pieces, axis=1)
     odd = pad_to(rows[24], 0, 24 * odd_columns).reshape(8, 3, odd_columns).swapaxes(0, 1)
     return jnp.concatenate([rows[:24].reshape(3, 8, rows.shape[1]), odd], axis=2)
-
-
-def picks():
-    table = jnp.asarray(feature_table())
-    return (table[:, None, :] == jnp.arange(HALF, dtype=jnp.int32)[None, :, None]).astype(BF16)
-
-
-def turning():
-    row = jnp.arange(128, dtype=jnp.int32)
-    return (((row % 16) * 8 + row // 16)[:, None] == row[None, :]).astype(BF16)
 
 
 def local(
@@ -890,8 +927,7 @@
     picked = jnp.sum(jnp.where(hits[None], values[:, None, :], 0), axis=2)
     scalars = picked.reshape(24)
 
-    pick = picks()
-    turn = turning()
+    features = jnp.asarray(np.repeat(feature_table(), 8, axis=0))
     gap = jnp.zeros((SHARD, CHP - CH), BF16)
     split = GATE_TILES * 256
     first_shard = pack_shard([w_inner[:, 0], gap, w_inner[:, 1, :split]], 128)
@@ -899,11 +935,9 @@
     out_shard = pack_shard([w_ssm_out.T, gap, w_attn_out.T], 128)
     x_rows = tokens.reshape(8, 128, HALF)
     in_gains = pad_to(in_gain[None], 0, 8)
-    history = pad_to(conv_state, 2, CHT)
     taps = pad_to(pad_to(jnp.concatenate([conv_weight, conv_bias[None]]), 0, 8), 1, CHT)
-    xproj = pad_to(pad_to(w_xproj, 0, CHT), 1, 256)
-    _, _, conv, gate, qkv, mix, other_mix = project_call(
-        scalars, first_shard, second_shard, x_rows, in_gains, pick, turn, history, taps, xproj
+    _, _, conv, gate, qkv, mix, other_mix, unpick = project_call(
+        scalars, first_shard, second_shard, x_rows, in_gains, features, conv_state, taps, w_xproj
     )
     params = pad_to(pad_to(jnp.stack([dt_bias, skip_gain]), 0, 8), 1, CHP)
     gains = jnp.stack(
@@ -927,8 +961,7 @@
         out_shard,
         x_rows,
         pad_to(gains, 0, 8),
-        pick,
-        turn,
+        unpick,
     )
     return out.reshape(8, 16, 8, HALF)
 

time: 210 us -> 205 us (0.976)
  other arithmetic: 7.69 us -> 3.66 us
    convert_element_type x2 -> x0, other arithmetic: 4.02 us -> none  [the longest x1 3.33 us: picks(): (table[:, None, :] == jnp.arange(HALF, dtype=jnp.int32)[None, :, None]).a...]
    unnamed x28 -> x26, local copies, waits for them, and re-layouts: 4.23 us -> 6.87 us
where the time goes in v5:
time: 205 us; the launch traced here: 204 us
  Pallas kernels  188 us (92%)
  local copies, waits for them, and re-layouts  12.7 us (6%)
  other arithmetic  3.66 us (2%)
    pallas_call x1, Pallas kernels, final_call(): pl.pallas_call(final_kernel, name='attend_scan_deliver', grid=(8,), in_sp...  98.5 us
    pallas_call x1, Pallas kernels, project_call(): pl.pallas_call(project_kernel, name='gather_project', out_shape=(jax.Shap...  89.3 us
    unnamed x26, local copies, waits for them, and re-layouts  6.87 us

profile of v5, /device:TPU:0, one launch (start us, length us, event | category | flops | bytes accessed | tf_op | source)
XLA Modules:
  0.0 204.4 jit_solution(10882668979452582740)
XLA Ops:
  0.0 0.8 fusion.1
  0.8 0.1 broadcast_compare_fusion
  0.9 0.1 select_reduce_fusion
  1.1 0.7 reshape.72.scalars
  1.7 1.0 slice.41
  2.8 0.0 copy-start.8
  2.8 0.0 copy-start.9
  2.8 0.0 copy-start.1
  2.8 0.0 copy-start.2
  2.9 1.0 copy.52
  3.8 0.1 concatenate.21
  4.0 0.7 pad_maximum_fusion.first_shard
  4.7 0.8 slice.44
  5.5 0.9 concatenate.23
  6.5 0.6 pad_maximum_fusion.2.second_shard
  7.1 2.2 %copy.41.xproj_in = bf16[1600,132]{1,0:T(8,128)(2,1)} copy(bf16[1600,132]{0,1:T(8,128)(2,1)} %param.36) | data formatting | bytes 844800 | tf_op args[13]
  9.3 0.0 copy-done
  9.3 0.8 copy.40.history_in
  10.1 0.0 copy-done.4
  10.1 0.0 copy-done.3
  10.1 0.6 pad.40.taps
  10.7 0.6 pad.38.gain
  11.4 89.3 %gather_project.1 = (bf16[3,4,4,4,8,3072]{5,4,3,2,1,0:T(8,128)(2,1)}, bf16[3,4,4,4,8,1280]{5,4,3,2,1,0:T(8,128)(2,1)}, bf16[1024,1792]{1,0:T(8,128)(2,1)}, bf16[...) custom-call(s32[24]{0:T(128)} %reshape.72.scalars, ...), custom_call_target="tpu_custom_call" | custom-call | tf_op jit(solution)/shard_map/gather_project/pallas_call | solution.py:464
  100.7 0.1 dynamic_slice.10
  100.8 0.1 dynamic_slice.11
  100.9 0.6 select_maximum_fusion.2.gains
  101.5 0.0 copy-done.1
  101.5 0.1 concatenate.26
  101.7 0.7 pad_maximum_fusion.1.shard
  102.4 0.6 pad.42.params
  103.0 98.5 %attend_scan_deliver.1 = (bf16[8,128,800]{2,1,0:T(8,128)(2,1)}, bf16[3,4,4,4,8,2304]{5,4,3,2,1,0:T(8,128)(2,1)}) custom-call(s32[24]{0:T(128)} %reshape.72.scalars, bf16[1024,768]{1,0:T(8,128)(2,1)} %get-tuple-element.12.qkv, bf16[8,256,256]{2,1,0:T(8,128)(2,1)} %cache.1, f32[1024,256]{1,0:T(8,128)} %get-tuple-element.13.mix_own, ...), custom_call_target="tpu_custom_call" | custom-call | tf_op jit(solution)/shard_map/attend_scan_deliver/pallas_call | solution.py:826
  201.5 2.9 %copy.59 = bf16[8,16,8,800]{3,2,1,0:T(8,128)(2,1)} copy(bf16[8,16,8,800]{3,2,1,0:T(8,128)(2,1)} %bitcast.36) | data formatting | bytes 3276800
  (43 shorter events, 0.4 us)
Async XLA Ops:
  0.0 9.3 %copy-start = (f32[8,3,1600]{2,0,1:T(8,128)S(1)}, f32[8,3,1600]{2,0,1:T(8,128)}, u32[]{:S(2)}) copy-start(f32[8,3,1600]{2,0,1:T(8,128)} %param.26) | copy-start | bytes 460804
  0.0 10.1 %copy-start.4 = (f32[1600]{0:T(1024)S(1)}, f32[1600]{0:T(1024)}, u32[]{:S(2)}) copy-start(f32[1600]{0:T(1024)} %param.35) | copy-start | bytes 19204
  0.0 10.1 %copy-start.3 = (f32[4,1600]{1,0:T(4,128)S(1)}, f32[4,1600]{1,0:T(4,128)}, u32[]{:S(2)}) copy-start(f32[4,1600]{1,0:T(4,128)} %param.34) | copy-start | bytes 76804
  0.0 10.7 %copy-start.7 = (f32[800]{0:T(1024)S(1)}, f32[800]{0:T(1024)}, u32[]{:S(2)}) copy-start(f32[800]{0:T(1024)} %param.30) | copy-start | bytes 9604
  2.8 97.9 %copy-start.8 = (f32[1600]{0:T(1024)S(1)}, f32[1600]{0:T(1024)}, u32[]{:S(2)}) copy-start(f32[1600]{0:T(1024)} %param.43) | copy-start | bytes 19204
  2.8 98.0 %copy-start.9 = (f32[1600]{0:T(1024)S(1)}, f32[1600]{0:T(1024)}, u32[]{:S(2)}) copy-start(f32[1600]{0:T(1024)} %param.44) | copy-start | bytes 19204
  2.8 98.7 %copy-start.1 = (bf16[1600,25]{0,1:T(8,128)(2,1)S(1)}, bf16[1600,25]{0,1:T(8,128)(2,1)}, u32[]{:S(2)}) copy-start(bf16[1600,25]{0,1:T(8,128)(2,1)} %param.42) | copy-start | bytes 240004
  2.8 98.7 %copy-start.2 = (bf16[512,25]{0,1:T(8,128)(2,1)S(1)}, bf16[512,25]{0,1:T(8,128)(2,1)}, u32[]{:S(2)}) copy-start(bf16[512,25]{0,1:T(8,128)(2,1)} %param.41) | copy-start | bytes 76804
  3.9 98.4 %copy-start.5 = (f32[1600]{0:T(1024)S(1)}, f32[1600]{0:T(1024)}, u32[]{:S(2)}) copy-start(f32[1600]{0:T(1024)} %param.38) | copy-start | bytes 19204
  3.9 98.4 %copy-start.6 = (f32[1600]{0:T(1024)S(1)}, f32[1600]{0:T(1024)}, u32[]{:S(2)}) copy-start(f32[1600]{0:T(1024)} %param.40) | copy-start | bytes 19204

commit v6 on v5

--- a/solution.py
+++ b/solution.py
@@ -511,7 +511,7 @@
     return [high, middle, low]
 
 
-POLLS = ((0, 0, 1), (0, 1, 2), (1, 1, 3), (2, 0, 4), (2, 1, 5), (3, 0, 6), (3, 1, 7))
+POLLS = ((0, 0, 1), (0, 1, 2), (1, 1, 3), (2, 0, 4), (2, 1, 5), (3, 1, 6), (4, 0, 7))
 
 
 def final_kernel(

time: 205 us -> 204 us (level)
  no operation moved by 1% of the time
where the time goes in v6:
time: 204 us; the launch traced here: 203 us
  Pallas kernels  187 us (92%)
  local copies, waits for them, and re-layouts  12.7 us (6%)
  other arithmetic  3.66 us (2%)
    pallas_call x1, Pallas kernels, final_call(): pl.pallas_call(final_kernel, name='attend_scan_deliver', grid=(8,), in_sp...  97.5 us
    pallas_call x1, Pallas kernels, project_call(): pl.pallas_call(project_kernel, name='gather_project', out_shape=(jax.Shap...  89.3 us
    unnamed x26, local copies, waits for them, and re-layouts  6.87 us

profile of v6, /device:TPU:0, one launch (start us, length us, event | category | flops | bytes accessed | tf_op | source)
XLA Modules:
  0.0 203.4 jit_solution(1557035266983233751)
XLA Ops:
  0.0 0.8 fusion.1
  0.8 0.1 broadcast_compare_fusion
  0.9 0.1 select_reduce_fusion
  1.1 0.7 reshape.72.scalars
  1.7 1.0 slice.41
  2.8 0.0 copy-start.8
  2.8 0.0 copy-start.9
  2.8 0.0 copy-start.1
  2.8 0.0 copy-start.2
  2.9 1.0 copy.52
  3.8 0.1 concatenate.21
  4.0 0.7 pad_maximum_fusion.first_shard
  4.7 0.8 slice.44
  5.5 0.9 concatenate.23
  6.5 0.6 pad_maximum_fusion.2.second_shard
  7.1 2.2 %copy.41.xproj_in = bf16[1600,132]{1,0:T(8,128)(2,1)} copy(bf16[1600,132]{0,1:T(8,128)(2,1)} %param.36) | data formatting | bytes 844800 | tf_op args[13]
  9.3 0.0 copy-done
  9.3 0.8 copy.40.history_in
  10.1 0.0 copy-done.4
  10.1 0.0 copy-done.3
  10.1 0.6 pad.40.taps
  10.7 0.6 pad.38.gain
  11.4 89.3 %gather_project.1 = (bf16[3,4,4,4,8,3072]{5,4,3,2,1,0:T(8,128)(2,1)}, bf16[3,4,4,4,8,1280]{5,4,3,2,1,0:T(8,128)(2,1)}, bf16[1024,1792]{1,0:T(8,128)(2,1)}, bf16[...) custom-call(s32[24]{0:T(128)} %reshape.72.scalars, ...), custom_call_target="tpu_custom_call" | custom-call | tf_op jit(solution)/shard_map/gather_project/pallas_call | solution.py:464
  100.7 0.0 copy-done.8
  100.7 0.1 dynamic_slice.10
  100.8 0.1 dynamic_slice.11
  100.9 0.6 select_maximum_fusion.2.gains
  101.5 0.1 concatenate.26
  101.7 0.7 pad_maximum_fusion.1.shard
  102.4 0.6 pad.42.params
  103.0 97.5 %attend_scan_deliver.1 = (bf16[8,128,800]{2,1,0:T(8,128)(2,1)}, bf16[3,4,4,4,8,2304]{5,4,3,2,1,0:T(8,128)(2,1)}) custom-call(s32[24]{0:T(128)} %reshape.72.scalars, bf16[1024,768]{1,0:T(8,128)(2,1)} %get-tuple-element.12.qkv, bf16[8,256,256]{2,1,0:T(8,128)(2,1)} %cache.1, f32[1024,256]{1,0:T(8,128)} %get-tuple-element.13.mix_own, ...), custom_call_target="tpu_custom_call" | custom-call | tf_op jit(solution)/shard_map/attend_scan_deliver/pallas_call | solution.py:826
  200.5 2.9 %copy.59 = bf16[8,16,8,800]{3,2,1,0:T(8,128)(2,1)} copy(bf16[8,16,8,800]{3,2,1,0:T(8,128)(2,1)} %bitcast.36) | data formatting | bytes 3276800
  (43 shorter events, 0.4 us)
Async XLA Ops:
  0.0 9.3 %copy-start = (f32[8,3,1600]{2,0,1:T(8,128)S(1)}, f32[8,3,1600]{2,0,1:T(8,128)}, u32[]{:S(2)}) copy-start(f32[8,3,1600]{2,0,1:T(8,128)} %param.26) | copy-start | bytes 460804
  0.0 10.1 %copy-start.4 = (f32[1600]{0:T(1024)S(1)}, f32[1600]{0:T(1024)}, u32[]{:S(2)}) copy-start(f32[1600]{0:T(1024)} %param.35) | copy-start | bytes 19204
  0.0 10.1 %copy-start.3 = (f32[4,1600]{1,0:T(4,128)S(1)}, f32[4,1600]{1,0:T(4,128)}, u32[]{:S(2)}) copy-start(f32[4,1600]{1,0:T(4,128)} %param.34) | copy-start | bytes 76804
  0.0 10.7 %copy-start.7 = (f32[800]{0:T(1024)S(1)}, f32[800]{0:T(1024)}, u32[]{:S(2)}) copy-start(f32[800]{0:T(1024)} %param.30) | copy-start | bytes 9604
  2.8 97.9 %copy-start.8 = (f32[1600]{0:T(1024)S(1)}, f32[1600]{0:T(1024)}, u32[]{:S(2)}) copy-start(f32[1600]{0:T(1024)} %param.43) | copy-start | bytes 19204
  2.8 98.0 %copy-start.9 = (f32[1600]{0:T(1024)S(1)}, f32[1600]{0:T(1024)}, u32[]{:S(2)}) copy-start(f32[1600]{0:T(1024)} %param.44) | copy-start | bytes 19204
  2.8 98.7 %copy-start.1 = (bf16[1600,25]{0,1:T(8,128)(2,1)S(1)}, bf16[1600,25]{0,1:T(8,128)(2,1)}, u32[]{:S(2)}) copy-start(bf16[1600,25]{0,1:T(8,128)(2,1)} %param.42) | copy-start | bytes 240004
  2.8 98.7 %copy-start.2 = (bf16[512,25]{0,1:T(8,128)(2,1)S(1)}, bf16[512,25]{0,1:T(8,128)(2,1)}, u32[]{:S(2)}) copy-start(bf16[512,25]{0,1:T(8,128)(2,1)} %param.41) | copy-start | bytes 76804
  3.9 98.4 %copy-start.5 = (f32[1600]{0:T(1024)S(1)}, f32[1600]{0:T(1024)}, u32[]{:S(2)}) copy-start(f32[1600]{0:T(1024)} %param.38) | copy-start | bytes 19204
  3.9 98.4 %copy-start.6 = (f32[1600]{0:T(1024)S(1)}, f32[1600]{0:T(1024)}, u32[]{:S(2)}) copy-start(f32[1600]{0:T(1024)} %param.40) | copy-start | bytes 19204
